TPU v7x, 256 devices: a whole 4x4x8 slice. The times are simulated.
256 devices in a mesh: tile: 64 (over x, z, core), section: 4 (over y).
Axes of the slice: x: 4, y: 4, z: 8, core: 2. Of those that a mesh axis runs over, the one named last changes fastest.
Arguments:
- block_inputs: bfloat16 [4, 4, 4, 2048, 1024], P('section', None, None, 'tile'), may hold values from -16 to 16
- out_grad: bfloat16 [4, 4, 2048, 1024], P(None, None, 'tile'), may hold values from -4 to 4
- tissue: int32 [4, 256], P(None, 'tile'), may hold values 0 or 1
- w_reduce: bfloat16 [4, 1024, 256], P('section'), may hold values from -0.1875 to 0.1875
- w_conv: bfloat16 [4, 3, 3, 256, 256], P('section'), may hold values from -0.125 to 0.125
- w_expand: bfloat16 [4, 256, 1024], P('section'), may hold values from -0.375 to 0.375
- inner_affine: float32 [4, 4, 256], P('section'), may hold values from -0.5 to 1
- outer_affine: float32 [4, 2, 1024], P('section'), may hold values from -0.5 to 1
Outputs:
- grad_inputs: bfloat16 [4, 4, 4, 2048, 1024], P('section', None, None, 'tile')
- grad_reduce: float32 [4, 1024, 256], P('section', 'tile')
- grad_conv: float32 [4, 3, 3, 256, 256], P('section', None, None, 'tile')
- grad_expand: float32 [4, 256, 1024], P('section', 'tile')
All inputs are finite; a program needn't handle non-finite values. No bound on the sum of `tissue` on one device may be relied on, other than what follows from the above.
Results may differ from a plain program's by a relative error of at most 0.023.
The roundings to bfloat16 on the way count: a program that leaves them out, or rounds other values in their place, can miss the bound.
Values may be sent and summed in bfloat16 or wider, within the bound.
No kernel may reach another device: no remote copies, remote signals or barrier semaphores. Data moves between devices by JAX's collectives and lax.ppermute only.
A program may use at most 128 MiB of HBM per device.

v0:
```python
import jax
import jax.numpy as jnp
from jax import lax
from jax.sharding import PartitionSpec as P

TILE_W = 8


def extended(block, sides, width):
    for axis, dim in sides:
        count = lax.axis_size(axis)
        forward = [(i, i + 1) for i in range(count - 1)]
        backward = [(target, source) for source, target in forward]
        low = lax.ppermute(
            lax.slice_in_dim(block, block.shape[dim] - width, None, axis=dim), axis, forward
        )
        high = lax.ppermute(lax.slice_in_dim(block, 0, width, axis=dim), axis, backward)
        block = jnp.concatenate([low, block, high], axis=dim)
    return block


def shifted(value, axis, steps):
    count = lax.axis_size(axis)
    leading, last = (max(0, -steps), min(count, count - steps))
    return lax.ppermute(value, axis, [(source, source + steps) for source in range(leading, last)])


def contract(left, right):
    return lax.dot_general(
        left, right, (((0,), (0,)), ((), ())), preferred_element_type=jnp.float32
    )


def block_grad(inputs, grad_out, w_reduce, w_conv, w_expand, inner, outer):
    count, height, width, channels = inputs.shape
    inner_w = w_reduce.shape[1]
    flat_x = inputs.reshape(-1, channels)
    pre_one = jnp.dot(flat_x, w_reduce, preferred_element_type=jnp.float32) * inner[0] + inner[1]
    hidden_one = (
        jnp.maximum(pre_one, 0.0).astype(jnp.bfloat16).reshape(count, height, width, inner_w)
    )
    rimmed = extended(hidden_one, (("tile", 2),), 1)
    padded = jnp.pad(rimmed, ((0, 0), (1, 1), (0, 0), (0, 0)))
    pieces = []
    for row_off in range(3):
        for col_off in range(3):
            pieces.append(
                padded[:, row_off : row_off + height, col_off : col_off + width].reshape(
                    -1, inner_w
                )
            )
    total = jnp.zeros((count * height * width, inner_w), jnp.float32)
    for offset in range(9):
        total = total + jnp.dot(
            pieces[offset], w_conv[offset // 3, offset % 3], preferred_element_type=jnp.float32
        )
    pre_two = total * inner[2] + inner[3]
    hidden_two = jnp.maximum(pre_two, 0.0).astype(jnp.bfloat16)
    summed = (
        jnp.dot(hidden_two, w_expand, preferred_element_type=jnp.float32) * outer[0]
        + outer[1]
        + flat_x.astype(jnp.float32)
    )
    flat_g = grad_out.reshape(-1, channels)
    grad_sum = jnp.where(summed > 0, flat_g.astype(jnp.float32), 0.0).astype(jnp.bfloat16)
    grad_three = (grad_sum.astype(jnp.float32) * outer[0]).astype(jnp.bfloat16)
    g_expand = contract(hidden_two, grad_three)
    grad_two = jnp.where(
        pre_two > 0,
        jnp.dot(grad_three, w_expand.T, preferred_element_type=jnp.float32) * inner[2],
        0.0,
    ).astype(jnp.bfloat16)
    g_conv = jnp.stack([contract(pieces[offset], grad_two) for offset in range(9)]).reshape(
        3, 3, inner_w, inner_w
    )
    rim_grad = extended(grad_two.reshape(count, height, width, inner_w), (("tile", 2),), 1)
    padded_grad = jnp.pad(rim_grad, ((0, 0), (1, 1), (0, 0), (0, 0)))
    back = jnp.zeros((count * height * width, inner_w), jnp.float32)
    for row_off in range(3):
        for col_off in range(3):
            piece = padded_grad[
                :, 2 - row_off : 2 - row_off + height, 2 - col_off : 2 - col_off + width
            ].reshape(-1, inner_w)
            back = back + jnp.dot(
                piece, w_conv[row_off, col_off].T, preferred_element_type=jnp.float32
            )
    grad_one = jnp.where(pre_one > 0, back * inner[0], 0.0).astype(jnp.bfloat16)
    g_reduce = contract(flat_x, grad_one)
    grad_in = (
        grad_sum.astype(jnp.float32)
        + jnp.dot(grad_one, w_reduce.T, preferred_element_type=jnp.float32)
    ).astype(jnp.bfloat16)
    return (grad_in.reshape(inputs.shape), g_reduce, g_conv, g_expand)


def per_device(
    block_inputs, out_grad, tissue, w_reduce, w_conv, w_expand, inner_affine, outer_affine
):
    section_now = lax.axis_index("section")
    sections = lax.axis_size("section")
    inputs = block_inputs[0]
    rows = inputs.shape[0]
    coverage = jnp.repeat(tissue, TILE_W, axis=1).astype(jnp.bfloat16)[:, None, :, None]
    seeded = out_grad * coverage
    batch = 1
    groups = rows // batch
    weights_r = w_reduce[0]
    weights_c = w_conv[0]
    weights_e = w_expand[0]
    inner = inner_affine[0]
    outer = outer_affine[0]
    inner_w = weights_r.shape[1]
    channels = weights_r.shape[0]
    carried = jnp.zeros((batch,) + inputs.shape[1:], jnp.bfloat16)
    grad_inputs = jnp.zeros_like(inputs)
    total_r = jnp.zeros((channels, inner_w), jnp.float32)
    total_c = jnp.zeros((3, 3, inner_w, inner_w), jnp.float32)
    total_e = jnp.zeros((inner_w, channels), jnp.float32)
    last_step = groups + sections - 2
    for step in range(last_step + 1):
        micro = step - (sections - 1 - section_now)
        valid = (micro >= 0) & (micro < groups)
        start = jnp.clip(micro, 0, groups - 1) * batch
        x_block = lax.dynamic_slice_in_dim(inputs, start, batch, 0)
        seed_block = lax.dynamic_slice_in_dim(seeded, start, batch, 0)
        grad_out = jnp.where(section_now == sections - 1, seed_block, carried)
        weight = valid.astype(jnp.float32)
        grad_in, g_r, g_c, g_e = block_grad(
            x_block, grad_out, weights_r, weights_c, weights_e, inner, outer
        )
        total_r, total_c, total_e = (
            total_r + g_r * weight,
            total_c + g_c * weight,
            total_e + g_e * weight,
        )
        kept = lax.dynamic_slice_in_dim(grad_inputs, start, batch, 0)
        grad_inputs = lax.dynamic_update_slice_in_dim(
            grad_inputs, jnp.where(valid, grad_in, kept), start, 0
        )
        carried = shifted(grad_in, "section", -1)
    total_r, total_c, total_e = (
        lax.psum_scatter(total_r, "tile", scatter_dimension=0, tiled=True),
        lax.psum_scatter(total_c, "tile", scatter_dimension=2, tiled=True),
        lax.psum_scatter(total_e, "tile", scatter_dimension=0, tiled=True),
    )
    return (grad_inputs[None], total_r[None], total_c[None], total_e[None])


def solution(mesh):
    in_specs = (
        P("section", None, None, "tile", None),
        P(None, None, "tile", None),
        P(None, "tile"),
        P("section", None, None),
        P("section", None, None, None, None),
        P("section", None, None),
        P("section", None, None),
        P("section", None, None),
    )
    out_specs = (
        P("section", None, None, "tile", None),
        P("section", "tile", None),
        P("section", None, None, "tile", None),
        P("section", "tile", None),
    )
    return jax.shard_map(
        per_device, mesh=mesh, in_specs=in_specs, out_specs=out_specs, check_vma=False
    )
```

profile of v0, /device:TPU:22, one launch (start us, length us, event | category | flops | bytes accessed | tf_op | source)
XLA Modules:
  0.0 585.1 jit_solution(18222607035549991463)
XLA Ops:
  8.1 2.5 constant_dynamic-slice_fusion.2
  14.2 7.5 %collective-permute-start.20 = (bf16[1,4,1,256]{3,2,1,0:T(2,128)(2,1)}, bf16[1,4,1,256]{3,2,1,0:T(2,128)(2,1)}, u32[]{:S(2)}, u32[]{:S(2)}) collective-permute-start(bf16[1,4,1,256]{3,2,1,0:T(2,128)(2,1)} %get-tuple-element.120), channel_id=1, source_target_pairs={{4,0},{8,4},{12,8},{16,12},{20,16},{24,20},{28,24},{32,28},{36,32}... | collective-permute-start | bytes 6152 | tf_op jit(solution)/shard_map/ppermute | solution.py:17
  28.5 5.8 collective-permute-start.25
  49.5 5.8 collective-permute-start.1
  58.2 5.8 collective-permute-start.5
  66.6 1.9 collective-permute-start.9
  68.5 5.8 collective-permute-start.10
  76.7 5.8 collective-permute-start.15
  83.1 1.9 collective-permute-start.30
  85.1 2.4 collective-permute-start.2
  87.9 5.3 collective-permute-start.3
  108.4 2.3 collective-permute-start.6
  111.3 5.4 collective-permute-done.6
  119.5 5.8 collective-permute-start.8
  129.7 2.5 collective-permute-start.11
  132.6 5.3 collective-permute-done.11
  140.8 5.8 collective-permute-start.13
  151.0 2.4 collective-permute-start.16
  153.7 5.6 collective-permute-done.16
  162.2 5.8 collective-permute-start.18
  172.4 2.4 collective-permute-start.21
  175.1 5.6 collective-permute-done.21
  183.6 5.8 collective-permute-start.23
  193.7 2.4 collective-permute-start.26
  196.5 5.6 collective-permute-done.26
  205.0 5.8 collective-permute-start.28
  215.1 2.3 collective-permute-start.31
  218.7 4.7 collective-permute-done.31
  226.9 6.0 %collective-permute-start.33 = (bf16[1,4,1,256]{3,2,1,0:T(2,128)(2,1)S(1)}, bf16[1,4,1,256]{3,2,1,0:T(2,128)(2,1)S(1)}, u32[]{:S(2)}, u32[]{:S(2)}) collective-permute-start(bf16[1,4,1,256]{3,2,1,0:T(2,128)(2,1)S(1)} %get-tuple-element.100), channel_id=1, source_target_pairs={{4,0},{8,4},{12,8},{16,12},{20,16},{24,20},{28,24},{32,28},{36,32}... | collective-permute-start | bytes 6152 | tf_op jit(solution)/shard_map/ppermute | solution.py:17
  241.5 4.6 add_add_fusion
  253.2 181.6 %all-reduce.19.cloned.1.call-done = (f32[3,3,256,256]{3,2,1,0:T(8,128)}, f32[256,1024]{1,0:T(8,128)}) async-done(((f32[3,3,256,256]{3,2,1,0:T(8,128)}, f32[256,1024]{1,0:T(8,128)}), (f32[3,3,256,256]{3,2,1,0:T(8,128)}, f32[256,1024]{1,0:T(8,128)})) %all-reduce.19.cloned.1.call-update) | async-done | bytes 3407888
  437.6 140.6 %reduce-scatter.3.cloned.1.call-done = f32[16,256]{1,0:T(8,128)} async-done(((f32[1024,256]{1,0:T(8,128)}), f32[16,256]{1,0:T(8,128)}) %reduce-scatter.3.cloned.1.call-update) | async-done | bytes 16400 | tf_op jit(solution)/shard_map/reduce_scatter | solution.py:142
  (458 shorter events, 109.1 us)
Async XLA Ops:
  7.2 427.6 %all-reduce.19.cloned.1.call-start = ((), (), s32[]{:S(2)}) async-start(), calls=%async_computation.2 | async-start | bytes 6815744
  12.3 82.0 %collective-permute-start.19 = (bf16[1,4,1,256]{3,2,1,0:T(2,128)(2,1)}, bf16[1,4,1,256]{3,2,1,0:T(2,128)(2,1)}, u32[]{:S(2)}, u32[]{:S(2)}) collective-permute-start(bf16[1,4,1,256]{3,2,1,0:T(2,128)(2,1)} %get-tuple-element.119), channel_id=1, source_target_pairs={{0,4},{4,8},{8,12},{12,16},{16,20},{20,24},{24,28},{28,32},{32,36}... | collective-permute-start | bytes 6152 | tf_op jit(solution)/shard_map/ppermute | solution.py:14
  14.2 80.1 %collective-permute-start.20 = (bf16[1,4,1,256]{3,2,1,0:T(2,128)(2,1)}, bf16[1,4,1,256]{3,2,1,0:T(2,128)(2,1)}, u32[]{:S(2)}, u32[]{:S(2)}) collective-permute-start(bf16[1,4,1,256]{3,2,1,0:T(2,128)(2,1)} %get-tuple-element.120), channel_id=1, source_target_pairs={{4,0},{8,4},{12,8},{16,12},{20,16},{24,20},{28,24},{32,28},{36,32}... | collective-permute-start | bytes 6152 | tf_op jit(solution)/shard_map/ppermute | solution.py:17
  23.2 64.8 %collective-permute-start.29 = (bf16[1,4,1,256]{3,2,1,0:T(2,128)(2,1)}, bf16[1,4,1,256]{3,2,1,0:T(2,128)(2,1)}, u32[]{:S(2)}, u32[]{:S(2)}) collective-permute-start(bf16[1,4,1,256]{3,2,1,0:T(2,128)(2,1)} %get-tuple-element.103), channel_id=1, source_target_pairs={{0,4},{4,8},{8,12},{12,16},{16,20},{20,24},{24,28},{28,32},{32,36}... | collective-permute-start | bytes 6152 | tf_op jit(solution)/shard_map/ppermute | solution.py:14
  26.6 21.0 %collective-permute-start.24 = (bf16[1,4,1,256]{3,2,1,0:T(2,128)(2,1)}, bf16[1,4,1,256]{3,2,1,0:T(2,128)(2,1)}, u32[]{:S(2)}, u32[]{:S(2)}) collective-permute-start(bf16[1,4,1,256]{3,2,1,0:T(2,128)(2,1)} %get-tuple-element.111), channel_id=1, source_target_pairs={{0,4},{4,8},{8,12},{12,16},{16,20},{20,24},{24,28},{28,32},{32,36}... | collective-permute-start | bytes 6152 | tf_op jit(solution)/shard_map/ppermute | solution.py:14
  28.5 21.0 %collective-permute-start.25 = (bf16[1,4,1,256]{3,2,1,0:T(2,128)(2,1)}, bf16[1,4,1,256]{3,2,1,0:T(2,128)(2,1)}, u32[]{:S(2)}, u32[]{:S(2)}) collective-permute-start(bf16[1,4,1,256]{3,2,1,0:T(2,128)(2,1)} %get-tuple-element.112), channel_id=1, source_target_pairs={{4,0},{8,4},{12,8},{16,12},{20,16},{24,20},{28,24},{32,28},{36,32}... | collective-permute-start | bytes 6152 | tf_op jit(solution)/shard_map/ppermute | solution.py:17
  47.6 8.6 %collective-permute-start = (bf16[1,4,1,256]{3,2,1,0:T(2,128)(2,1)S(1)}, bf16[1,4,1,256]{3,2,1,0:T(2,128)(2,1)S(1)}, u32[]{:S(2)}, u32[]{:S(2)}) collective-permute-start(bf16[1,4,1,256]{3,2,1,0:T(2,128)(2,1)S(1)} %get-tuple-element.151), channel_id=1, source_target_pairs={{0,4},{4,8},{8,12},{12,16},{16,20},{20,24},{24,28},{28,32},{32,36}... | collective-permute-start | bytes 6152 | tf_op jit(solution)/shard_map/ppermute | solution.py:14
  49.5 8.6 %collective-permute-start.1 = (bf16[1,4,1,256]{3,2,1,0:T(2,128)(2,1)S(1)}, bf16[1,4,1,256]{3,2,1,0:T(2,128)(2,1)S(1)}, u32[]{:S(2)}, u32[]{:S(2)}) collective-permute-start(bf16[1,4,1,256]{3,2,1,0:T(2,128)(2,1)S(1)} %get-tuple-element.152), channel_id=1, source_target_pairs={{4,0},{8,4},{12,8},{16,12},{20,16},{24,20},{28,24},{32,28},{36,32}... | collective-permute-start | bytes 6152 | tf_op jit(solution)/shard_map/ppermute | solution.py:17
  56.2 10.3 %collective-permute-start.4 = (bf16[1,4,1,256]{3,2,1,0:T(2,128)(2,1)S(1)}, bf16[1,4,1,256]{3,2,1,0:T(2,128)(2,1)S(1)}, u32[]{:S(2)}, u32[]{:S(2)}) collective-permute-start(bf16[1,4,1,256]{3,2,1,0:T(2,128)(2,1)S(1)} %get-tuple-element.143), channel_id=1, source_target_pairs={{0,4},{4,8},{8,12},{12,16},{16,20},{20,24},{24,28},{28,32},{32,36}... | collective-permute-start | bytes 6152 | tf_op jit(solution)/shard_map/ppermute | solution.py:14
  58.2 10.3 %collective-permute-start.5 = (bf16[1,4,1,256]{3,2,1,0:T(2,128)(2,1)S(1)}, bf16[1,4,1,256]{3,2,1,0:T(2,128)(2,1)S(1)}, u32[]{:S(2)}, u32[]{:S(2)}) collective-permute-start(bf16[1,4,1,256]{3,2,1,0:T(2,128)(2,1)S(1)} %get-tuple-element.144), channel_id=1, source_target_pairs={{4,0},{8,4},{12,8},{16,12},{20,16},{24,20},{28,24},{32,28},{36,32}... | collective-permute-start | bytes 6152 | tf_op jit(solution)/shard_map/ppermute | solution.py:17
  66.6 8.1 %collective-permute-start.9 = (bf16[1,4,1,256]{3,2,1,0:T(2,128)(2,1)S(1)}, bf16[1,4,1,256]{3,2,1,0:T(2,128)(2,1)S(1)}, u32[]{:S(2)}, u32[]{:S(2)}) collective-permute-start(bf16[1,4,1,256]{3,2,1,0:T(2,128)(2,1)S(1)} %get-tuple-element.135), channel_id=1, source_target_pairs={{0,4},{4,8},{8,12},{12,16},{16,20},{20,24},{24,28},{28,32},{32,36}... | collective-permute-start | bytes 6152 | tf_op jit(solution)/shard_map/ppermute | solution.py:14
  68.5 8.1 %collective-permute-start.10 = (bf16[1,4,1,256]{3,2,1,0:T(2,128)(2,1)S(1)}, bf16[1,4,1,256]{3,2,1,0:T(2,128)(2,1)S(1)}, u32[]{:S(2)}, u32[]{:S(2)}) collective-permute-start(bf16[1,4,1,256]{3,2,1,0:T(2,128)(2,1)S(1)} %get-tuple-element.136), channel_id=1, source_target_pairs={{4,0},{8,4},{12,8},{16,12},{20,16},{24,20},{28,24},{32,28},{36,32}... | collective-permute-start | bytes 6152 | tf_op jit(solution)/shard_map/ppermute | solution.py:17
  74.8 8.4 %collective-permute-start.14 = (bf16[1,4,1,256]{3,2,1,0:T(2,128)(2,1)S(1)}, bf16[1,4,1,256]{3,2,1,0:T(2,128)(2,1)S(1)}, u32[]{:S(2)}, u32[]{:S(2)}) collective-permute-start(bf16[1,4,1,256]{3,2,1,0:T(2,128)(2,1)S(1)} %copy-done.48), channel_id=1, source_target_pairs={{0,4},{4,8},{8,12},{12,16},{16,20},{20,24},{24,28},{28,32},{32,36}... | collective-permute-start | bytes 6152 | tf_op jit(solution)/shard_map/ppermute | solution.py:14
  76.7 8.4 %collective-permute-start.15 = (bf16[1,4,1,256]{3,2,1,0:T(2,128)(2,1)S(1)}, bf16[1,4,1,256]{3,2,1,0:T(2,128)(2,1)S(1)}, u32[]{:S(2)}, u32[]{:S(2)}) collective-permute-start(bf16[1,4,1,256]{3,2,1,0:T(2,128)(2,1)S(1)} %copy-done.47), channel_id=1, source_target_pairs={{4,0},{8,4},{12,8},{16,12},{20,16},{24,20},{28,24},{32,28},{36,32}... | collective-permute-start | bytes 6152 | tf_op jit(solution)/shard_map/ppermute | solution.py:17
  83.1 10.1 %collective-permute-start.30 = (bf16[1,4,1,256]{3,2,1,0:T(2,128)(2,1)S(1)}, bf16[1,4,1,256]{3,2,1,0:T(2,128)(2,1)S(1)}, u32[]{:S(2)}, u32[]{:S(2)}) collective-permute-start(bf16[1,4,1,256]{3,2,1,0:T(2,128)(2,1)S(1)} %copy-done.46), channel_id=1, source_target_pairs={{4,0},{8,4},{12,8},{16,12},{20,16},{24,20},{28,24},{32,28},{36,32}... | collective-permute-start | bytes 6152 | tf_op jit(solution)/shard_map/ppermute | solution.py:17
  85.1 21.2 %collective-permute-start.2 = (bf16[1,4,1,256]{3,2,1,0:T(2,128)(2,1)S(1)}, bf16[1,4,1,256]{3,2,1,0:T(2,128)(2,1)S(1)}, u32[]{:S(2)}, u32[]{:S(2)}) collective-permute-start(bf16[1,4,1,256]{3,2,1,0:T(2,128)(2,1)S(1)} %get-tuple-element.147), channel_id=1, source_target_pairs={{0,4},{4,8},{8,12},{12,16},{16,20},{20,24},{24,28},{28,32},{32,36}... | collective-permute-start | bytes 6152 | tf_op jit(solution)/shard_map/ppermute | solution.py:14
  87.9 18.4 %collective-permute-start.3 = (bf16[1,4,1,256]{3,2,1,0:T(2,128)(2,1)S(1)}, bf16[1,4,1,256]{3,2,1,0:T(2,128)(2,1)S(1)}, u32[]{:S(2)}, u32[]{:S(2)}) collective-permute-start(bf16[1,4,1,256]{3,2,1,0:T(2,128)(2,1)S(1)} %get-tuple-element.148), channel_id=1, source_target_pairs={{4,0},{8,4},{12,8},{16,12},{20,16},{24,20},{28,24},{32,28},{36,32}... | collective-permute-start | bytes 6152 | tf_op jit(solution)/shard_map/ppermute | solution.py:17
  108.4 8.3 %collective-permute-start.6 = (bf16[1,4,32,1024]{3,2,1,0:T(8,128)(2,1)S(1)}, bf16[1,4,32,1024]{3,2,1,0:T(8,128)(2,1)S(1)}, u32[]{:S(2)}, u32[]{:S(2)}) collective-permute-start(bf16[1,4,32,1024]{3,2,1,0:T(8,128)(2,1)S(1)} %bitcast.1163), channel_id=1, source_target_pairs={{1,0},{2,1},{3,2},{5,4},{6,5},{7,6},{9,8},{10,9},{11,10},{13,12},{... | collective-permute-start | bytes 786440 | tf_op jit(solution)/shard_map/ppermute | solution.py:25
  117.6 9.9 %collective-permute-start.7 = (bf16[1,4,1,256]{3,2,1,0:T(2,128)(2,1)S(1)}, bf16[1,4,1,256]{3,2,1,0:T(2,128)(2,1)S(1)}, u32[]{:S(2)}, u32[]{:S(2)}) collective-permute-start(bf16[1,4,1,256]{3,2,1,0:T(2,128)(2,1)S(1)} %get-tuple-element.139), channel_id=1, source_target_pairs={{0,4},{4,8},{8,12},{12,16},{16,20},{20,24},{24,28},{28,32},{32,36}... | collective-permute-start | bytes 6152 | tf_op jit(solution)/shard_map/ppermute | solution.py:14
  129.7 8.3 %collective-permute-start.11 = (bf16[1,4,32,1024]{3,2,1,0:T(8,128)(2,1)S(1)}, bf16[1,4,32,1024]{3,2,1,0:T(8,128)(2,1)S(1)}, u32[]{:S(2)}, u32[]{:S(2)}) collective-permute-start(bf16[1,4,32,1024]{3,2,1,0:T(8,128)(2,1)S(1)} %bitcast.1159), channel_id=1, source_target_pairs={{1,0},{2,1},{3,2},{5,4},{6,5},{7,6},{9,8},{10,9},{11,10},{13,12},{... | collective-permute-start | bytes 786440 | tf_op jit(solution)/shard_map/ppermute | solution.py:25
  138.9 9.9 %collective-permute-start.12 = (bf16[1,4,1,256]{3,2,1,0:T(2,128)(2,1)S(1)}, bf16[1,4,1,256]{3,2,1,0:T(2,128)(2,1)S(1)}, u32[]{:S(2)}, u32[]{:S(2)}) collective-permute-start(bf16[1,4,1,256]{3,2,1,0:T(2,128)(2,1)S(1)} %get-tuple-element.131), channel_id=1, source_target_pairs={{0,4},{4,8},{8,12},{12,16},{16,20},{20,24},{24,28},{28,32},{32,36}... | collective-permute-start | bytes 6152 | tf_op jit(solution)/shard_map/ppermute | solution.py:14
  140.8 8.0 %collective-permute-start.13 = (bf16[1,4,1,256]{3,2,1,0:T(2,128)(2,1)S(1)}, bf16[1,4,1,256]{3,2,1,0:T(2,128)(2,1)S(1)}, u32[]{:S(2)}, u32[]{:S(2)}) collective-permute-start(bf16[1,4,1,256]{3,2,1,0:T(2,128)(2,1)S(1)} %get-tuple-element.132), channel_id=1, source_target_pairs={{4,0},{8,4},{12,8},{16,12},{20,16},{24,20},{28,24},{32,28},{36,32}... | collective-permute-start | bytes 6152 | tf_op jit(solution)/shard_map/ppermute | solution.py:17
  151.0 8.4 %collective-permute-start.16 = (bf16[1,4,32,1024]{3,2,1,0:T(8,128)(2,1)S(1)}, bf16[1,4,32,1024]{3,2,1,0:T(8,128)(2,1)S(1)}, u32[]{:S(2)}, u32[]{:S(2)}) collective-permute-start(bf16[1,4,32,1024]{3,2,1,0:T(8,128)(2,1)S(1)} %bitcast.1151), channel_id=1, source_target_pairs={{1,0},{2,1},{3,2},{5,4},{6,5},{7,6},{9,8},{10,9},{11,10},{13,12},{... | collective-permute-start | bytes 786440 | tf_op jit(solution)/shard_map/ppermute | solution.py:25
  160.3 9.9 %collective-permute-start.17 = (bf16[1,4,1,256]{3,2,1,0:T(2,128)(2,1)S(1)}, bf16[1,4,1,256]{3,2,1,0:T(2,128)(2,1)S(1)}, u32[]{:S(2)}, u32[]{:S(2)}) collective-permute-start(bf16[1,4,1,256]{3,2,1,0:T(2,128)(2,1)S(1)} %get-tuple-element.123), channel_id=1, source_target_pairs={{0,4},{4,8},{8,12},{12,16},{16,20},{20,24},{24,28},{28,32},{32,36}... | collective-permute-start | bytes 6152 | tf_op jit(solution)/shard_map/ppermute | solution.py:14
  172.4 8.4 %collective-permute-start.21 = (bf16[1,4,32,1024]{3,2,1,0:T(8,128)(2,1)S(1)}, bf16[1,4,32,1024]{3,2,1,0:T(8,128)(2,1)S(1)}, u32[]{:S(2)}, u32[]{:S(2)}) collective-permute-start(bf16[1,4,32,1024]{3,2,1,0:T(8,128)(2,1)S(1)} %bitcast.1153), channel_id=1, source_target_pairs={{1,0},{2,1},{3,2},{5,4},{6,5},{7,6},{9,8},{10,9},{11,10},{13,12},{... | collective-permute-start | bytes 786440 | tf_op jit(solution)/shard_map/ppermute | solution.py:25
  181.7 9.9 %collective-permute-start.22 = (bf16[1,4,1,256]{3,2,1,0:T(2,128)(2,1)S(1)}, bf16[1,4,1,256]{3,2,1,0:T(2,128)(2,1)S(1)}, u32[]{:S(2)}, u32[]{:S(2)}) collective-permute-start(bf16[1,4,1,256]{3,2,1,0:T(2,128)(2,1)S(1)} %get-tuple-element.115), channel_id=1, source_target_pairs={{0,4},{4,8},{8,12},{12,16},{16,20},{20,24},{24,28},{28,32},{32,36}... | collective-permute-start | bytes 6152 | tf_op jit(solution)/shard_map/ppermute | solution.py:14
  193.7 8.4 %collective-permute-start.26 = (bf16[1,4,32,1024]{3,2,1,0:T(8,128)(2,1)S(1)}, bf16[1,4,32,1024]{3,2,1,0:T(8,128)(2,1)S(1)}, u32[]{:S(2)}, u32[]{:S(2)}) collective-permute-start(bf16[1,4,32,1024]{3,2,1,0:T(8,128)(2,1)S(1)} %bitcast.1155), channel_id=1, source_target_pairs={{1,0},{2,1},{3,2},{5,4},{6,5},{7,6},{9,8},{10,9},{11,10},{13,12},{... | collective-permute-start | bytes 786440 | tf_op jit(solution)/shard_map/ppermute | solution.py:25
  203.0 9.9 %collective-permute-start.27 = (bf16[1,4,1,256]{3,2,1,0:T(2,128)(2,1)S(1)}, bf16[1,4,1,256]{3,2,1,0:T(2,128)(2,1)S(1)}, u32[]{:S(2)}, u32[]{:S(2)}) collective-permute-start(bf16[1,4,1,256]{3,2,1,0:T(2,128)(2,1)S(1)} %get-tuple-element.107), channel_id=1, source_target_pairs={{0,4},{4,8},{8,12},{12,16},{16,20},{20,24},{24,28},{28,32},{32,36}... | collective-permute-start | bytes 6152 | tf_op jit(solution)/shard_map/ppermute | solution.py:14
  215.1 8.3 %collective-permute-start.31 = (bf16[1,4,32,1024]{3,2,1,0:T(8,128)(2,1)S(1)}, bf16[1,4,32,1024]{3,2,1,0:T(8,128)(2,1)S(1)}, u32[]{:S(2)}, u32[]{:S(2)}) collective-permute-start(bf16[1,4,32,1024]{3,2,1,0:T(8,128)(2,1)S(1)} %bitcast.1157), channel_id=1, source_target_pairs={{1,0},{2,1},{3,2},{5,4},{6,5},{7,6},{9,8},{10,9},{11,10},{13,12},{... | collective-permute-start | bytes 786440 | tf_op jit(solution)/shard_map/ppermute | solution.py:25
  225.0 21.4 %collective-permute-start.32 = (bf16[1,4,1,256]{3,2,1,0:T(2,128)(2,1)S(1)}, bf16[1,4,1,256]{3,2,1,0:T(2,128)(2,1)S(1)}, u32[]{:S(2)}, u32[]{:S(2)}) collective-permute-start(bf16[1,4,1,256]{3,2,1,0:T(2,128)(2,1)S(1)} %get-tuple-element.99), channel_id=1, source_target_pairs={{0,4},{4,8},{8,12},{12,16},{16,20},{20,24},{24,28},{28,32},{32,36}... | collective-permute-start | bytes 6152 | tf_op jit(solution)/shard_map/ppermute | solution.py:14
  226.9 19.4 %collective-permute-start.33 = (bf16[1,4,1,256]{3,2,1,0:T(2,128)(2,1)S(1)}, bf16[1,4,1,256]{3,2,1,0:T(2,128)(2,1)S(1)}, u32[]{:S(2)}, u32[]{:S(2)}) collective-permute-start(bf16[1,4,1,256]{3,2,1,0:T(2,128)(2,1)S(1)} %get-tuple-element.100), channel_id=1, source_target_pairs={{4,0},{8,4},{12,8},{16,12},{20,16},{24,20},{28,24},{32,28},{36,32}... | collective-permute-start | bytes 6152 | tf_op jit(solution)/shard_map/ppermute | solution.py:17
  246.3 331.9 %reduce-scatter.3.cloned.1.call-start = ((), (), s32[]{:S(2)}) async-start(), calls=%async_computation.1 | async-start | bytes 1064960 | tf_op jit(solution)/shard_map/reduce_scatter | solution.py:142
  (55 other events, 452.9 us)
Sparse Core Ops, SparseCore 0:
  246.4 188.2 all-reduce.18
  439.8 138.3 reduce-scatter.2
where the time goes:
time: 588 us; the launch traced here: 585 us
  waiting for transfers between devices  355 us (60%)
  starting transfers between devices  120 us (20%)
  matrix products  67 us (11%)
  between operations  17.6 us (3%)
  local copies, waits for them, and re-layouts  14.8 us (3%)
  other arithmetic  11.3 us (2%)
    unnamed x3, waiting for transfers between devices  182 us
    reduce_scatter x1, waiting for transfers between devices, per_device(): lax.psum_scatter(total_r, 'tile', scatter_dimension=0, tiled=True)  141 us
    ppermute x14, starting transfers between devices, extended(): lax.ppermute(lax.slice_in_dim(block, 0, width, axis=dim), axis, backward)  78.1 us
    ppermute x6, waiting for transfers between devices, shifted(): lax.ppermute(value, axis, [(source, source + steps) for source in range(l...  32.3 us
    ppermute x14, starting transfers between devices, extended(): lax.ppermute(lax.slice_in_dim(block, block.shape[dim] - width, None, axis...  27.3 us
    dot_general x77, matrix products, contract(): lax.dot_general(left, right, (((0,), (0,)), ((), ())), preferred_element_...  26.8 us
    dot_general x63, matrix products, block_grad(): jnp.dot(pieces[offset], w_conv[offset // 3, offset % 3], preferred_elemen...  14.9 us
    ppermute x6, starting transfers between devices, shifted(): lax.ppermute(value, axis, [(source, source + steps) for source in range(l...  14.3 us
  transfers between devices with their start and end apart: 36, of which 8 were waited for; matrix products, arithmetic and copies ran while one was open for 11% of the time, Pallas kernels for 0%

commit v1 on v0

v1 whole, which is shorter than its diff:
```python
import functools

import jax
import jax.numpy as jnp
from jax import lax
from jax.experimental import pallas as pl
from jax.experimental.pallas import tpu as pltpu
from jax.sharding import PartitionSpec as P

TILE_W = 8
X, Z, CORES = 4, 8, 2
EDGE = 8
RIM = 4
BF16, F32 = jnp.bfloat16, jnp.float32
LAG = 2
SEGS, A_SEGS = 17, 8
Z_ORDER = (7, 3, 5, 1, 6, 2, 4, 0)


def params(mib):
    return pltpu.CompilerParams(vmem_limit_bytes=mib * 1024 * 1024)


def dot(left, right):
    return jnp.dot(left, right, preferred_element_type=F32)


def full(shape):
    return pl.BlockSpec(shape, lambda *_: (0,) * len(shape), pipeline_mode=pl.Buffered(1))


def edges_kernel(x0_ref, x1_ref, og0_ref, og1_ref, cov0_ref, cov1_ref, first_ref, last_ref):
    for x_ref, og_ref, cov_ref, out in (
        (x0_ref, og0_ref, cov0_ref, first_ref),
        (x1_ref, og1_ref, cov1_ref, last_ref),
    ):
        out[0] = x_ref[...]
        out[1] = (og_ref[...].astype(F32) * cov_ref[:, :, 0:1][:, None]).astype(BF16)


def edges(x, og, cov):
    rows, hgt, width, ch = x.shape
    part = (rows, hgt, EDGE, ch)
    end = width // EDGE - 1

    def at(shape, block):
        index = (0,) * (len(shape) - 2) + (block, 0)
        return pl.BlockSpec(shape, lambda i: index)

    cov_part = (rows, EDGE, cov.shape[2])
    return pl.pallas_call(
        edges_kernel,
        out_shape=[jax.ShapeDtypeStruct((2,) + part, BF16)] * 2,
        grid=(1,),
        in_specs=[at(part, 0), at(part, end), at(part, 0), at(part, end), at(cov_part, 0), at(cov_part, end)],
        out_specs=[full((2,) + part)] * 2,
        compiler_params=params(60),
        name="edge_columns",
    )(x, x, og, og, cov, cov)


def forward_kernel(
    ends, x_ref, lo_ref, hi_ref, og_ref, cov_ref, wr_ref, wc_ref, we_ref, inner_ref, outer_ref,
    mz_ref, h2_ref, h1_ref, pad_ref, seed_ref, xs, hs, patches, ss,
):
    rows, hgt, width, ch = x_ref.shape
    inner_w = wr_ref.shape[1]
    wide = width + 2 * RIM
    per_row = hgt * wide
    hs[:, 0] = jnp.zeros((rows, width + 2 * EDGE, inner_w), F32)
    hs[:, hgt + 1] = jnp.zeros((rows, width + 2 * EDGE, inner_w), F32)
    sides = (
        (lo_ref.at[0], 0, ends[0]),
        (x_ref, EDGE, None),
        (hi_ref.at[0], EDGE + width, ends[1]),
    )
    for ref, at, keep in sides:
        part = ref[...]
        cols = part.shape[2]
        xs[:, :, at : at + cols] = part.astype(F32)
        pre = dot(part.astype(F32).reshape(-1, ch).astype(BF16), wr_ref[...])
        pre = pre * inner_ref[0:1] + inner_ref[1:2]
        hid = jnp.maximum(pre, 0.0).astype(BF16).astype(F32)
        if keep is not None:
            hid = hid * keep.astype(F32)
        hs[:, 1 : hgt + 1, at : at + cols] = hid.reshape(rows, hgt, cols, inner_w)
    pad_ref[...] = hs[...].astype(BF16)
    first = EDGE - RIM - 1
    for k in range(9):
        dr, dc = divmod(k, 3)
        piece = hs[:, dr : dr + hgt, first + dc : first + dc + wide]
        piece = piece.reshape(-1, inner_w).astype(BF16)
        patches[:, k * inner_w : (k + 1) * inner_w] = piece
        if k == 4:
            h1_ref[...] = piece.reshape(rows, hgt * wide, inner_w)
    pre = dot(patches[...], wc_ref[...]) * inner_ref[2:3] + inner_ref[3:4]
    hid = jnp.maximum(pre, 0.0).astype(BF16)
    h2_ref[...] = hid.reshape(rows, hgt * wide, inner_w)
    for r in range(rows):
        part = hid[r * per_row : (r + 1) * per_row]
        z = dot(part, we_ref[...]) * outer_ref[0:1] + outer_ref[1:2]
        z = z + xs[r, :, EDGE - RIM : EDGE - RIM + wide].reshape(per_row, ch)
        mz_ref[r] = jnp.where(z > 0, 1.0, 0.0).astype(BF16)
        ss[:, 0:EDGE] = lo_ref[1, r].astype(F32)
        ss[:, EDGE : EDGE + width] = og_ref[r].astype(F32) * cov_ref[r, :, 0:1][None]
        ss[:, EDGE + width :] = hi_ref[1, r].astype(F32)
        seed_ref[r] = ss[:, EDGE - RIM : EDGE - RIM + wide].reshape(per_row, ch).astype(BF16)


def forward(ends, x, lo, hi, og, cov, wr, wc, we, inner, outer):
    rows, hgt, width, ch = x.shape
    inner_w = wr.shape[1]
    wide = width + 2 * RIM
    pos = hgt * wide
    out_shapes = (
        (rows, pos, ch),
        (rows, pos, inner_w),
        (rows, pos, inner_w),
        (rows, hgt + 2, width + 2 * EDGE, inner_w),
        (rows, pos, ch),
    )
    args = (x, lo, hi, og, cov, wr, wc, we, inner, outer)
    return pl.pallas_call(
        forward_kernel,
        out_shape=[jax.ShapeDtypeStruct(s, BF16) for s in out_shapes],
        grid_spec=pltpu.PrefetchScalarGridSpec(
            num_scalar_prefetch=1,
            grid=(1,),
            in_specs=[full(a.shape) for a in args],
            out_specs=[full(s) for s in out_shapes],
            scratch_shapes=[
                pltpu.VMEM((rows, hgt, width + 2 * EDGE, ch), F32),
                pltpu.VMEM((rows, hgt + 2, width + 2 * EDGE, inner_w), F32),
                pltpu.VMEM((rows * pos, 9 * inner_w), BF16),
                pltpu.VMEM((hgt, width + 2 * EDGE, ch), F32),
            ],
        ),
        compiler_params=params(32),
        cost_estimate=pl.CostEstimate(flops=2_000_000_000, bytes_accessed=12_000_000, transcendentals=0),
        name="forward_all_rows",
    )(ends, *args)


def chain_kernel(
    info, gy_ref, seed_ref, mz_ref, h2_ref, h1_ref, wet_ref, wct_ref, wrt_ref, inner_ref, outer_ref,
    wire_ref, gi_ref, g3_ref, g2_ref, g1_ref, wide_s, pad_s,
):
    pos, ch = gy_ref.shape
    inner_w = wet_ref.shape[1]
    hgt, wide = wide_s.shape[:2]
    width = wide - 2 * RIM
    lead = 8

    def center(value):
        lanes = value.shape[1]
        wide_s[:, :, :lanes] = value.reshape(hgt, wide, lanes)
        return wide_s[:, RIM : RIM + width, :lanes].reshape(hgt * width, lanes).astype(BF16)

    gy = jnp.where(info[1] == 1, seed_ref[0], gy_ref[...]).astype(F32)
    gz = gy * mz_ref[0].astype(F32)
    g3 = (gz * outer_ref[0:1]).astype(BF16)
    g3_ref[...] = center(g3.astype(F32))
    g2 = jnp.where(h2_ref[0].astype(F32) > 0, dot(g3, wet_ref[...]) * inner_ref[2:3], 0.0)
    g2 = g2.astype(BF16).astype(F32)
    pad_s[...] = jnp.zeros_like(pad_s)
    pad_s[1 : hgt + 1, lead : lead + wide] = g2.reshape(hgt, wide, inner_w)
    g2_ref[...] = (
        pad_s[1 : hgt + 1, lead + RIM : lead + RIM + width].reshape(hgt * width, inner_w).astype(BF16)
    )
    pieces = []
    for k in range(9):
        dr, dc = divmod(k, 3)
        piece = pad_s[2 - dr : 2 - dr + hgt, lead + 1 - dc : lead + 1 - dc + wide]
        pieces.append(piece.reshape(pos, inner_w).astype(BF16))
    back = dot(jnp.concatenate(pieces, axis=1), wct_ref[...])
    g1 = jnp.where(h1_ref[0].astype(F32) > 0, back * inner_ref[0:1], 0.0).astype(BF16)
    g1_ref[...] = center(g1.astype(F32))
    gi = gz + dot(g1, wrt_ref[...])
    wire_ref[...] = gi.astype(BF16)
    gi_ref[...] = center(gi)


def chain_step(info, gy, seed, mz, h2, h1, wet, wct, wrt, inner, outer, hgt):
    pos, ch = gy.shape
    inner_w = wet.shape[1]
    wide = pos // hgt
    kept = hgt * (wide - 2 * RIM)

    def row(lanes):
        return pl.BlockSpec((1, pos, lanes), lambda i, info: (info[0], 0, 0))

    const = (wet, wct, wrt, inner, outer)
    out_shapes = (gy.shape, (kept, ch), (kept, ch), (kept, inner_w), (kept, inner_w))
    return pl.pallas_call(
        chain_kernel,
        out_shape=[jax.ShapeDtypeStruct(s, BF16) for s in out_shapes],
        grid_spec=pltpu.PrefetchScalarGridSpec(
            num_scalar_prefetch=1,
            grid=(1,),
            in_specs=[full(gy.shape), row(ch), row(ch), row(inner_w), row(inner_w)]
            + [full(c.shape) for c in const],
            out_specs=[full(s) for s in out_shapes],
            scratch_shapes=[
                pltpu.VMEM((hgt, wide, ch), F32),
                pltpu.VMEM((hgt + 2, wide + 16, inner_w), F32),
            ],
        ),
        compiler_params=params(24),
        cost_estimate=pl.CostEstimate(flops=360_000_000, bytes_accessed=5_000_000, transcendentals=0),
        name="chain_row",
    )(info, gy, seed, mz, h2, h1, *const)


def picks(inner_w, z):
    row = jnp.arange(inner_w)
    each = row % 4
    own = jnp.asarray(Z_ORDER, row.dtype)[(row // 4) % Z] ^ z
    mid = (row // (4 * Z)) % 4
    core = row // (4 * Z * 4)
    whole = ((mid * Z + own) * CORES + core) * 4 + each
    part = (own * CORES + core) * 16 + mid * 4 + each
    return (jnp.stack([whole, part])[:, :, None] == row[None, None]).astype(BF16)


def turn_kernel(x_ref, pad_ref, h2_ref, pick_ref, xt_ref, pt_ref, ht_ref):
    rows, hgt, width, ch = x_ref.shape
    inner_w = h2_ref.shape[2]
    half = inner_w // CORES
    wide = width + 2 * RIM

    def turned(order, value, ref, at, stride):
        out = lax.dot_general(
            pick_ref[order], value, (((1,), (1,)), ((), ())), preferred_element_type=F32
        ).astype(BF16)
        for core in range(CORES):
            ref[core * stride + at : core * stride + at + half] = out[core * half : (core + 1) * half]

    flat = x_ref[...].astype(F32).reshape(-1, ch).astype(BF16)
    for part in range(ch // inner_w):
        turned(1, flat[:, part * inner_w : (part + 1) * inner_w], xt_ref, part * half, ch // CORES)
    padded = pad_ref[...].astype(F32)
    for k in range(9):
        dr, dc = divmod(k, 3)
        piece = padded[:, dr : dr + hgt, EDGE - 1 + dc : EDGE - 1 + dc + width]
        turned(0, piece.reshape(-1, inner_w).astype(BF16), pt_ref, k * half, 9 * half)
    h2 = h2_ref[...].astype(F32).reshape(rows * hgt, wide, inner_w)[:, RIM : RIM + width]
    turned(0, h2.reshape(-1, inner_w).astype(BF16), ht_ref, 0, half)


def turn(x, pad, h2, pick):
    rows, hgt, width, ch = x.shape
    inner_w = h2.shape[2]
    pos = rows * hgt * width
    args = (x, pad, h2, pick)
    shapes = ((ch, pos), (9 * inner_w, pos), (inner_w, pos))
    return pl.pallas_call(
        turn_kernel,
        out_shape=[jax.ShapeDtypeStruct(s, BF16) for s in shapes],
        grid=(1,),
        in_specs=[full(a.shape) for a in args],
        out_specs=[full(s) for s in shapes],
        compiler_params=params(32),
        cost_estimate=pl.CostEstimate(flops=2_000_000_000, bytes_accessed=8_000_000, transcendentals=0),
        name="turn_activations",
    )(*args)


def place(segment, target, x):
    as_int = lambda cond: jnp.where(cond, 1, 0)
    if segment < A_SEGS:
        side = as_int((x == 1) | (x == 2))
        keep = as_int(side == (1 if target in (1, 2) else 0))
        last = as_int(x // 2 == target // 2)
        return ((keep * 2 + last) * A_SEGS + segment) * 32
    keep = as_int(x // 2 == target // 2)
    same = as_int(x % 2 == target % 2)
    last = jnp.where(keep == 1, same, 1 - same)
    return X * A_SEGS * 32 + ((keep * 2 + last) * (SEGS - A_SEGS) + segment - A_SEGS) * 32


def weights_kernel(slots, info, xt_ref, pt_ref, ht_ref, *refs):
    by_slot = [refs[i * slots : (i + 1) * slots] for i in range(4)]
    keep_ref, send_ref, gi_ref, g3_s, g2_s, g1_s, sems = refs[4 * slots :]
    core, x, section = info[0], info[1], info[2]
    rows, kept, ch = gi_ref.shape
    inner_w = ht_ref.shape[0]
    half = inner_w // CORES
    into = (g1_s, g2_s, g3_s, gi_ref)

    def copy(which, r, slot):
        return pltpu.make_async_copy(by_slot[which][slot], into[which].at[r], sems.at[which, r])

    sections = (slots - rows) // LAG + 1
    for s in range(sections):
        @pl.when(section == s)
        def _():
            for which in range(4):
                for r in range(rows):
                    copy(which, r, LAG * (sections - 1 - s) + r).start()

    def arrived(which):
        for r in range(rows):
            copy(which, r, r).wait()
        if which < 3:
            return into[which][...].reshape(rows * kept, into[which].shape[2])

    outs = ((keep_ref, core), (send_ref, 1 - core))

    def put(ref, target, segment, value):
        at = pl.multiple_of(place(segment, target, x), 32)
        ref[pl.ds(at, value.shape[0])] = value.astype(BF16)

    g1 = arrived(0)
    for ref, side in outs:
        total = dot(xt_ref[pl.ds(pl.multiple_of(side * (ch // CORES), half), ch // CORES)], g1)
        for target in range(X):
            put(ref, target, 0, total[target * half : (target + 1) * half])
    g2 = arrived(1)
    for ref, side in outs:
        total = dot(pt_ref[pl.ds(pl.multiple_of(side * 9 * half, half), 9 * half)], g2)
        for k in range(9):
            for target in range(X):
                at = k * half + target * 32
                put(ref, target, 4 + k, total[at : at + 32])
    g3 = arrived(2)
    for ref, side in outs:
        total = dot(ht_ref[pl.ds(pl.multiple_of(side * half, half), half)], g3)
        for j in range(4):
            for target in range(X):
                part = total[target * 32 : target * 32 + 32, j * inner_w : (j + 1) * inner_w]
                put(ref, target, 13 + j, part)
    arrived(3)


def weight_grads(info, xt, pt, ht, g1, g2, g3, gi, rows):
    inner_w = ht.shape[0]
    slots = len(gi)
    kept, ch = gi[0].shape
    shape = (SEGS * X * 32, inner_w)
    args = (xt, pt, ht)
    return pl.pallas_call(
        functools.partial(weights_kernel, slots),
        out_shape=[jax.ShapeDtypeStruct(s, BF16) for s in (shape, shape, (rows, kept, ch))],
        grid_spec=pltpu.PrefetchScalarGridSpec(
            num_scalar_prefetch=1,
            grid=(1,),
            in_specs=[full(a.shape) for a in args] + [pl.BlockSpec(memory_space=pl.ANY)] * (4 * slots),
            out_specs=[full(shape), full(shape), pl.BlockSpec(memory_space=pl.ANY)],
            scratch_shapes=[
                pltpu.VMEM((rows, kept, ch), BF16),
                pltpu.VMEM((rows, kept, inner_w), BF16),
                pltpu.VMEM((rows, kept, inner_w), BF16),
                pltpu.SemaphoreType.DMA((4, rows)),
            ],
        ),
        compiler_params=params(32),
        cost_estimate=pl.CostEstimate(flops=1_200_000_000, bytes_accessed=8_000_000, transcendentals=0),
        name="weight_gradients",
    )(info, *args, *g1, *g2, *g3, *gi)


def tile_pairs(partner):
    pairs = []
    for x in range(X):
        for z in range(Z):
            for c in range(CORES):
                px, pz, pc = partner(x, z, c)
                pairs.append(((x * Z + z) * CORES + c, (px * Z + pz) * CORES + pc))
    return pairs


def swap(value, partner):
    return lax.ppermute(value.astype(BF16), "tile", tile_pairs(partner))


def scatter_sum(keep, send):
    lanes = keep.shape[-1]
    got = swap(send, lambda x, z, c: (x, z, 1 - c))
    inner_pair = lambda x, z, c: (x ^ 1, z, c)
    outer_pair = lambda x, z, c: (3 - x, z, c)
    cut = X * A_SEGS * 32

    def own(first, last):
        return keep[first:last].astype(F32) + got[first:last].astype(F32)

    half_a, half_b = cut // 2, (keep.shape[0] - cut) // 2
    quart_a, quart_b = half_a // 2, half_b // 2
    got_a = swap(own(0, half_a), inner_pair)
    got_b = swap(own(cut, cut + half_b), outer_pair)
    at_a, at_b = half_a, cut + half_b
    got_a2 = swap(own(at_a, at_a + quart_a) + got_a[:quart_a].astype(F32), outer_pair)
    got_b2 = swap(own(at_b, at_b + quart_b) + got_b[:quart_b].astype(F32), inner_pair)
    part_a = own(at_a + quart_a, cut) + got_a[quart_a:].astype(F32) + got_a2.astype(F32)
    part_b = own(at_b + quart_b, keep.shape[0]) + got_b[quart_b:].astype(F32) + got_b2.astype(F32)
    total = jnp.concatenate([part_a, part_b], axis=0).reshape(SEGS, Z * 4, lanes)
    for bit in (1, 2, 4):
        count = total.shape[1] // 2
        got = swap(total[:, :count], lambda x, z, c, b=bit: (x, z ^ b, c))
        total = total[:, count:] + got.astype(F32)
    g_reduce = total[:4].reshape(16, lanes)
    g_conv = total[4:13].reshape(3, 3, 4, lanes)
    g_expand = total[13:].transpose(1, 0, 2).reshape(4, 4 * lanes)
    return g_reduce, g_conv, g_expand


def neighbours(first, last, tiles):
    pairs = [(i, i + 1) for i in range(tiles - 1)]
    low = lax.ppermute(last, "tile", pairs)
    high = lax.ppermute(first, "tile", [(b, a) for a, b in pairs])
    return low, high


def per_device(block_inputs, out_grad, tissue, w_reduce, w_conv, w_expand, inner_affine, outer_affine):
    section = lax.axis_index("section")
    sections = lax.axis_size("section")
    tile = lax.axis_index("tile")
    tiles = lax.axis_size("tile")
    x = block_inputs[0]
    rows, hgt, width, ch = x.shape
    wr, we = w_reduce[0], w_expand[0]
    inner_w = wr.shape[1]
    wc = w_conv[0].reshape(9 * inner_w, inner_w)
    inner, outer = inner_affine[0], outer_affine[0]
    pos = hgt * (width + 2 * RIM)

    cover = jnp.repeat(tissue.astype(F32), TILE_W, axis=1)[:, :, None]
    cover = jnp.broadcast_to(cover, (rows, width, 128))
    lo, hi = neighbours(*edges(x, out_grad, cover), tiles)

    wet = we.T
    wrt = wr.T
    wct = w_conv[0].transpose(0, 1, 3, 2).reshape(9 * inner_w, inner_w)

    ends = jnp.stack([tile > 0, tile < tiles - 1]).astype(jnp.int32)
    mz, h2, h1, pad, seed = forward(
        ends, x, lo, hi, out_grad, cover, wr, wc, we, inner, outer
    )
    z_now = (tile // CORES) % Z
    xt, pt, ht = turn(x, pad, h2, picks(inner_w, z_now))

    back_one = [(i, i - 1) for i in range(1, sections)]
    slots = rows + LAG * (sections - 1)
    arriving = [jnp.zeros((pos, ch), BF16)] * LAG
    per_slot = []
    for slot in range(slots):
        micro = slot - LAG * (sections - 1 - section)
        info = jnp.stack(
            [jnp.clip(micro, 0, rows - 1), (section == sections - 1).astype(micro.dtype)]
        ).astype(jnp.int32)
        wire, *saved = chain_step(
            info, arriving[slot], seed, mz, h2, h1, wet, wct, wrt, inner, outer, hgt
        )
        per_slot.append(saved)
        if slot + LAG < slots:
            arriving.append(lax.ppermute(wire, "section", back_one))
    gi, g3, g2, g1 = zip(*per_slot)
    info = jnp.stack([tile % CORES, tile // (CORES * Z), section]).astype(jnp.int32)
    keep, send, grad_inputs = weight_grads(info, xt, pt, ht, g1, g2, g3, gi, rows)
    g_reduce, g_conv, g_expand = scatter_sum(keep, send)
    grad_inputs = grad_inputs.reshape(rows, hgt, width, ch)
    return grad_inputs[None], g_reduce[None], g_conv[None], g_expand[None]


def solution(mesh):
    in_specs = (
        P("section", None, None, "tile", None),
        P(None, None, "tile", None),
        P(None, "tile"),
        P("section", None, None),
        P("section", None, None, None, None),
        P("section", None, None),
        P("section", None, None),
        P("section", None, None),
    )
    out_specs = (
        P("section", None, None, "tile", None),
        P("section", "tile", None),
        P("section", None, None, "tile", None),
        P("section", "tile", None),
    )
    return jax.shard_map(
        per_device, mesh=mesh, in_specs=in_specs, out_specs=out_specs, check_vma=False
    )
```

time: 588 us -> 140 us (0.24)
  waiting for transfers between devices: 355 us -> 54.1 us
  starting transfers between devices: 120 us -> 40.1 us
  matrix products: 67 us -> 0 us
  Pallas kernels: 0 us -> 30.1 us
  between operations: 17.6 us -> 1.05 us
  other arithmetic: 11.3 us -> 2.28 us
    unnamed x3 -> x0, waiting for transfers between devices: 182 us -> none
    reduce_scatter x1 -> x0, waiting for transfers between devices: 141 us -> none  [per_device(): lax.psum_scatter(total_r, 'tile', scatter_dimension=0, tiled=True)]
    ppermute x34 -> x18, starting transfers between devices: 120 us -> 40.1 us  [the longest x8 19 us: per_device(): arriving.append(lax.ppermute(wire, 'section', back_one))]
    dot_general x231 -> x0, matrix products: 67 us -> none  [the longest x77 26.8 us: contract(): lax.dot_general(left, right, (((0,), (0,)), ((), ())), preferred_element_...]
    pallas_call x0 -> x14, Pallas kernels: none -> 30.1 us  [the longest x10 18.2 us: chain_step(): pl.pallas_call(chain_kernel, out_shape=[jax.ShapeDtypeStruct(s, BF16) for...]
    ppermute x34 -> x18, waiting for transfers between devices: 32.4 us -> 54.1 us  [the longest x8 27.1 us: swap(): return lax.ppermute(value.astype(BF16), 'tile', tile_pairs(partner))]
  transfers between devices with their start and end apart: 36 -> 18, of which waited for: 8 -> 18; matrix products, arithmetic and copies ran while one was open for 11% -> 3% of each run, Pallas kernels for 0% -> 11%
where the time goes in v1:
time: 140 us; the launch traced here: 138 us
  waiting for transfers between devices  54.1 us (39%)
  starting transfers between devices  40.1 us (29%)
  Pallas kernels  30.1 us (22%)
  local copies, waits for them, and re-layouts  10.7 us (8%)
  other arithmetic  2.28 us (2%)
    ppermute x8, waiting for transfers between devices, swap(): return lax.ppermute(value.astype(BF16), 'tile', tile_pairs(partner))  27.1 us
    ppermute x8, waiting for transfers between devices, per_device(): arriving.append(lax.ppermute(wire, 'section', back_one))  24.1 us
    ppermute x8, starting transfers between devices, per_device(): arriving.append(lax.ppermute(wire, 'section', back_one))  19 us
    pallas_call x10, Pallas kernels, chain_step(): pl.pallas_call(chain_kernel, out_shape=[jax.ShapeDtypeStruct(s, BF16) for...  18.2 us
    ppermute x8, starting transfers between devices, swap(): return lax.ppermute(value.astype(BF16), 'tile', tile_pairs(partner))  11.7 us
    ppermute x1, starting transfers between devices, neighbours(): high = lax.ppermute(first, 'tile', [(b, a) for a, b in pairs])  7.47 us
    unnamed x20, local copies, waits for them, and re-layouts  7.18 us
    pallas_call x1, Pallas kernels, forward(): pl.pallas_call(forward_kernel, out_shape=[jax.ShapeDtypeStruct(s, BF16) f...  5.02 us
  transfers between devices with their start and end apart: 18, of which 18 were waited for; matrix products, arithmetic and copies ran while one was open for 3% of the time, Pallas kernels for 11%

profile of v1, /device:TPU:22, one launch (start us, length us, event | category | flops | bytes accessed | tf_op | source)
XLA Modules:
  0.0 138.3 jit_solution(2182319032774848900)
XLA Ops:
  2.2 2.4 %edge_columns.1 = (bf16[2,4,4,8,1024]{4,3,2,1,0:T(8,128)(2,1)}, bf16[2,4,4,8,1024]{4,3,2,1,0:T(8,128)(2,1)}) custom-call(bf16[4,4,32,1024]{3,2,1,0:T(8,128)(2,1)} %bitcast.70, bf16[4,4,32,1024]{3,2,1,0:T(8,128)(2,1)} %bitcast.71, bf16[4,4,32,1024]{3,2,1,0:T(8,128)(2,1)} %og_ref.1, bf16[4,4,32,1024]{3,2,1,0:T(8,128)(2,1)} %og_ref.1, ...), custom_call_target="tpu_custom_call" | custom-call | tf_op jit(solution)/shard_map/edge_columns/pallas_call | solution.py:51
  4.5 1.9 %collective-permute-start = (bf16[2,4,4,8,1024]{4,3,2,1,0:T(8,128)(2,1)}, bf16[2,4,4,8,1024]{4,3,2,1,0:T(8,128)(2,1)}, u32[]{:S(2)}, u32[]{:S(2)}) collective-permute-start(bf16[2,4,4,8,1024]{4,3,2,1,0:T(8,128)(2,1)} %get-tuple-element.65), channel_id=1, source_target_pairs={{0,4},{4,8},{8,12},{12,16},{16,20},{20,24},{24,28},{28,32},{32,36}... | collective-permute-start | bytes 1572872 | tf_op jit(solution)/shard_map/ppermute | solution.py:408
  6.5 7.5 %collective-permute-start.1 = (bf16[2,4,4,8,1024]{4,3,2,1,0:T(8,128)(2,1)}, bf16[2,4,4,8,1024]{4,3,2,1,0:T(8,128)(2,1)}, u32[]{:S(2)}, u32[]{:S(2)}) collective-permute-start(bf16[2,4,4,8,1024]{4,3,2,1,0:T(8,128)(2,1)} %get-tuple-element.66), channel_id=1, source_target_pairs={{4,0},{8,4},{12,8},{16,12},{20,16},{24,20},{28,24},{32,28},{36,32}... | collective-permute-start | bytes 1572872 | tf_op jit(solution)/shard_map/ppermute | solution.py:409
  19.2 1.8 %collective-permute-done.1.hi_ref = bf16[2,4,4,8,1024]{4,3,2,1,0:T(8,128)(2,1)} collective-permute-done((bf16[2,4,4,8,1024]{4,3,2,1,0:T(8,128)(2,1)}, bf16[2,4,4,8,1024]{4,3,2,1,0:T(8,128)(2,1)}, u32[]{:S(2)}, u32[]{:S(2)}) %collective-permute-start.1) | collective-permute-done | bytes 524320 | tf_op jit(solution)/shard_map/ppermute | solution.py:409
  25.5 5.0 %forward_all_rows.1 = (bf16[4,160,1024]{2,1,0:T(8,128)(2,1)S(1)}, bf16[4,160,256]{2,1,0:T(8,128)(2,1)S(1)}, bf16[4,160,256]{2,1,0:T(8,128)(2,1)S(1)}, bf16[4,6,4...) custom-call(s32[2]{0:T(128)S(1)} %add_convert_fusion.4.ends, bf16[4,4,32,1024]{3,2,1,0:T(8,128)(2,1)S(1)} %bitcast.72, ...), custom_call_target="tpu_custom_call" | custom-call | flops 2000000000 | bytes 12000000 | tf_op jit(solution)/shard_map/forward_all_rows/pallas_call | solution.py:123
  32.3 2.4 %collective-permute-start.3 = (bf16[160,1024]{1,0:T(8,128)(2,1)S(1)}, bf16[160,1024]{1,0:T(8,128)(2,1)S(1)}, u32[]{:S(2)}, u32[]{:S(2)}) collective-permute-start(bf16[160,1024]{1,0:T(8,128)(2,1)S(1)} %get-tuple-element.79), channel_id=1, source_target_pairs={{1,0},{2,1},{3,2},{5,4},{6,5},{7,6},{9,8},{10,9},{11,10},{13,12},{... | collective-permute-start | bytes 983048 | tf_op jit(solution)/shard_map/ppermute | solution.py:455
  36.3 2.4 %collective-permute-start.2 = (bf16[160,1024]{1,0:T(8,128)(2,1)S(1)}, bf16[160,1024]{1,0:T(8,128)(2,1)S(1)}, u32[]{:S(2)}, u32[]{:S(2)}) collective-permute-start(bf16[160,1024]{1,0:T(8,128)(2,1)S(1)} %get-tuple-element.77), channel_id=1, source_target_pairs={{1,0},{2,1},{3,2},{5,4},{6,5},{7,6},{9,8},{10,9},{11,10},{13,12},{... | collective-permute-start | bytes 983048 | tf_op jit(solution)/shard_map/ppermute | solution.py:455
  38.8 6.0 %collective-permute-done.3.gy_ref = bf16[160,1024]{1,0:T(8,128)(2,1)S(1)} collective-permute-done((bf16[160,1024]{1,0:T(8,128)(2,1)S(1)}, bf16[160,1024]{1,0:T(8,128)(2,1)S(1)}, u32[]{:S(2)}, u32[]{:S(2)}) %collective-permute-start.3) | collective-permute-done | bytes 327712 | tf_op jit(solution)/shard_map/ppermute | solution.py:455
  46.5 2.4 %collective-permute-start.5 = (bf16[160,1024]{1,0:T(8,128)(2,1)S(1)}, bf16[160,1024]{1,0:T(8,128)(2,1)S(1)}, u32[]{:S(2)}, u32[]{:S(2)}) collective-permute-start(bf16[160,1024]{1,0:T(8,128)(2,1)S(1)} %get-tuple-element.83), channel_id=1, source_target_pairs={{1,0},{2,1},{3,2},{5,4},{6,5},{7,6},{9,8},{10,9},{11,10},{13,12},{... | collective-permute-start | bytes 983048 | tf_op jit(solution)/shard_map/ppermute | solution.py:455
  48.9 3.0 %collective-permute-done.2.gy_ref = bf16[160,1024]{1,0:T(8,128)(2,1)S(1)} collective-permute-done((bf16[160,1024]{1,0:T(8,128)(2,1)S(1)}, bf16[160,1024]{1,0:T(8,128)(2,1)S(1)}, u32[]{:S(2)}, u32[]{:S(2)}) %collective-permute-start.2) | collective-permute-done | bytes 327712 | tf_op jit(solution)/shard_map/ppermute | solution.py:455
  53.5 2.4 %collective-permute-start.4 = (bf16[160,1024]{1,0:T(8,128)(2,1)S(1)}, bf16[160,1024]{1,0:T(8,128)(2,1)S(1)}, u32[]{:S(2)}, u32[]{:S(2)}) collective-permute-start(bf16[160,1024]{1,0:T(8,128)(2,1)S(1)} %get-tuple-element.81), channel_id=1, source_target_pairs={{1,0},{2,1},{3,2},{5,4},{6,5},{7,6},{9,8},{10,9},{11,10},{13,12},{... | collective-permute-start | bytes 983048 | tf_op jit(solution)/shard_map/ppermute | solution.py:455
  55.9 3.1 %collective-permute-done.5.gy_ref = bf16[160,1024]{1,0:T(8,128)(2,1)S(1)} collective-permute-done((bf16[160,1024]{1,0:T(8,128)(2,1)S(1)}, bf16[160,1024]{1,0:T(8,128)(2,1)S(1)}, u32[]{:S(2)}, u32[]{:S(2)}) %collective-permute-start.5) | collective-permute-done | bytes 327712 | tf_op jit(solution)/shard_map/ppermute | solution.py:455
  60.7 2.4 %collective-permute-start.7 = (bf16[160,1024]{1,0:T(8,128)(2,1)S(1)}, bf16[160,1024]{1,0:T(8,128)(2,1)S(1)}, u32[]{:S(2)}, u32[]{:S(2)}) collective-permute-start(bf16[160,1024]{1,0:T(8,128)(2,1)S(1)} %get-tuple-element.87), channel_id=1, source_target_pairs={{1,0},{2,1},{3,2},{5,4},{6,5},{7,6},{9,8},{10,9},{11,10},{13,12},{... | collective-permute-start | bytes 983048 | tf_op jit(solution)/shard_map/ppermute | solution.py:455
  63.1 3.0 %collective-permute-done.4.gy_ref = bf16[160,1024]{1,0:T(8,128)(2,1)S(1)} collective-permute-done((bf16[160,1024]{1,0:T(8,128)(2,1)S(1)}, bf16[160,1024]{1,0:T(8,128)(2,1)S(1)}, u32[]{:S(2)}, u32[]{:S(2)}) %collective-permute-start.4) | collective-permute-done | bytes 327712 | tf_op jit(solution)/shard_map/ppermute | solution.py:455
  67.8 2.4 %collective-permute-start.6 = (bf16[160,1024]{1,0:T(8,128)(2,1)S(1)}, bf16[160,1024]{1,0:T(8,128)(2,1)S(1)}, u32[]{:S(2)}, u32[]{:S(2)}) collective-permute-start(bf16[160,1024]{1,0:T(8,128)(2,1)S(1)} %get-tuple-element.85), channel_id=1, source_target_pairs={{1,0},{2,1},{3,2},{5,4},{6,5},{7,6},{9,8},{10,9},{11,10},{13,12},{... | collective-permute-start | bytes 983048 | tf_op jit(solution)/shard_map/ppermute | solution.py:455
  70.3 2.9 %collective-permute-done.7.gy_ref = bf16[160,1024]{1,0:T(8,128)(2,1)S(1)} collective-permute-done((bf16[160,1024]{1,0:T(8,128)(2,1)S(1)}, bf16[160,1024]{1,0:T(8,128)(2,1)S(1)}, u32[]{:S(2)}, u32[]{:S(2)}) %collective-permute-start.7) | collective-permute-done | bytes 327712 | tf_op jit(solution)/shard_map/ppermute | solution.py:455
  75.0 2.5 %collective-permute-start.9 = (bf16[160,1024]{1,0:T(8,128)(2,1)S(1)}, bf16[160,1024]{1,0:T(8,128)(2,1)S(1)}, u32[]{:S(2)}, u32[]{:S(2)}) collective-permute-start(bf16[160,1024]{1,0:T(8,128)(2,1)S(1)} %get-tuple-element.91), channel_id=1, source_target_pairs={{1,0},{2,1},{3,2},{5,4},{6,5},{7,6},{9,8},{10,9},{11,10},{13,12},{... | collective-permute-start | bytes 983048 | tf_op jit(solution)/shard_map/ppermute | solution.py:455
  77.5 2.8 %collective-permute-done.6.gy_ref = bf16[160,1024]{1,0:T(8,128)(2,1)S(1)} collective-permute-done((bf16[160,1024]{1,0:T(8,128)(2,1)S(1)}, bf16[160,1024]{1,0:T(8,128)(2,1)S(1)}, u32[]{:S(2)}, u32[]{:S(2)}) %collective-permute-start.6) | collective-permute-done | bytes 327712 | tf_op jit(solution)/shard_map/ppermute | solution.py:455
  82.0 2.4 %collective-permute-start.8 = (bf16[160,1024]{1,0:T(8,128)(2,1)S(1)}, bf16[160,1024]{1,0:T(8,128)(2,1)S(1)}, u32[]{:S(2)}, u32[]{:S(2)}) collective-permute-start(bf16[160,1024]{1,0:T(8,128)(2,1)S(1)} %get-tuple-element.89), channel_id=1, source_target_pairs={{1,0},{2,1},{3,2},{5,4},{6,5},{7,6},{9,8},{10,9},{11,10},{13,12},{... | collective-permute-start | bytes 983048 | tf_op jit(solution)/shard_map/ppermute | solution.py:455
  85.6 1.9 %collective-permute-done.9.gy_ref = bf16[160,1024]{1,0:T(8,128)(2,1)S(1)} collective-permute-done((bf16[160,1024]{1,0:T(8,128)(2,1)S(1)}, bf16[160,1024]{1,0:T(8,128)(2,1)S(1)}, u32[]{:S(2)}, u32[]{:S(2)}) %collective-permute-start.9) | collective-permute-done | bytes 327712 | tf_op jit(solution)/shard_map/ppermute | solution.py:455
  87.5 2.4 %chain_row.19 = (bf16[160,1024]{1,0:T(8,128)(2,1)}, bf16[128,1024]{1,0:T(8,128)(2,1)S(1)}, bf16[128,1024]{1,0:T(8,128)(2,1)S(1)}, bf16[128,256]{1,0:T(8,128)(2,1)S(1)}, bf16[128,256]{1,0:T(8,128)(2,1)S(1)}) custom-call(s32[2]{0:T(128)S(1)} %pad_add_fusion.11.info, bf16[160,1024]{1,0:T(8,128)(2,1)S(1)} %collective-permute-done.9.gy_ref, ...), custom_call_target="tpu_custom_call" | custom-call | flops 360000000 | bytes 5000000 | tf_op jit(solution)/shard_map/chain_row/pallas_call | solution.py:194
  91.3 2.4 %chain_row.18 = (bf16[160,1024]{1,0:T(8,128)(2,1)}, bf16[128,1024]{1,0:T(8,128)(2,1)S(1)}, bf16[128,1024]{1,0:T(8,128)(2,1)S(1)}, bf16[128,256]{1,0:T(8,128)(2,1)S(1)}, bf16[128,256]{1,0:T(8,128)(2,1)S(1)}) custom-call(s32[2]{0:T(128)S(1)} %pad_add_fusion.10.info, bf16[160,1024]{1,0:T(8,128)(2,1)S(1)} %collective-permute-done.8.gy_ref, ...), custom_call_target="tpu_custom_call" | custom-call | flops 360000000 | bytes 5000000 | tf_op jit(solution)/shard_map/chain_row/pallas_call | solution.py:194
  93.7 3.3 %weight_gradients.1 = (bf16[2176,256]{1,0:T(8,128)(2,1)S(1)}, bf16[2176,256]{1,0:T(8,128)(2,1)S(1)}, bf16[4,128,1024]{2,1,0:T(8,128)(2,1)}) custom-call(s32[3]{0:T(128)S(1)} %pad_add_fusion.1.info, bf16[1024,512]{1,0:T(8,128)(2,1)S(1)} %get-tuple-element.69.xt_ref, bf16[2304,512]{1,0:T(8,128)(2,1)S(1)} %get-tuple-element.70.pt_ref, ...), custom_call_target="tpu_custom_call" | custom-call | flops 1200000000 | bytes 8000000 | tf_op jit(solution)/shard_map/weight_gradients/pallas_call | solution.py:341
  97.1 2.7 %collective-permute-done.10 = bf16[2176,256]{1,0:T(8,128)(2,1)S(1)} collective-permute-done((bf16[2176,256]{1,0:T(8,128)(2,1)S(1)}, bf16[2176,256]{1,0:T(8,128)(2,1)S(1)}, u32[]{:S(2)}, u32[]{:S(2)}) %collective-permute-start.10) | collective-permute-done | bytes 1114144 | tf_op jit(solution)/shard_map/ppermute | solution.py:373
  102.2 6.2 %collective-permute-done.11 = bf16[512,256]{1,0:T(8,128)(2,1)S(1)} collective-permute-done((bf16[512,256]{1,0:T(8,128)(2,1)S(1)}, bf16[512,256]{1,0:T(8,128)(2,1)S(1)}, u32[]{:S(2)}, u32[]{:S(2)}) %collective-permute-start.11) | collective-permute-done | bytes 262176 | tf_op jit(solution)/shard_map/ppermute | solution.py:373
  108.8 2.3 %collective-permute-done.13 = bf16[576,256]{1,0:T(8,128)(2,1)S(1)} collective-permute-done((bf16[576,256]{1,0:T(8,128)(2,1)S(1)}, bf16[576,256]{1,0:T(8,128)(2,1)S(1)}, u32[]{:S(2)}, u32[]{:S(2)}) %collective-permute-start.13) | collective-permute-done | bytes 294944 | tf_op jit(solution)/shard_map/ppermute | solution.py:373
  111.2 3.5 %collective-permute-done.12 = bf16[256,256]{1,0:T(8,128)(2,1)S(1)} collective-permute-done((bf16[256,256]{1,0:T(8,128)(2,1)S(1)}, bf16[256,256]{1,0:T(8,128)(2,1)S(1)}, u32[]{:S(2)}, u32[]{:S(2)}) %collective-permute-start.12) | collective-permute-done | bytes 131104 | tf_op jit(solution)/shard_map/ppermute | solution.py:373
  116.9 4.7 %collective-permute-done.15 = bf16[17,16,256]{2,1,0:T(8,128)(2,1)S(1)} collective-permute-done((bf16[17,16,256]{2,1,0:T(8,128)(2,1)S(1)}, bf16[17,16,256]{2,1,0:T(8,128)(2,1)S(1)}, u32[]{:S(2)}, u32[]{:S(2)}) %collective-permute-start.15) | collective-permute-done | bytes 139296 | tf_op jit(solution)/shard_map/ppermute | solution.py:373
  121.7 1.8 %collective-permute-start.16 = (bf16[17,8,256]{2,1,0:T(8,128)(2,1)S(1)}, bf16[17,8,256]{2,1,0:T(8,128)(2,1)S(1)}, u32[]{:S(2)}, u32[]{:S(2)}) collective-permute-start(bf16[17,8,256]{2,1,0:T(8,128)(2,1)S(1)} %slice.154), channel_id=1, source_target_pairs={{0,16},{4,20},{8,24},{12,28},{16,0},{20,4},{24,8},{28,12},{32,48},... | collective-permute-start | bytes 208904 | tf_op jit(solution)/shard_map/ppermute | solution.py:373
  123.5 4.2 %collective-permute-done.16 = bf16[17,8,256]{2,1,0:T(8,128)(2,1)S(1)} collective-permute-done((bf16[17,8,256]{2,1,0:T(8,128)(2,1)S(1)}, bf16[17,8,256]{2,1,0:T(8,128)(2,1)S(1)}, u32[]{:S(2)}, u32[]{:S(2)}) %collective-permute-start.16) | collective-permute-done | bytes 69664 | tf_op jit(solution)/shard_map/ppermute | solution.py:373
  127.7 6.8 %collective-permute-start.17 = (bf16[17,4,256]{2,1,0:T(4,128)(2,1)S(1)}, bf16[17,4,256]{2,1,0:T(4,128)(2,1)S(1)}, u32[]{:S(2)}, u32[]{:S(2)}) collective-permute-start(bf16[17,4,256]{2,1,0:T(4,128)(2,1)S(1)} %slice.155), channel_id=1, source_target_pairs={{0,32},{4,36},{8,40},{12,44},{16,48},{20,52},{24,56},{28,60},{32,0... | collective-permute-start | bytes 104456 | tf_op jit(solution)/shard_map/ppermute | solution.py:373
  134.5 1.9 %collective-permute-done.17 = bf16[17,4,256]{2,1,0:T(4,128)(2,1)S(1)} collective-permute-done((bf16[17,4,256]{2,1,0:T(4,128)(2,1)S(1)}, bf16[17,4,256]{2,1,0:T(4,128)(2,1)S(1)}, u32[]{:S(2)}, u32[]{:S(2)}) %collective-permute-start.17) | collective-permute-done | bytes 34848 | tf_op jit(solution)/shard_map/ppermute | solution.py:373
  (77 shorter events, 34.7 us)
Async XLA Ops:
  2.2 11.9 %copy-start.2 = (bf16[1,3,3,256,256]{4,3,2,1,0:T(8,128)(2,1)S(1)}, bf16[1,3,3,256,256]{4,3,2,1,0:T(8,128)(2,1)}, u32[]{:S(2)}) copy-start(bf16[1,3,3,256,256]{4,3,2,1,0:T(8,128)(2,1)} %param.13) | copy-start | bytes 3538948
  4.5 14.6 %collective-permute-start = (bf16[2,4,4,8,1024]{4,3,2,1,0:T(8,128)(2,1)}, bf16[2,4,4,8,1024]{4,3,2,1,0:T(8,128)(2,1)}, u32[]{:S(2)}, u32[]{:S(2)}) collective-permute-start(bf16[2,4,4,8,1024]{4,3,2,1,0:T(8,128)(2,1)} %get-tuple-element.65), channel_id=1, source_target_pairs={{0,4},{4,8},{8,12},{12,16},{16,20},{20,24},{24,28},{28,32},{32,36}... | collective-permute-start | bytes 1572872 | tf_op jit(solution)/shard_map/ppermute | solution.py:408
  6.5 14.5 %collective-permute-start.1 = (bf16[2,4,4,8,1024]{4,3,2,1,0:T(8,128)(2,1)}, bf16[2,4,4,8,1024]{4,3,2,1,0:T(8,128)(2,1)}, u32[]{:S(2)}, u32[]{:S(2)}) collective-permute-start(bf16[2,4,4,8,1024]{4,3,2,1,0:T(8,128)(2,1)} %get-tuple-element.66), channel_id=1, source_target_pairs={{4,0},{8,4},{12,8},{16,12},{20,16},{24,20},{28,24},{32,28},{36,32}... | collective-permute-start | bytes 1572872 | tf_op jit(solution)/shard_map/ppermute | solution.py:409
  14.8 6.2 %copy-start = (bf16[4,4,32,1024]{3,2,1,0:T(8,128)(2,1)S(1)}, bf16[4,4,32,1024]{3,2,1,0:T(8,128)(2,1)}, u32[]{:S(2)}) copy-start(bf16[4,4,32,1024]{3,2,1,0:T(8,128)(2,1)} %og_ref.1) | copy-start | bytes 3145732
  14.8 6.1 %copy-start.4 = (f32[1,2,1024]{2,1,0:T(2,128)S(1)}, f32[1,2,1024]{2,1,0:T(2,128)}, u32[]{:S(2)}) copy-start(f32[1,2,1024]{2,1,0:T(2,128)} %param.16) | copy-start | bytes 24580
  14.8 6.1 %copy-start.5 = (f32[4,32,128]{2,1,0:T(8,128)S(1)}, f32[4,32,128]{2,1,0:T(8,128)}, u32[]{:S(2)}) copy-start(f32[4,32,128]{2,1,0:T(8,128)} %broadcast_in_dim.18.cov0_ref.cov1_ref.cov_ref) | copy-start | bytes 196612
  14.8 6.1 %copy-start.8 = (f32[1,4,256]{2,1,0:T(4,128)S(1)}, f32[1,4,256]{2,1,0:T(4,128)}, u32[]{:S(2)}) copy-start(f32[1,4,256]{2,1,0:T(4,128)} %param.15) | copy-start | bytes 12292
  21.0 1.2 copy-start.1
  22.2 1.3 copy-start.3
  23.5 1.0 copy-start.6
  24.5 1.0 copy-start.7
  32.3 12.5 %collective-permute-start.3 = (bf16[160,1024]{1,0:T(8,128)(2,1)S(1)}, bf16[160,1024]{1,0:T(8,128)(2,1)S(1)}, u32[]{:S(2)}, u32[]{:S(2)}) collective-permute-start(bf16[160,1024]{1,0:T(8,128)(2,1)S(1)} %get-tuple-element.79), channel_id=1, source_target_pairs={{1,0},{2,1},{3,2},{5,4},{6,5},{7,6},{9,8},{10,9},{11,10},{13,12},{... | collective-permute-start | bytes 983048 | tf_op jit(solution)/shard_map/ppermute | solution.py:455
  36.3 15.5 %collective-permute-start.2 = (bf16[160,1024]{1,0:T(8,128)(2,1)S(1)}, bf16[160,1024]{1,0:T(8,128)(2,1)S(1)}, u32[]{:S(2)}, u32[]{:S(2)}) collective-permute-start(bf16[160,1024]{1,0:T(8,128)(2,1)S(1)} %get-tuple-element.77), channel_id=1, source_target_pairs={{1,0},{2,1},{3,2},{5,4},{6,5},{7,6},{9,8},{10,9},{11,10},{13,12},{... | collective-permute-start | bytes 983048 | tf_op jit(solution)/shard_map/ppermute | solution.py:455
  46.5 12.5 %collective-permute-start.5 = (bf16[160,1024]{1,0:T(8,128)(2,1)S(1)}, bf16[160,1024]{1,0:T(8,128)(2,1)S(1)}, u32[]{:S(2)}, u32[]{:S(2)}) collective-permute-start(bf16[160,1024]{1,0:T(8,128)(2,1)S(1)} %get-tuple-element.83), channel_id=1, source_target_pairs={{1,0},{2,1},{3,2},{5,4},{6,5},{7,6},{9,8},{10,9},{11,10},{13,12},{... | collective-permute-start | bytes 983048 | tf_op jit(solution)/shard_map/ppermute | solution.py:455
  53.5 12.5 %collective-permute-start.4 = (bf16[160,1024]{1,0:T(8,128)(2,1)S(1)}, bf16[160,1024]{1,0:T(8,128)(2,1)S(1)}, u32[]{:S(2)}, u32[]{:S(2)}) collective-permute-start(bf16[160,1024]{1,0:T(8,128)(2,1)S(1)} %get-tuple-element.81), channel_id=1, source_target_pairs={{1,0},{2,1},{3,2},{5,4},{6,5},{7,6},{9,8},{10,9},{11,10},{13,12},{... | collective-permute-start | bytes 983048 | tf_op jit(solution)/shard_map/ppermute | solution.py:455
  60.7 12.5 %collective-permute-start.7 = (bf16[160,1024]{1,0:T(8,128)(2,1)S(1)}, bf16[160,1024]{1,0:T(8,128)(2,1)S(1)}, u32[]{:S(2)}, u32[]{:S(2)}) collective-permute-start(bf16[160,1024]{1,0:T(8,128)(2,1)S(1)} %get-tuple-element.87), channel_id=1, source_target_pairs={{1,0},{2,1},{3,2},{5,4},{6,5},{7,6},{9,8},{10,9},{11,10},{13,12},{... | collective-permute-start | bytes 983048 | tf_op jit(solution)/shard_map/ppermute | solution.py:455
  67.8 12.5 %collective-permute-start.6 = (bf16[160,1024]{1,0:T(8,128)(2,1)S(1)}, bf16[160,1024]{1,0:T(8,128)(2,1)S(1)}, u32[]{:S(2)}, u32[]{:S(2)}) collective-permute-start(bf16[160,1024]{1,0:T(8,128)(2,1)S(1)} %get-tuple-element.85), channel_id=1, source_target_pairs={{1,0},{2,1},{3,2},{5,4},{6,5},{7,6},{9,8},{10,9},{11,10},{13,12},{... | collective-permute-start | bytes 983048 | tf_op jit(solution)/shard_map/ppermute | solution.py:455
  75.0 12.5 %collective-permute-start.9 = (bf16[160,1024]{1,0:T(8,128)(2,1)S(1)}, bf16[160,1024]{1,0:T(8,128)(2,1)S(1)}, u32[]{:S(2)}, u32[]{:S(2)}) collective-permute-start(bf16[160,1024]{1,0:T(8,128)(2,1)S(1)} %get-tuple-element.91), channel_id=1, source_target_pairs={{1,0},{2,1},{3,2},{5,4},{6,5},{7,6},{9,8},{10,9},{11,10},{13,12},{... | collective-permute-start | bytes 983048 | tf_op jit(solution)/shard_map/ppermute | solution.py:455
  82.0 9.3 %collective-permute-start.8 = (bf16[160,1024]{1,0:T(8,128)(2,1)S(1)}, bf16[160,1024]{1,0:T(8,128)(2,1)S(1)}, u32[]{:S(2)}, u32[]{:S(2)}) collective-permute-start(bf16[160,1024]{1,0:T(8,128)(2,1)S(1)} %get-tuple-element.89), channel_id=1, source_target_pairs={{1,0},{2,1},{3,2},{5,4},{6,5},{7,6},{9,8},{10,9},{11,10},{13,12},{... | collective-permute-start | bytes 983048 | tf_op jit(solution)/shard_map/ppermute | solution.py:455
  97.0 2.8 %collective-permute-start.10 = (bf16[2176,256]{1,0:T(8,128)(2,1)S(1)}, bf16[2176,256]{1,0:T(8,128)(2,1)S(1)}, u32[]{:S(2)}, u32[]{:S(2)}) collective-permute-start(bf16[2176,256]{1,0:T(8,128)(2,1)S(1)} %get-tuple-element.125), channel_id=1, source_target_pairs={{0,4},{4,0},{8,12},{12,8},{16,20},{20,16},{24,28},{28,24},{32,36},... | collective-permute-start | bytes 3342344 | tf_op jit(solution)/shard_map/ppermute | solution.py:373
  100.0 8.4 %collective-permute-start.11 = (bf16[512,256]{1,0:T(8,128)(2,1)S(1)}, bf16[512,256]{1,0:T(8,128)(2,1)S(1)}, u32[]{:S(2)}, u32[]{:S(2)}) collective-permute-start(bf16[512,256]{1,0:T(8,128)(2,1)S(1)} %add_convert_fusion.1), channel_id=1, source_target_pairs={{0,64},{4,68},{8,72},{12,76},{16,80},{20,84},{24,88},{28,92},{32,9... | collective-permute-start | bytes 786440 | tf_op jit(solution)/shard_map/ppermute | solution.py:373
  100.9 10.1 %collective-permute-start.13 = (bf16[576,256]{1,0:T(8,128)(2,1)S(1)}, bf16[576,256]{1,0:T(8,128)(2,1)S(1)}, u32[]{:S(2)}, u32[]{:S(2)}) collective-permute-start(bf16[576,256]{1,0:T(8,128)(2,1)S(1)} %add_convert_fusion), channel_id=1, source_target_pairs={{0,192},{4,196},{8,200},{12,204},{16,208},{20,212},{24,216},{28,22... | collective-permute-start | bytes 884744 | tf_op jit(solution)/shard_map/ppermute | solution.py:373
  108.4 6.3 %collective-permute-start.12 = (bf16[256,256]{1,0:T(8,128)(2,1)S(1)}, bf16[256,256]{1,0:T(8,128)(2,1)S(1)}, u32[]{:S(2)}, u32[]{:S(2)}) collective-permute-start(bf16[256,256]{1,0:T(8,128)(2,1)S(1)} %add_convert_fusion.3), channel_id=1, source_target_pairs={{0,192},{4,196},{8,200},{12,204},{16,208},{20,212},{24,216},{28,22... | collective-permute-start | bytes 393224 | tf_op jit(solution)/shard_map/ppermute | solution.py:373
  111.1 5.2 %collective-permute-start.14 = (bf16[288,256]{1,0:T(8,128)(2,1)S(1)}, bf16[288,256]{1,0:T(8,128)(2,1)S(1)}, u32[]{:S(2)}, u32[]{:S(2)}) collective-permute-start(bf16[288,256]{1,0:T(8,128)(2,1)S(1)} %add_convert_fusion.2), channel_id=1, source_target_pairs={{0,64},{4,68},{8,72},{12,76},{16,80},{20,84},{24,88},{28,92},{32,9... | collective-permute-start | bytes 442376 | tf_op jit(solution)/shard_map/ppermute | solution.py:373
  116.5 5.1 %collective-permute-start.15 = (bf16[17,16,256]{2,1,0:T(8,128)(2,1)S(1)}, bf16[17,16,256]{2,1,0:T(8,128)(2,1)S(1)}, u32[]{:S(2)}, u32[]{:S(2)}) collective-permute-start(bf16[17,16,256]{2,1,0:T(8,128)(2,1)S(1)} %slice.153), channel_id=1, source_target_pairs={{0,8},{4,12},{8,0},{12,4},{16,24},{20,28},{24,16},{28,20},{32,40},... | collective-permute-start | bytes 417800 | tf_op jit(solution)/shard_map/ppermute | solution.py:373
  121.7 6.0 %collective-permute-start.16 = (bf16[17,8,256]{2,1,0:T(8,128)(2,1)S(1)}, bf16[17,8,256]{2,1,0:T(8,128)(2,1)S(1)}, u32[]{:S(2)}, u32[]{:S(2)}) collective-permute-start(bf16[17,8,256]{2,1,0:T(8,128)(2,1)S(1)} %slice.154), channel_id=1, source_target_pairs={{0,16},{4,20},{8,24},{12,28},{16,0},{20,4},{24,8},{28,12},{32,48},... | collective-permute-start | bytes 208904 | tf_op jit(solution)/shard_map/ppermute | solution.py:373
  127.7 8.7 %collective-permute-start.17 = (bf16[17,4,256]{2,1,0:T(4,128)(2,1)S(1)}, bf16[17,4,256]{2,1,0:T(4,128)(2,1)S(1)}, u32[]{:S(2)}, u32[]{:S(2)}) collective-permute-start(bf16[17,4,256]{2,1,0:T(4,128)(2,1)S(1)} %slice.155), channel_id=1, source_target_pairs={{0,32},{4,36},{8,40},{12,44},{16,48},{20,52},{24,56},{28,60},{32,0... | collective-permute-start | bytes 104456 | tf_op jit(solution)/shard_map/ppermute | solution.py:373

commit v2 on v1

--- a/solution.py
+++ b/solution.py
@@ -25,43 +25,83 @@
     return jnp.dot(left, right, preferred_element_type=F32)
 
 
+def dot_t(left, right):
+    return lax.dot_general(left, right, (((1,), (1,)), ((), ())), preferred_element_type=F32)
+
+
 def full(shape):
     return pl.BlockSpec(shape, lambda *_: (0,) * len(shape), pipeline_mode=pl.Buffered(1))
 
 
-def edges_kernel(x0_ref, x1_ref, og0_ref, og1_ref, cov0_ref, cov1_ref, first_ref, last_ref):
-    for x_ref, og_ref, cov_ref, out in (
-        (x0_ref, og0_ref, cov0_ref, first_ref),
-        (x1_ref, og1_ref, cov1_ref, last_ref),
+def edges_kernel(tissue, x0_ref, x1_ref, og0_ref, og1_ref, first_ref, last_ref):
+    rows, hgt = x0_ref.shape[:2]
+    for x_ref, og_ref, out, tile, at in (
+        (x0_ref, og0_ref, first_ref, 0, 0),
+        (x1_ref, og1_ref, last_ref, tissue.shape[1] - 1, EDGE - RIM),
     ):
-        out[0] = x_ref[...]
-        out[1] = (og_ref[...].astype(F32) * cov_ref[:, :, 0:1][:, None]).astype(BF16)
-
-
-def edges(x, og, cov):
+        out[:, :hgt] = x_ref[...]
+        for r in range(rows):
+            seed = og_ref[r].astype(F32)[:, at : at + RIM] * tissue[r, tile].astype(F32)
+            for pair in range(hgt // 2):
+                both = jnp.concatenate([seed[2 * pair], seed[2 * pair + 1]], axis=0)
+                out[r, hgt + pair] = both.astype(BF16)
+
+
+def edges(tissue, x, og):
     rows, hgt, width, ch = x.shape
     part = (rows, hgt, EDGE, ch)
+    out = (rows, hgt + hgt // 2, EDGE, ch)
     end = width // EDGE - 1
 
-    def at(shape, block):
-        index = (0,) * (len(shape) - 2) + (block, 0)
-        return pl.BlockSpec(shape, lambda i: index)
-
-    cov_part = (rows, EDGE, cov.shape[2])
+    def at(block):
+        return pl.BlockSpec(part, lambda i, tissue: (0, 0, block, 0))
+
     return pl.pallas_call(
         edges_kernel,
-        out_shape=[jax.ShapeDtypeStruct((2,) + part, BF16)] * 2,
-        grid=(1,),
-        in_specs=[at(part, 0), at(part, end), at(part, 0), at(part, end), at(cov_part, 0), at(cov_part, end)],
-        out_specs=[full((2,) + part)] * 2,
+        out_shape=[jax.ShapeDtypeStruct(out, BF16)] * 2,
+        grid_spec=pltpu.PrefetchScalarGridSpec(
+            num_scalar_prefetch=1,
+            grid=(1,),
+            in_specs=[at(0), at(end), at(0), at(end)],
+            out_specs=[full(out)] * 2,
+        ),
         compiler_params=params(60),
         name="edge_columns",
-    )(x, x, og, og, cov, cov)
+    )(tissue, x, x, og, og)
+
+
+def hidden_one(part, wr, inner_ref):
+    rows, hgt, cols, ch = part.shape
+    flat = part.astype(F32).reshape(-1, ch).astype(BF16)
+    pre = dot(flat, wr) * inner_ref[0:1] + inner_ref[1:2]
+    return jnp.maximum(pre, 0.0).astype(BF16).astype(F32).reshape(rows, hgt, cols, -1)
+
+
+def inside_kernel(x_ref, wr_ref, inner_ref, og_ref, wc_ref, we_ref, h1_ref, *kept):
+    h1_ref[...] = hidden_one(x_ref[...], wr_ref[...], inner_ref).astype(BF16)
+    for ref, out in zip((x_ref, og_ref, wr_ref, wc_ref, we_ref), kept):
+        out[...] = ref[...]
+
+
+def inside(x, wr, inner, og, wc, we):
+    args = (x, wr, inner, og, wc, we)
+    shapes = (x.shape[:3] + (wr.shape[1],),) + tuple(a.shape for a in (x, og, wr, wc, we))
+    return pl.pallas_call(
+        inside_kernel,
+        out_shape=[jax.ShapeDtypeStruct(s, BF16) for s in shapes],
+        grid=(1,),
+        in_specs=[full(a.shape) for a in args],
+        out_specs=[full(s) for s in shapes],
+        compiler_params=params(12),
+        cost_estimate=pl.CostEstimate(flops=300_000_000, bytes_accessed=9_000_000, transcendentals=0),
+        name="forward_own_columns",
+    )(*args)
 
 
 def forward_kernel(
-    ends, x_ref, lo_ref, hi_ref, og_ref, cov_ref, wr_ref, wc_ref, we_ref, inner_ref, outer_ref,
-    mz_ref, h2_ref, h1_ref, pad_ref, seed_ref, xs, hs, patches, ss,
+    ends, tissue, lo_ref, hi_ref, own_ref, inner_ref, outer_ref, x_ref, og_ref, wr_ref, wc_ref, we_ref,
+    mz_ref, h2_ref, h1_ref, pad_ref, seed_ref,
+    xs, hs, patches, ss,
 ):
     rows, hgt, width, ch = x_ref.shape
     inner_w = wr_ref.shape[1]
@@ -69,21 +109,11 @@
     per_row = hgt * wide
     hs[:, 0] = jnp.zeros((rows, width + 2 * EDGE, inner_w), F32)
     hs[:, hgt + 1] = jnp.zeros((rows, width + 2 * EDGE, inner_w), F32)
-    sides = (
-        (lo_ref.at[0], 0, ends[0]),
-        (x_ref, EDGE, None),
-        (hi_ref.at[0], EDGE + width, ends[1]),
-    )
-    for ref, at, keep in sides:
-        part = ref[...]
-        cols = part.shape[2]
-        xs[:, :, at : at + cols] = part.astype(F32)
-        pre = dot(part.astype(F32).reshape(-1, ch).astype(BF16), wr_ref[...])
-        pre = pre * inner_ref[0:1] + inner_ref[1:2]
-        hid = jnp.maximum(pre, 0.0).astype(BF16).astype(F32)
-        if keep is not None:
-            hid = hid * keep.astype(F32)
-        hs[:, 1 : hgt + 1, at : at + cols] = hid.reshape(rows, hgt, cols, inner_w)
+    hs[:, 1 : hgt + 1, EDGE : EDGE + width] = own_ref[...].astype(F32)
+    for ref, at, keep in ((lo_ref, 0, ends[0]), (hi_ref, EDGE + width, ends[1])):
+        part = ref[:, :hgt]
+        xs[:, :, at : at + EDGE] = part.astype(F32)
+        hs[:, 1 : hgt + 1, at : at + EDGE] = hidden_one(part, wr_ref[...], inner_ref) * keep.astype(F32)
     pad_ref[...] = hs[...].astype(BF16)
     first = EDGE - RIM - 1
     for k in range(9):
@@ -96,18 +126,25 @@
     pre = dot(patches[...], wc_ref[...]) * inner_ref[2:3] + inner_ref[3:4]
     hid = jnp.maximum(pre, 0.0).astype(BF16)
     h2_ref[...] = hid.reshape(rows, hgt * wide, inner_w)
+    xs[:, :, EDGE : EDGE + width] = x_ref[...].astype(F32)
     for r in range(rows):
         part = hid[r * per_row : (r + 1) * per_row]
         z = dot(part, we_ref[...]) * outer_ref[0:1] + outer_ref[1:2]
         z = z + xs[r, :, EDGE - RIM : EDGE - RIM + wide].reshape(per_row, ch)
         mz_ref[r] = jnp.where(z > 0, 1.0, 0.0).astype(BF16)
-        ss[:, 0:EDGE] = lo_ref[1, r].astype(F32)
-        ss[:, EDGE : EDGE + width] = og_ref[r].astype(F32) * cov_ref[r, :, 0:1][None]
-        ss[:, EDGE + width :] = hi_ref[1, r].astype(F32)
-        seed_ref[r] = ss[:, EDGE - RIM : EDGE - RIM + wide].reshape(per_row, ch).astype(BF16)
-
-
-def forward(ends, x, lo, hi, og, cov, wr, wc, we, inner, outer):
+        for ref, at in ((lo_ref, 0), (hi_ref, RIM + width)):
+            for pair in range(hgt // 2):
+                both = ref[r, hgt + pair].astype(F32)
+                ss[2 * pair, at : at + RIM] = both[:RIM]
+                ss[2 * pair + 1, at : at + RIM] = both[RIM:]
+        og = og_ref[r].astype(F32)
+        for tile in range(width // TILE_W):
+            cols = og[:, tile * TILE_W : (tile + 1) * TILE_W] * tissue[r, tile].astype(F32)
+            ss[:, RIM + tile * TILE_W : RIM + (tile + 1) * TILE_W] = cols
+        seed_ref[r] = ss[...].reshape(per_row, ch).astype(BF16)
+
+
+def forward(ends, tissue, lo, hi, own, inner, outer, x, og, wr, wc, we):
     rows, hgt, width, ch = x.shape
     inner_w = wr.shape[1]
     wide = width + 2 * RIM
@@ -119,35 +156,36 @@
         (rows, hgt + 2, width + 2 * EDGE, inner_w),
         (rows, pos, ch),
     )
-    args = (x, lo, hi, og, cov, wr, wc, we, inner, outer)
+    blocks = (lo, hi, own, inner, outer, x, og, wr, wc, we)
     return pl.pallas_call(
         forward_kernel,
         out_shape=[jax.ShapeDtypeStruct(s, BF16) for s in out_shapes],
         grid_spec=pltpu.PrefetchScalarGridSpec(
-            num_scalar_prefetch=1,
+            num_scalar_prefetch=2,
             grid=(1,),
-            in_specs=[full(a.shape) for a in args],
+            in_specs=[full(a.shape) for a in blocks],
             out_specs=[full(s) for s in out_shapes],
             scratch_shapes=[
                 pltpu.VMEM((rows, hgt, width + 2 * EDGE, ch), F32),
                 pltpu.VMEM((rows, hgt + 2, width + 2 * EDGE, inner_w), F32),
                 pltpu.VMEM((rows * pos, 9 * inner_w), BF16),
-                pltpu.VMEM((hgt, width + 2 * EDGE, ch), F32),
+                pltpu.VMEM((hgt, wide, ch), F32),
             ],
         ),
-        compiler_params=params(32),
+        compiler_params=params(20),
         cost_estimate=pl.CostEstimate(flops=2_000_000_000, bytes_accessed=12_000_000, transcendentals=0),
         name="forward_all_rows",
-    )(ends, *args)
+    )(ends, tissue, *blocks)
 
 
 def chain_kernel(
-    info, gy_ref, seed_ref, mz_ref, h2_ref, h1_ref, wet_ref, wct_ref, wrt_ref, inner_ref, outer_ref,
-    wire_ref, gi_ref, g3_ref, g2_ref, g1_ref, wide_s, pad_s,
+    info, gy_ref, seed_ref, mz_ref, h2_ref, h1_ref, we_ref, wc_ref, wr_ref, inner_ref, outer_ref,
+    gi_ref, g3_ref, g2_ref, g1_ref, *more,
 ):
-    pos, ch = gy_ref.shape
-    inner_w = wet_ref.shape[1]
-    hgt, wide = wide_s.shape[:2]
+    *wire_ref, wide_s, pad_s = more
+    inner_w = we_ref.shape[0]
+    hgt, wide, ch = wide_s.shape
+    pos = hgt * wide
     width = wide - 2 * RIM
     lead = 8
 
@@ -160,37 +198,37 @@
     gz = gy * mz_ref[0].astype(F32)
     g3 = (gz * outer_ref[0:1]).astype(BF16)
     g3_ref[...] = center(g3.astype(F32))
-    g2 = jnp.where(h2_ref[0].astype(F32) > 0, dot(g3, wet_ref[...]) * inner_ref[2:3], 0.0)
+    g2 = jnp.where(h2_ref[0].astype(F32) > 0, dot_t(g3, we_ref[...]) * inner_ref[2:3], 0.0)
     g2 = g2.astype(BF16).astype(F32)
     pad_s[...] = jnp.zeros_like(pad_s)
     pad_s[1 : hgt + 1, lead : lead + wide] = g2.reshape(hgt, wide, inner_w)
     g2_ref[...] = (
         pad_s[1 : hgt + 1, lead + RIM : lead + RIM + width].reshape(hgt * width, inner_w).astype(BF16)
     )
-    pieces = []
+    back = jnp.zeros((pos, inner_w), F32)
     for k in range(9):
         dr, dc = divmod(k, 3)
         piece = pad_s[2 - dr : 2 - dr + hgt, lead + 1 - dc : lead + 1 - dc + wide]
-        pieces.append(piece.reshape(pos, inner_w).astype(BF16))
-    back = dot(jnp.concatenate(pieces, axis=1), wct_ref[...])
+        back = back + dot_t(piece.reshape(pos, inner_w).astype(BF16), wc_ref[k * inner_w : (k + 1) * inner_w])
     g1 = jnp.where(h1_ref[0].astype(F32) > 0, back * inner_ref[0:1], 0.0).astype(BF16)
     g1_ref[...] = center(g1.astype(F32))
-    gi = gz + dot(g1, wrt_ref[...])
-    wire_ref[...] = gi.astype(BF16)
+    gi = gz + dot_t(g1, wr_ref[...])
+    if wire_ref:
+        wire_ref[0][...] = gi.astype(BF16)
     gi_ref[...] = center(gi)
 
 
-def chain_step(info, gy, seed, mz, h2, h1, wet, wct, wrt, inner, outer, hgt):
-    pos, ch = gy.shape
-    inner_w = wet.shape[1]
+def chain_step(info, gy, seed, mz, h2, h1, we, wc, wr, inner, outer, hgt, hand_on):
+    pos, ch = seed.shape[1:]
+    inner_w = we.shape[0]
     wide = pos // hgt
     kept = hgt * (wide - 2 * RIM)
 
     def row(lanes):
         return pl.BlockSpec((1, pos, lanes), lambda i, info: (info[0], 0, 0))
 
-    const = (wet, wct, wrt, inner, outer)
-    out_shapes = (gy.shape, (kept, ch), (kept, ch), (kept, inner_w), (kept, inner_w))
+    const = (we, wc, wr, inner, outer)
+    out_shapes = [(kept, ch), (kept, ch), (kept, inner_w), (kept, inner_w)] + [gy.shape] * hand_on
     return pl.pallas_call(
         chain_kernel,
         out_shape=[jax.ShapeDtypeStruct(s, BF16) for s in out_shapes],
@@ -205,7 +243,7 @@
                 pltpu.VMEM((hgt + 2, wide + 16, inner_w), F32),
             ],
         ),
-        compiler_params=params(24),
+        compiler_params=params(12),
         cost_estimate=pl.CostEstimate(flops=360_000_000, bytes_accessed=5_000_000, transcendentals=0),
         name="chain_row",
     )(info, gy, seed, mz, h2, h1, *const)
@@ -259,7 +297,7 @@
         grid=(1,),
         in_specs=[full(a.shape) for a in args],
         out_specs=[full(s) for s in shapes],
-        compiler_params=params(32),
+        compiler_params=params(20),
         cost_estimate=pl.CostEstimate(flops=2_000_000_000, bytes_accessed=8_000_000, transcendentals=0),
         name="turn_activations",
     )(*args)
@@ -353,7 +391,7 @@
                 pltpu.SemaphoreType.DMA((4, rows)),
             ],
         ),
-        compiler_params=params(32),
+        compiler_params=params(20),
         cost_estimate=pl.CostEstimate(flops=1_200_000_000, bytes_accessed=8_000_000, transcendentals=0),
         name="weight_gradients",
     )(info, *args, *g1, *g2, *g3, *gi)
@@ -393,14 +431,42 @@
     part_a = own(at_a + quart_a, cut) + got_a[quart_a:].astype(F32) + got_a2.astype(F32)
     part_b = own(at_b + quart_b, keep.shape[0]) + got_b[quart_b:].astype(F32) + got_b2.astype(F32)
     total = jnp.concatenate([part_a, part_b], axis=0).reshape(SEGS, Z * 4, lanes)
-    for bit in (1, 2, 4):
-        count = total.shape[1] // 2
-        got = swap(total[:, :count], lambda x, z, c, b=bit: (x, z ^ b, c))
-        total = total[:, count:] + got.astype(F32)
-    g_reduce = total[:4].reshape(16, lanes)
-    g_conv = total[4:13].reshape(3, 3, 4, lanes)
-    g_expand = total[13:].transpose(1, 0, 2).reshape(4, 4 * lanes)
-    return g_reduce, g_conv, g_expand
+    count = Z * 4 // 2
+    got = swap(total[:, :count], lambda x, z, c: (x, z ^ 1, c))
+    total = total[:, count:] + got.astype(F32)
+    shares = [
+        swap(total[:, 4 * i : 4 * i + 4], lambda x, z, c, b=Z_ORDER[Z // 2 + i]: (x, z ^ b, c))
+        for i in range(Z // 2 - 1)
+    ]
+    return finish(total[:, count - 4 :], shares)
+
+
+def finish_kernel(own_ref, *refs):
+    reduce_ref, conv_ref, expand_ref = refs[-3:]
+    total = own_ref[...]
+    for ref in refs[:-3]:
+        total = total + ref[...].astype(F32)
+    lanes = total.shape[2]
+    for q in range(4):
+        reduce_ref[4 * q : 4 * q + 4] = total[q]
+        expand_ref[:, q * lanes : (q + 1) * lanes] = total[13 + q]
+    conv_ref[...] = total[4:13]
+
+
+def finish(own, shares):
+    lanes = own.shape[2]
+    shapes = ((16, lanes), (9, 4, lanes), (4, 4 * lanes))
+    args = (own, *shares)
+    g_reduce, g_conv, g_expand = pl.pallas_call(
+        finish_kernel,
+        out_shape=[jax.ShapeDtypeStruct(s, F32) for s in shapes],
+        grid=(1,),
+        in_specs=[full(a.shape) for a in args],
+        out_specs=[full(s) for s in shapes],
+        compiler_params=params(4),
+        name="finish_gradients",
+    )(*args)
+    return g_reduce, g_conv.reshape(3, 3, 4, lanes), g_expand
 
 
 def neighbours(first, last, tiles):
@@ -421,38 +487,35 @@
     inner_w = wr.shape[1]
     wc = w_conv[0].reshape(9 * inner_w, inner_w)
     inner, outer = inner_affine[0], outer_affine[0]
-    pos = hgt * (width + 2 * RIM)
-
-    cover = jnp.repeat(tissue.astype(F32), TILE_W, axis=1)[:, :, None]
-    cover = jnp.broadcast_to(cover, (rows, width, 128))
-    lo, hi = neighbours(*edges(x, out_grad, cover), tiles)
-
-    wet = we.T
-    wrt = wr.T
-    wct = w_conv[0].transpose(0, 1, 3, 2).reshape(9 * inner_w, inner_w)
+
+    lo, hi = neighbours(*edges(tissue, x, out_grad), tiles)
+    own, *at_hand = inside(x, wr, inner, out_grad, wc, we)
 
     ends = jnp.stack([tile > 0, tile < tiles - 1]).astype(jnp.int32)
     mz, h2, h1, pad, seed = forward(
-        ends, x, lo, hi, out_grad, cover, wr, wc, we, inner, outer
+        ends, tissue, lo, hi, own, inner, outer, *at_hand
     )
     z_now = (tile // CORES) % Z
     xt, pt, ht = turn(x, pad, h2, picks(inner_w, z_now))
 
     back_one = [(i, i - 1) for i in range(1, sections)]
     slots = rows + LAG * (sections - 1)
-    arriving = [jnp.zeros((pos, ch), BF16)] * LAG
+    arriving = [jnp.zeros((hgt * (width + 2 * RIM), ch), BF16)] * LAG
     per_slot = []
     for slot in range(slots):
         micro = slot - LAG * (sections - 1 - section)
         info = jnp.stack(
             [jnp.clip(micro, 0, rows - 1), (section == sections - 1).astype(micro.dtype)]
         ).astype(jnp.int32)
-        wire, *saved = chain_step(
-            info, arriving[slot], seed, mz, h2, h1, wet, wct, wrt, inner, outer, hgt
+        hand_on = slot + LAG < slots
+        *saved, last = chain_step(
+            info, arriving[slot], seed, mz, h2, h1, at_hand[4], at_hand[3], at_hand[2], inner, outer, hgt, hand_on
         )
+        if hand_on:
+            arriving.append(lax.ppermute(last, "section", back_one))
+        else:
+            saved.append(last)
         per_slot.append(saved)
-        if slot + LAG < slots:
-            arriving.append(lax.ppermute(wire, "section", back_one))
     gi, g3, g2, g1 = zip(*per_slot)
     info = jnp.stack([tile % CORES, tile // (CORES * Z), section]).astype(jnp.int32)
     keep, send, grad_inputs = weight_grads(info, xt, pt, ht, g1, g2, g3, gi, rows)

time: 140 us -> 130 us (0.929)
  local copies, waits for them, and re-layouts: 10.7 us -> 2.2 us
  Pallas kernels: 30.1 us -> 34 us
  waiting for transfers between devices: 54.1 us -> 51.8 us
  starting transfers between devices: 40.1 us -> 38.2 us
    unnamed x20 -> x16, local copies, waits for them, and re-layouts: 7.18 us -> 2.1 us
    pallas_call x10, Pallas kernels: 18.2 us -> 20.5 us  [chain_step(): pl.pallas_call(chain_kernel, out_shape=[jax.ShapeDtypeStruct(s, BF16) for...]
    pallas_call x1 -> x3, Pallas kernels: 2.36 us -> 4.39 us  [the longest x1 3.1 us: edges(): pl.pallas_call(edges_kernel, out_shape=[jax.ShapeDtypeStruct(out, BF16)]...]
    ppermute x8 -> x9, starting transfers between devices: 11.7 us -> 9.78 us  [swap(): return lax.ppermute(value.astype(BF16), 'tile', tile_pairs(partner))]
    ppermute x8, waiting for transfers between devices: 24.1 us -> 22.6 us  [per_device(): arriving.append(lax.ppermute(last, 'section', back_one))]
    ppermute x8 -> x9, waiting for transfers between devices: 27.1 us -> 27.1 us  [swap(): return lax.ppermute(value.astype(BF16), 'tile', tile_pairs(partner))]
  transfers between devices with their start and end apart: 18 -> 19, of which waited for: 18 -> 19; matrix products, arithmetic and copies ran while one was open for 3% -> 1% of each run, Pallas kernels for 11% -> 14%
where the time goes in v2:
time: 130 us; the launch traced here: 129 us
  waiting for transfers between devices  51.8 us (40%)
  starting transfers between devices  38.2 us (29%)
  Pallas kernels  34 us (26%)
  local copies, waits for them, and re-layouts  2.2 us (2%)
  other arithmetic  1.53 us (1%)
    ppermute x9, waiting for transfers between devices, swap(): return lax.ppermute(value.astype(BF16), 'tile', tile_pairs(partner))  27.1 us
    ppermute x8, waiting for transfers between devices, per_device(): arriving.append(lax.ppermute(last, 'section', back_one))  22.6 us
    pallas_call x10, Pallas kernels, chain_step(): pl.pallas_call(chain_kernel, out_shape=[jax.ShapeDtypeStruct(s, BF16) for...  20.5 us
    ppermute x8, starting transfers between devices, per_device(): arriving.append(lax.ppermute(last, 'section', back_one))  19 us
    ppermute x9, starting transfers between devices, swap(): return lax.ppermute(value.astype(BF16), 'tile', tile_pairs(partner))  9.78 us
    ppermute x1, starting transfers between devices, neighbours(): high = lax.ppermute(first, 'tile', [(b, a) for a, b in pairs])  7.47 us
    pallas_call x1, Pallas kernels, forward(): pl.pallas_call(forward_kernel, out_shape=[jax.ShapeDtypeStruct(s, BF16) f...  4.51 us
    pallas_call x1, Pallas kernels, weight_grads(): pl.pallas_call(functools.partial(weights_kernel, slots), out_shape=[jax.S...  3.37 us
  transfers between devices with their start and end apart: 19, of which 19 were waited for; matrix products, arithmetic and copies ran while one was open for 1% of the time, Pallas kernels for 14%

profile of v2, /device:TPU:22, one launch (start us, length us, event | category | flops | bytes accessed | tf_op | source)
XLA Modules:
  0.0 128.7 jit_solution(17609262564637677939)
XLA Ops:
  0.7 3.1 %edge_columns.1 = (bf16[4,6,8,1024]{3,2,1,0:T(8,128)(2,1)}, bf16[4,6,8,1024]{3,2,1,0:T(8,128)(2,1)}) custom-call(s32[4,4]{1,0:T(4,128)} %tissue.3, bf16[4,4,32,1024]{3,2,1,0:T(8,128)(2,1)} %bitcast.29, bf16[4,4,32,1024]{3,2,1,0:T(8,128)(2,1)} %bitcast.30, bf16[4,4,32,1024]{3,2,1,0:T(8,128)(2,1)} %og_ref.1, bf16[4,4,32,1024]{3,2,1,0:T(8,128)(2,1)} %og_ref.1), custom_call_target="tpu_custom_call" | custom-call | tf_op jit(solution)/shard_map/edge_columns/pallas_call | solution.py:59
  5.7 7.5 %collective-permute-start.1 = (bf16[4,6,8,1024]{3,2,1,0:T(8,128)(2,1)}, bf16[4,6,8,1024]{3,2,1,0:T(8,128)(2,1)}, u32[]{:S(2)}, u32[]{:S(2)}) collective-permute-start(bf16[4,6,8,1024]{3,2,1,0:T(8,128)(2,1)} %get-tuple-element.75), channel_id=1, source_target_pairs={{4,0},{8,4},{12,8},{16,12},{20,16},{24,20},{28,24},{32,28},{36,32}... | collective-permute-start | bytes 1179656 | tf_op jit(solution)/shard_map/ppermute | solution.py:475
  18.8 4.5 %forward_all_rows.1 = (bf16[4,160,1024]{2,1,0:T(8,128)(2,1)S(1)}, bf16[4,160,256]{2,1,0:T(8,128)(2,1)S(1)}, bf16[4,160,256]{2,1,0:T(8,128)(2,1)S(1)}, bf16[4,6,4...) custom-call(s32[2]{0:T(128)S(1)} %add_convert_fusion.4.ends, s32[4,4]{1,0:T(4,128)S(1)} %copy-done.7, ...), custom_call_target="tpu_custom_call" | custom-call | flops 2000000000 | bytes 12000000 | tf_op jit(solution)/shard_map/forward_all_rows/pallas_call | solution.py:160
  23.3 2.1 %chain_row.11 = (bf16[128,1024]{1,0:T(8,128)(2,1)S(1)}, bf16[128,1024]{1,0:T(8,128)(2,1)S(1)}, bf16[128,256]{1,0:T(8,128)(2,1)S(1)}, bf16[128,256]{1,0:T(8,128)(2,1)S(1)}, bf16[160,1024]{1,0:T(8,128)(2,1)S(1)}) custom-call(s32[2]{0:T(128)S(1)} %get-tuple-element.152.info, bf16[160,1024]{1,0:T(8,128)(2,1)S(1)} %broadcast_in_dim.12.gy_ref, ...), custom_call_target="tpu_custom_call" | custom-call | flops 360000000 | bytes 5000000 | tf_op jit(solution)/shard_map/chain_row/pallas_call | solution.py:232
  25.4 2.4 %collective-permute-start.3 = (bf16[160,1024]{1,0:T(8,128)(2,1)S(1)}, bf16[160,1024]{1,0:T(8,128)(2,1)S(1)}, u32[]{:S(2)}, u32[]{:S(2)}) collective-permute-start(bf16[160,1024]{1,0:T(8,128)(2,1)S(1)} %get-tuple-element.94), channel_id=1, source_target_pairs={{1,0},{2,1},{3,2},{5,4},{6,5},{7,6},{9,8},{10,9},{11,10},{13,12},{... | collective-permute-start | bytes 983048 | tf_op jit(solution)/shard_map/ppermute | solution.py:515
  27.7 2.1 %chain_row.10 = (bf16[128,1024]{1,0:T(8,128)(2,1)S(1)}, bf16[128,1024]{1,0:T(8,128)(2,1)S(1)}, bf16[128,256]{1,0:T(8,128)(2,1)S(1)}, bf16[128,256]{1,0:T(8,128)(2,1)S(1)}, bf16[160,1024]{1,0:T(8,128)(2,1)S(1)}) custom-call(s32[2]{0:T(128)S(1)} %get-tuple-element.151.info, bf16[160,1024]{1,0:T(8,128)(2,1)S(1)} %broadcast_in_dim.12.gy_ref, ...), custom_call_target="tpu_custom_call" | custom-call | flops 360000000 | bytes 5000000 | tf_op jit(solution)/shard_map/chain_row/pallas_call | solution.py:232
  29.8 2.4 %collective-permute-start.2 = (bf16[160,1024]{1,0:T(8,128)(2,1)S(1)}, bf16[160,1024]{1,0:T(8,128)(2,1)S(1)}, u32[]{:S(2)}, u32[]{:S(2)}) collective-permute-start(bf16[160,1024]{1,0:T(8,128)(2,1)S(1)} %get-tuple-element.92), channel_id=1, source_target_pairs={{1,0},{2,1},{3,2},{5,4},{6,5},{7,6},{9,8},{10,9},{11,10},{13,12},{... | collective-permute-start | bytes 983048 | tf_op jit(solution)/shard_map/ppermute | solution.py:515
  32.3 5.7 %collective-permute-done.3.gy_ref = bf16[160,1024]{1,0:T(8,128)(2,1)S(1)} collective-permute-done((bf16[160,1024]{1,0:T(8,128)(2,1)S(1)}, bf16[160,1024]{1,0:T(8,128)(2,1)S(1)}, u32[]{:S(2)}, u32[]{:S(2)}) %collective-permute-start.3) | collective-permute-done | bytes 327712 | tf_op jit(solution)/shard_map/ppermute | solution.py:515
  37.9 2.1 %chain_row.13 = (bf16[128,1024]{1,0:T(8,128)(2,1)S(1)}, bf16[128,1024]{1,0:T(8,128)(2,1)S(1)}, bf16[128,256]{1,0:T(8,128)(2,1)S(1)}, bf16[128,256]{1,0:T(8,128)(2,1)S(1)}, bf16[160,1024]{1,0:T(8,128)(2,1)S(1)}) custom-call(s32[2]{0:T(128)S(1)} %pad_add_fusion.5.info, bf16[160,1024]{1,0:T(8,128)(2,1)S(1)} %collective-permute-done.3.gy_ref, ...), custom_call_target="tpu_custom_call" | custom-call | flops 360000000 | bytes 5000000 | tf_op jit(solution)/shard_map/chain_row/pallas_call | solution.py:232
  40.0 2.4 %collective-permute-start.5 = (bf16[160,1024]{1,0:T(8,128)(2,1)S(1)}, bf16[160,1024]{1,0:T(8,128)(2,1)S(1)}, u32[]{:S(2)}, u32[]{:S(2)}) collective-permute-start(bf16[160,1024]{1,0:T(8,128)(2,1)S(1)} %get-tuple-element.98), channel_id=1, source_target_pairs={{1,0},{2,1},{3,2},{5,4},{6,5},{7,6},{9,8},{10,9},{11,10},{13,12},{... | collective-permute-start | bytes 983048 | tf_op jit(solution)/shard_map/ppermute | solution.py:515
  42.3 2.6 %collective-permute-done.2.gy_ref = bf16[160,1024]{1,0:T(8,128)(2,1)S(1)} collective-permute-done((bf16[160,1024]{1,0:T(8,128)(2,1)S(1)}, bf16[160,1024]{1,0:T(8,128)(2,1)S(1)}, u32[]{:S(2)}, u32[]{:S(2)}) %collective-permute-start.2) | collective-permute-done | bytes 327712 | tf_op jit(solution)/shard_map/ppermute | solution.py:515
  44.9 2.1 %chain_row.12 = (bf16[128,1024]{1,0:T(8,128)(2,1)S(1)}, bf16[128,1024]{1,0:T(8,128)(2,1)S(1)}, bf16[128,256]{1,0:T(8,128)(2,1)S(1)}, bf16[128,256]{1,0:T(8,128)(2,1)S(1)}, bf16[160,1024]{1,0:T(8,128)(2,1)S(1)}) custom-call(s32[2]{0:T(128)S(1)} %pad_add_fusion.4.info, bf16[160,1024]{1,0:T(8,128)(2,1)S(1)} %collective-permute-done.2.gy_ref, ...), custom_call_target="tpu_custom_call" | custom-call | flops 360000000 | bytes 5000000 | tf_op jit(solution)/shard_map/chain_row/pallas_call | solution.py:232
  47.0 2.4 %collective-permute-start.4 = (bf16[160,1024]{1,0:T(8,128)(2,1)S(1)}, bf16[160,1024]{1,0:T(8,128)(2,1)S(1)}, u32[]{:S(2)}, u32[]{:S(2)}) collective-permute-start(bf16[160,1024]{1,0:T(8,128)(2,1)S(1)} %get-tuple-element.96), channel_id=1, source_target_pairs={{1,0},{2,1},{3,2},{5,4},{6,5},{7,6},{9,8},{10,9},{11,10},{13,12},{... | collective-permute-start | bytes 983048 | tf_op jit(solution)/shard_map/ppermute | solution.py:515
  49.4 2.9 %collective-permute-done.5.gy_ref = bf16[160,1024]{1,0:T(8,128)(2,1)S(1)} collective-permute-done((bf16[160,1024]{1,0:T(8,128)(2,1)S(1)}, bf16[160,1024]{1,0:T(8,128)(2,1)S(1)}, u32[]{:S(2)}, u32[]{:S(2)}) %collective-permute-start.5) | collective-permute-done | bytes 327712 | tf_op jit(solution)/shard_map/ppermute | solution.py:515
  54.4 2.4 %collective-permute-start.7 = (bf16[160,1024]{1,0:T(8,128)(2,1)S(1)}, bf16[160,1024]{1,0:T(8,128)(2,1)S(1)}, u32[]{:S(2)}, u32[]{:S(2)}) collective-permute-start(bf16[160,1024]{1,0:T(8,128)(2,1)S(1)} %get-tuple-element.102), channel_id=1, source_target_pairs={{1,0},{2,1},{3,2},{5,4},{6,5},{7,6},{9,8},{10,9},{11,10},{13,12},{... | collective-permute-start | bytes 983048 | tf_op jit(solution)/shard_map/ppermute | solution.py:515
  56.8 2.8 %collective-permute-done.4.gy_ref = bf16[160,1024]{1,0:T(8,128)(2,1)S(1)} collective-permute-done((bf16[160,1024]{1,0:T(8,128)(2,1)S(1)}, bf16[160,1024]{1,0:T(8,128)(2,1)S(1)}, u32[]{:S(2)}, u32[]{:S(2)}) %collective-permute-start.4) | collective-permute-done | bytes 327712 | tf_op jit(solution)/shard_map/ppermute | solution.py:515
  61.6 2.4 %collective-permute-start.6 = (bf16[160,1024]{1,0:T(8,128)(2,1)S(1)}, bf16[160,1024]{1,0:T(8,128)(2,1)S(1)}, u32[]{:S(2)}, u32[]{:S(2)}) collective-permute-start(bf16[160,1024]{1,0:T(8,128)(2,1)S(1)} %get-tuple-element.100), channel_id=1, source_target_pairs={{1,0},{2,1},{3,2},{5,4},{6,5},{7,6},{9,8},{10,9},{11,10},{13,12},{... | collective-permute-start | bytes 983048 | tf_op jit(solution)/shard_map/ppermute | solution.py:515
  64.2 2.8 %collective-permute-done.7.gy_ref = bf16[160,1024]{1,0:T(8,128)(2,1)S(1)} collective-permute-done((bf16[160,1024]{1,0:T(8,128)(2,1)S(1)}, bf16[160,1024]{1,0:T(8,128)(2,1)S(1)}, u32[]{:S(2)}, u32[]{:S(2)}) %collective-permute-start.7) | collective-permute-done | bytes 327712 | tf_op jit(solution)/shard_map/ppermute | solution.py:515
  69.0 2.5 %collective-permute-start.9 = (bf16[160,1024]{1,0:T(8,128)(2,1)S(1)}, bf16[160,1024]{1,0:T(8,128)(2,1)S(1)}, u32[]{:S(2)}, u32[]{:S(2)}) collective-permute-start(bf16[160,1024]{1,0:T(8,128)(2,1)S(1)} %get-tuple-element.106), channel_id=1, source_target_pairs={{1,0},{2,1},{3,2},{5,4},{6,5},{7,6},{9,8},{10,9},{11,10},{13,12},{... | collective-permute-start | bytes 983048 | tf_op jit(solution)/shard_map/ppermute | solution.py:515
  71.6 2.6 %collective-permute-done.6.gy_ref = bf16[160,1024]{1,0:T(8,128)(2,1)S(1)} collective-permute-done((bf16[160,1024]{1,0:T(8,128)(2,1)S(1)}, bf16[160,1024]{1,0:T(8,128)(2,1)S(1)}, u32[]{:S(2)}, u32[]{:S(2)}) %collective-permute-start.6) | collective-permute-done | bytes 327712 | tf_op jit(solution)/shard_map/ppermute | solution.py:515
  76.2 2.4 %collective-permute-start.8 = (bf16[160,1024]{1,0:T(8,128)(2,1)S(1)}, bf16[160,1024]{1,0:T(8,128)(2,1)S(1)}, u32[]{:S(2)}, u32[]{:S(2)}) collective-permute-start(bf16[160,1024]{1,0:T(8,128)(2,1)S(1)} %get-tuple-element.104), channel_id=1, source_target_pairs={{1,0},{2,1},{3,2},{5,4},{6,5},{7,6},{9,8},{10,9},{11,10},{13,12},{... | collective-permute-start | bytes 983048 | tf_op jit(solution)/shard_map/ppermute | solution.py:515
  80.9 2.1 %chain_row.19 = (bf16[128,1024]{1,0:T(8,128)(2,1)S(1)}, bf16[128,1024]{1,0:T(8,128)(2,1)S(1)}, bf16[128,256]{1,0:T(8,128)(2,1)S(1)}, bf16[128,256]{1,0:T(8,128)(2,1)S(1)}) custom-call(s32[2]{0:T(128)S(1)} %pad_add_fusion.11.info, bf16[160,1024]{1,0:T(8,128)(2,1)S(1)} %collective-permute-done.9.gy_ref, bf16[4,160,1024]{2,1,0:T(8,128)(2,1)S(1)} %get-tuple-element.87.seed_ref, ...), custom_call_target="tpu_custom_call" | custom-call | flops 360000000 | bytes 5000000 | tf_op jit(solution)/shard_map/chain_row/pallas_call | solution.py:232
  83.0 2.2 %collective-permute-done.8.gy_ref = bf16[160,1024]{1,0:T(8,128)(2,1)S(1)} collective-permute-done((bf16[160,1024]{1,0:T(8,128)(2,1)S(1)}, bf16[160,1024]{1,0:T(8,128)(2,1)S(1)}, u32[]{:S(2)}, u32[]{:S(2)}) %collective-permute-start.8) | collective-permute-done | bytes 327712 | tf_op jit(solution)/shard_map/ppermute | solution.py:515
  85.2 2.1 %chain_row.18 = (bf16[128,1024]{1,0:T(8,128)(2,1)S(1)}, bf16[128,1024]{1,0:T(8,128)(2,1)S(1)}, bf16[128,256]{1,0:T(8,128)(2,1)S(1)}, bf16[128,256]{1,0:T(8,128)(2,1)S(1)}) custom-call(s32[2]{0:T(128)S(1)} %pad_add_fusion.10.info, bf16[160,1024]{1,0:T(8,128)(2,1)S(1)} %collective-permute-done.8.gy_ref, bf16[4,160,1024]{2,1,0:T(8,128)(2,1)S(1)} %get-tuple-element.87.seed_ref, ...), custom_call_target="tpu_custom_call" | custom-call | flops 360000000 | bytes 5000000 | tf_op jit(solution)/shard_map/chain_row/pallas_call | solution.py:232
  87.2 3.4 %weight_gradients.1 = (bf16[2176,256]{1,0:T(8,128)(2,1)S(1)}, bf16[2176,256]{1,0:T(8,128)(2,1)S(1)}, bf16[4,128,1024]{2,1,0:T(8,128)(2,1)}) custom-call(s32[3]{0:T(128)S(1)} %pad_add_fusion.1.info, bf16[1024,512]{1,0:T(8,128)(2,1)S(1)} %get-tuple-element.84.xt_ref, bf16[2304,512]{1,0:T(8,128)(2,1)S(1)} %get-tuple-element.85.pt_ref, ...), custom_call_target="tpu_custom_call" | custom-call | flops 1200000000 | bytes 8000000 | tf_op jit(solution)/shard_map/weight_gradients/pallas_call | solution.py:379
  90.7 2.7 %collective-permute-done.10 = bf16[2176,256]{1,0:T(8,128)(2,1)S(1)} collective-permute-done((bf16[2176,256]{1,0:T(8,128)(2,1)S(1)}, bf16[2176,256]{1,0:T(8,128)(2,1)S(1)}, u32[]{:S(2)}, u32[]{:S(2)}) %collective-permute-start.10) | collective-permute-done | bytes 1114144 | tf_op jit(solution)/shard_map/ppermute | solution.py:411
  95.5 6.5 %collective-permute-done.11 = bf16[512,256]{1,0:T(8,128)(2,1)S(1)} collective-permute-done((bf16[512,256]{1,0:T(8,128)(2,1)S(1)}, bf16[512,256]{1,0:T(8,128)(2,1)S(1)}, u32[]{:S(2)}, u32[]{:S(2)}) %collective-permute-start.11) | collective-permute-done | bytes 262176 | tf_op jit(solution)/shard_map/ppermute | solution.py:411
  102.1 2.2 %collective-permute-done.13 = bf16[576,256]{1,0:T(8,128)(2,1)S(1)} collective-permute-done((bf16[576,256]{1,0:T(8,128)(2,1)S(1)}, bf16[576,256]{1,0:T(8,128)(2,1)S(1)}, u32[]{:S(2)}, u32[]{:S(2)}) %collective-permute-start.13) | collective-permute-done | bytes 294944 | tf_op jit(solution)/shard_map/ppermute | solution.py:411
  104.7 3.6 %collective-permute-done.12 = bf16[256,256]{1,0:T(8,128)(2,1)S(1)} collective-permute-done((bf16[256,256]{1,0:T(8,128)(2,1)S(1)}, bf16[256,256]{1,0:T(8,128)(2,1)S(1)}, u32[]{:S(2)}, u32[]{:S(2)}) %collective-permute-start.12) | collective-permute-done | bytes 131104 | tf_op jit(solution)/shard_map/ppermute | solution.py:411
  110.0 4.8 %collective-permute-done.15 = bf16[17,16,256]{2,1,0:T(8,128)(2,1)S(1)} collective-permute-done((bf16[17,16,256]{2,1,0:T(8,128)(2,1)S(1)}, bf16[17,16,256]{2,1,0:T(8,128)(2,1)S(1)}, u32[]{:S(2)}, u32[]{:S(2)}) %collective-permute-start.15) | collective-permute-done | bytes 139296 | tf_op jit(solution)/shard_map/ppermute | solution.py:411
  115.0 6.3 %collective-permute-start.18 = (bf16[17,4,256]{2,1,0:T(4,128)(2,1)S(1)}, bf16[17,4,256]{2,1,0:T(4,128)(2,1)S(1)}, u32[]{:S(2)}, u32[]{:S(2)}) collective-permute-start(bf16[17,4,256]{2,1,0:T(4,128)(2,1)S(1)} %get-tuple-element.146), channel_id=1, source_target_pairs={{0,32},{4,36},{8,40},{12,44},{16,48},{20,52},{24,56},{28,60},{32,0... | collective-permute-start | bytes 104456 | tf_op jit(solution)/shard_map/ppermute | solution.py:411
  123.3 3.1 %collective-permute-done.17.refs_1_ = bf16[17,4,256]{2,1,0:T(4,128)(2,1)S(1)} collective-permute-done((bf16[17,4,256]{2,1,0:T(4,128)(2,1)S(1)}, bf16[17,4,256]{2,1,0:T(4,128)(2,1)S(1)}, u32[]{:S(2)}, u32[]{:S(2)}) %collective-permute-start.17) | collective-permute-done | bytes 34848 | tf_op jit(solution)/shard_map/ppermute | solution.py:411
  (67 shorter events, 27.1 us)
Async XLA Ops:
  0.6 13.1 %copy-start = (bf16[4,4,32,1024]{3,2,1,0:T(8,128)(2,1)S(1)}, bf16[4,4,32,1024]{3,2,1,0:T(8,128)(2,1)}, u32[]{:S(2)}) copy-start(bf16[4,4,32,1024]{3,2,1,0:T(8,128)(2,1)} %og_ref.1) | copy-start | bytes 3145732
  0.6 13.1 %copy-start.1 = (bf16[1,4,4,32,1024]{4,3,2,1,0:T(8,128)(2,1)S(1)}, bf16[1,4,4,32,1024]{4,3,2,1,0:T(8,128)(2,1)}, u32[]{:S(2)}) copy-start(bf16[1,4,4,32,1024]{4,3,2,1,0:T(8,128)(2,1)} %param.9) | copy-start | bytes 3145732
  0.7 13.1 %copy-start.2 = (bf16[1,3,3,256,256]{4,3,2,1,0:T(8,128)(2,1)S(1)}, bf16[1,3,3,256,256]{4,3,2,1,0:T(8,128)(2,1)}, u32[]{:S(2)}) copy-start(bf16[1,3,3,256,256]{4,3,2,1,0:T(8,128)(2,1)} %param.13) | copy-start | bytes 3538948
  0.7 13.1 %copy-start.6 = (f32[1,4,256]{2,1,0:T(4,128)S(1)}, f32[1,4,256]{2,1,0:T(4,128)}, u32[]{:S(2)}) copy-start(f32[1,4,256]{2,1,0:T(4,128)} %param.15) | copy-start | bytes 12292
  3.8 13.2 %collective-permute-start = (bf16[4,6,8,1024]{3,2,1,0:T(8,128)(2,1)}, bf16[4,6,8,1024]{3,2,1,0:T(8,128)(2,1)}, u32[]{:S(2)}, u32[]{:S(2)}) collective-permute-start(bf16[4,6,8,1024]{3,2,1,0:T(8,128)(2,1)} %get-tuple-element.74), channel_id=1, source_target_pairs={{0,4},{4,8},{8,12},{12,16},{16,20},{20,24},{24,28},{28,32},{32,36}... | collective-permute-start | bytes 1179656 | tf_op jit(solution)/shard_map/ppermute | solution.py:474
  5.7 13.1 %collective-permute-start.1 = (bf16[4,6,8,1024]{3,2,1,0:T(8,128)(2,1)}, bf16[4,6,8,1024]{3,2,1,0:T(8,128)(2,1)}, u32[]{:S(2)}, u32[]{:S(2)}) collective-permute-start(bf16[4,6,8,1024]{3,2,1,0:T(8,128)(2,1)} %get-tuple-element.75), channel_id=1, source_target_pairs={{4,0},{8,4},{12,8},{16,12},{20,16},{24,20},{28,24},{32,28},{36,32}... | collective-permute-start | bytes 1179656 | tf_op jit(solution)/shard_map/ppermute | solution.py:475
  13.7 1.0 copy-start.4
  14.8 1.0 copy-start.5
  15.8 2.9 %copy-start.3 = (f32[1,2,1024]{2,1,0:T(2,128)S(1)}, f32[1,2,1024]{2,1,0:T(2,128)}, u32[]{:S(2)}) copy-start(f32[1,2,1024]{2,1,0:T(2,128)} %param.16) | copy-start | bytes 24580
  15.8 2.9 %copy-start.7 = (s32[4,4]{1,0:T(4,128)S(1)}, s32[4,4]{1,0:T(4,128)}, u32[]{:S(2)}) copy-start(s32[4,4]{1,0:T(4,128)} %tissue.3) | copy-start | bytes 196
  25.4 12.5 %collective-permute-start.3 = (bf16[160,1024]{1,0:T(8,128)(2,1)S(1)}, bf16[160,1024]{1,0:T(8,128)(2,1)S(1)}, u32[]{:S(2)}, u32[]{:S(2)}) collective-permute-start(bf16[160,1024]{1,0:T(8,128)(2,1)S(1)} %get-tuple-element.94), channel_id=1, source_target_pairs={{1,0},{2,1},{3,2},{5,4},{6,5},{7,6},{9,8},{10,9},{11,10},{13,12},{... | collective-permute-start | bytes 983048 | tf_op jit(solution)/shard_map/ppermute | solution.py:515
  29.8 15.1 %collective-permute-start.2 = (bf16[160,1024]{1,0:T(8,128)(2,1)S(1)}, bf16[160,1024]{1,0:T(8,128)(2,1)S(1)}, u32[]{:S(2)}, u32[]{:S(2)}) collective-permute-start(bf16[160,1024]{1,0:T(8,128)(2,1)S(1)} %get-tuple-element.92), channel_id=1, source_target_pairs={{1,0},{2,1},{3,2},{5,4},{6,5},{7,6},{9,8},{10,9},{11,10},{13,12},{... | collective-permute-start | bytes 983048 | tf_op jit(solution)/shard_map/ppermute | solution.py:515
  40.0 12.4 %collective-permute-start.5 = (bf16[160,1024]{1,0:T(8,128)(2,1)S(1)}, bf16[160,1024]{1,0:T(8,128)(2,1)S(1)}, u32[]{:S(2)}, u32[]{:S(2)}) collective-permute-start(bf16[160,1024]{1,0:T(8,128)(2,1)S(1)} %get-tuple-element.98), channel_id=1, source_target_pairs={{1,0},{2,1},{3,2},{5,4},{6,5},{7,6},{9,8},{10,9},{11,10},{13,12},{... | collective-permute-start | bytes 983048 | tf_op jit(solution)/shard_map/ppermute | solution.py:515
  47.0 12.5 %collective-permute-start.4 = (bf16[160,1024]{1,0:T(8,128)(2,1)S(1)}, bf16[160,1024]{1,0:T(8,128)(2,1)S(1)}, u32[]{:S(2)}, u32[]{:S(2)}) collective-permute-start(bf16[160,1024]{1,0:T(8,128)(2,1)S(1)} %get-tuple-element.96), channel_id=1, source_target_pairs={{1,0},{2,1},{3,2},{5,4},{6,5},{7,6},{9,8},{10,9},{11,10},{13,12},{... | collective-permute-start | bytes 983048 | tf_op jit(solution)/shard_map/ppermute | solution.py:515
  54.4 12.5 %collective-permute-start.7 = (bf16[160,1024]{1,0:T(8,128)(2,1)S(1)}, bf16[160,1024]{1,0:T(8,128)(2,1)S(1)}, u32[]{:S(2)}, u32[]{:S(2)}) collective-permute-start(bf16[160,1024]{1,0:T(8,128)(2,1)S(1)} %get-tuple-element.102), channel_id=1, source_target_pairs={{1,0},{2,1},{3,2},{5,4},{6,5},{7,6},{9,8},{10,9},{11,10},{13,12},{... | collective-permute-start | bytes 983048 | tf_op jit(solution)/shard_map/ppermute | solution.py:515
  61.6 12.5 %collective-permute-start.6 = (bf16[160,1024]{1,0:T(8,128)(2,1)S(1)}, bf16[160,1024]{1,0:T(8,128)(2,1)S(1)}, u32[]{:S(2)}, u32[]{:S(2)}) collective-permute-start(bf16[160,1024]{1,0:T(8,128)(2,1)S(1)} %get-tuple-element.100), channel_id=1, source_target_pairs={{1,0},{2,1},{3,2},{5,4},{6,5},{7,6},{9,8},{10,9},{11,10},{13,12},{... | collective-permute-start | bytes 983048 | tf_op jit(solution)/shard_map/ppermute | solution.py:515
  69.0 11.9 %collective-permute-start.9 = (bf16[160,1024]{1,0:T(8,128)(2,1)S(1)}, bf16[160,1024]{1,0:T(8,128)(2,1)S(1)}, u32[]{:S(2)}, u32[]{:S(2)}) collective-permute-start(bf16[160,1024]{1,0:T(8,128)(2,1)S(1)} %get-tuple-element.106), channel_id=1, source_target_pairs={{1,0},{2,1},{3,2},{5,4},{6,5},{7,6},{9,8},{10,9},{11,10},{13,12},{... | collective-permute-start | bytes 983048 | tf_op jit(solution)/shard_map/ppermute | solution.py:515
  76.2 9.0 %collective-permute-start.8 = (bf16[160,1024]{1,0:T(8,128)(2,1)S(1)}, bf16[160,1024]{1,0:T(8,128)(2,1)S(1)}, u32[]{:S(2)}, u32[]{:S(2)}) collective-permute-start(bf16[160,1024]{1,0:T(8,128)(2,1)S(1)} %get-tuple-element.104), channel_id=1, source_target_pairs={{1,0},{2,1},{3,2},{5,4},{6,5},{7,6},{9,8},{10,9},{11,10},{13,12},{... | collective-permute-start | bytes 983048 | tf_op jit(solution)/shard_map/ppermute | solution.py:515
  90.6 2.8 %collective-permute-start.10 = (bf16[2176,256]{1,0:T(8,128)(2,1)S(1)}, bf16[2176,256]{1,0:T(8,128)(2,1)S(1)}, u32[]{:S(2)}, u32[]{:S(2)}) collective-permute-start(bf16[2176,256]{1,0:T(8,128)(2,1)S(1)} %get-tuple-element.140), channel_id=1, source_target_pairs={{0,4},{4,0},{8,12},{12,8},{16,20},{20,16},{24,28},{28,24},{32,36},... | collective-permute-start | bytes 3342344 | tf_op jit(solution)/shard_map/ppermute | solution.py:411
  93.5 8.4 %collective-permute-start.11 = (bf16[512,256]{1,0:T(8,128)(2,1)S(1)}, bf16[512,256]{1,0:T(8,128)(2,1)S(1)}, u32[]{:S(2)}, u32[]{:S(2)}) collective-permute-start(bf16[512,256]{1,0:T(8,128)(2,1)S(1)} %add_convert_fusion.1), channel_id=1, source_target_pairs={{0,64},{4,68},{8,72},{12,76},{16,80},{20,84},{24,88},{28,92},{32,9... | collective-permute-start | bytes 786440 | tf_op jit(solution)/shard_map/ppermute | solution.py:411
  94.2 10.1 %collective-permute-start.13 = (bf16[576,256]{1,0:T(8,128)(2,1)S(1)}, bf16[576,256]{1,0:T(8,128)(2,1)S(1)}, u32[]{:S(2)}, u32[]{:S(2)}) collective-permute-start(bf16[576,256]{1,0:T(8,128)(2,1)S(1)} %add_convert_fusion), channel_id=1, source_target_pairs={{0,192},{4,196},{8,200},{12,204},{16,208},{20,212},{24,216},{28,22... | collective-permute-start | bytes 884744 | tf_op jit(solution)/shard_map/ppermute | solution.py:411
  102.0 6.3 %collective-permute-start.12 = (bf16[256,256]{1,0:T(8,128)(2,1)S(1)}, bf16[256,256]{1,0:T(8,128)(2,1)S(1)}, u32[]{:S(2)}, u32[]{:S(2)}) collective-permute-start(bf16[256,256]{1,0:T(8,128)(2,1)S(1)} %add_convert_fusion.3), channel_id=1, source_target_pairs={{0,192},{4,196},{8,200},{12,204},{16,208},{20,212},{24,216},{28,22... | collective-permute-start | bytes 393224 | tf_op jit(solution)/shard_map/ppermute | solution.py:411
  104.3 5.2 %collective-permute-start.14 = (bf16[288,256]{1,0:T(8,128)(2,1)S(1)}, bf16[288,256]{1,0:T(8,128)(2,1)S(1)}, u32[]{:S(2)}, u32[]{:S(2)}) collective-permute-start(bf16[288,256]{1,0:T(8,128)(2,1)S(1)} %add_convert_fusion.2), channel_id=1, source_target_pairs={{0,64},{4,68},{8,72},{12,76},{16,80},{20,84},{24,88},{28,92},{32,9... | collective-permute-start | bytes 442376 | tf_op jit(solution)/shard_map/ppermute | solution.py:411
  109.7 5.1 %collective-permute-start.15 = (bf16[17,16,256]{2,1,0:T(8,128)(2,1)S(1)}, bf16[17,16,256]{2,1,0:T(8,128)(2,1)S(1)}, u32[]{:S(2)}, u32[]{:S(2)}) collective-permute-start(bf16[17,16,256]{2,1,0:T(8,128)(2,1)S(1)} %slice.135), channel_id=1, source_target_pairs={{0,8},{4,12},{8,0},{12,4},{16,24},{20,28},{24,16},{28,20},{32,40},... | collective-permute-start | bytes 417800 | tf_op jit(solution)/shard_map/ppermute | solution.py:411
  115.0 8.4 %collective-permute-start.18 = (bf16[17,4,256]{2,1,0:T(4,128)(2,1)S(1)}, bf16[17,4,256]{2,1,0:T(4,128)(2,1)S(1)}, u32[]{:S(2)}, u32[]{:S(2)}) collective-permute-start(bf16[17,4,256]{2,1,0:T(4,128)(2,1)S(1)} %get-tuple-element.146), channel_id=1, source_target_pairs={{0,32},{4,36},{8,40},{12,44},{16,48},{20,52},{24,56},{28,60},{32,0... | collective-permute-start | bytes 104456 | tf_op jit(solution)/shard_map/ppermute | solution.py:411
  121.2 5.2 %collective-permute-start.17 = (bf16[17,4,256]{2,1,0:T(4,128)(2,1)S(1)}, bf16[17,4,256]{2,1,0:T(4,128)(2,1)S(1)}, u32[]{:S(2)}, u32[]{:S(2)}) collective-permute-start(bf16[17,4,256]{2,1,0:T(4,128)(2,1)S(1)} %get-tuple-element.147), channel_id=1, source_target_pairs={{0,16},{4,20},{8,24},{12,28},{16,0},{20,4},{24,8},{28,12},{32,48},... | collective-permute-start | bytes 104456 | tf_op jit(solution)/shard_map/ppermute | solution.py:411
  122.0 6.1 %collective-permute-start.16 = (bf16[17,4,256]{2,1,0:T(4,128)(2,1)S(1)}, bf16[17,4,256]{2,1,0:T(4,128)(2,1)S(1)}, u32[]{:S(2)}, u32[]{:S(2)}) collective-permute-start(bf16[17,4,256]{2,1,0:T(4,128)(2,1)S(1)} %get-tuple-element.148), channel_id=1, source_target_pairs={{0,48},{4,52},{8,56},{12,60},{16,32},{20,36},{24,40},{28,44},{32,1... | collective-permute-start | bytes 104456 | tf_op jit(solution)/shard_map/ppermute | solution.py:411

commit v3 on v2

--- a/solution.py
+++ b/solution.py
@@ -8,6 +8,7 @@
 from jax.sharding import PartitionSpec as P
 
 TILE_W = 8
+SECTIONS = 4
 X, Z, CORES = 4, 8, 2
 EDGE = 8
 RIM = 4
@@ -182,7 +183,7 @@
     info, gy_ref, seed_ref, mz_ref, h2_ref, h1_ref, we_ref, wc_ref, wr_ref, inner_ref, outer_ref,
     gi_ref, g3_ref, g2_ref, g1_ref, *more,
 ):
-    *wire_ref, wide_s, pad_s = more
+    *wire_ref, wide_s, pad_s, flat_s = more
     inner_w = we_ref.shape[0]
     hgt, wide, ch = wide_s.shape
     pos = hgt * wide
@@ -194,7 +195,13 @@
         wide_s[:, :, :lanes] = value.reshape(hgt, wide, lanes)
         return wide_s[:, RIM : RIM + width, :lanes].reshape(hgt * width, lanes).astype(BF16)
 
-    gy = jnp.where(info[1] == 1, seed_ref[0], gy_ref[...]).astype(F32)
+    cols = gy_ref.shape[0] // hgt
+    at = (wide - cols) // 2
+    flat_s[: hgt * cols] = gy_ref[...].astype(F32)
+    wide_s[...] = jnp.zeros_like(wide_s)
+    for h in range(hgt):
+        wide_s[h, at : at + cols] = flat_s[h * cols : (h + 1) * cols]
+    gy = jnp.where(info[1] == 1, seed_ref[0].astype(F32), wide_s[...].reshape(pos, ch))
     gz = gy * mz_ref[0].astype(F32)
     g3 = (gz * outer_ref[0:1]).astype(BF16)
     g3_ref[...] = center(g3.astype(F32))
@@ -213,12 +220,16 @@
     g1 = jnp.where(h1_ref[0].astype(F32) > 0, back * inner_ref[0:1], 0.0).astype(BF16)
     g1_ref[...] = center(g1.astype(F32))
     gi = gz + dot_t(g1, wr_ref[...])
+    gi_ref[...] = center(gi)
     if wire_ref:
-        wire_ref[0][...] = gi.astype(BF16)
-    gi_ref[...] = center(gi)
-
-
-def chain_step(info, gy, seed, mz, h2, h1, we, wc, wr, inner, outer, hgt, hand_on):
+        cols = wire_ref[0].shape[0] // hgt
+        at = (wide - cols) // 2
+        for h in range(hgt):
+            flat_s[h * cols : (h + 1) * cols] = wide_s[h, at : at + cols]
+        wire_ref[0][...] = flat_s[: hgt * cols].astype(BF16)
+
+
+def chain_step(info, gy, seed, mz, h2, h1, we, wc, wr, inner, outer, hgt, hand_on, sent):
     pos, ch = seed.shape[1:]
     inner_w = we.shape[0]
     wide = pos // hgt
@@ -228,7 +239,7 @@
         return pl.BlockSpec((1, pos, lanes), lambda i, info: (info[0], 0, 0))
 
     const = (we, wc, wr, inner, outer)
-    out_shapes = [(kept, ch), (kept, ch), (kept, inner_w), (kept, inner_w)] + [gy.shape] * hand_on
+    out_shapes = [(kept, ch), (kept, ch), (kept, inner_w), (kept, inner_w)] + [(hgt * sent, ch)] * hand_on
     return pl.pallas_call(
         chain_kernel,
         out_shape=[jax.ShapeDtypeStruct(s, BF16) for s in out_shapes],
@@ -241,10 +252,11 @@
             scratch_shapes=[
                 pltpu.VMEM((hgt, wide, ch), F32),
                 pltpu.VMEM((hgt + 2, wide + 16, inner_w), F32),
+                pltpu.VMEM((pos, ch), F32),
             ],
         ),
         compiler_params=params(12),
-        cost_estimate=pl.CostEstimate(flops=360_000_000, bytes_accessed=5_000_000, transcendentals=0),
+        cost_estimate=pl.CostEstimate(flops=3_600_000_000, bytes_accessed=50_000_000, transcendentals=0),
         name="chain_row",
     )(info, gy, seed, mz, h2, h1, *const)
 
@@ -313,88 +325,135 @@
     keep = as_int(x // 2 == target // 2)
     same = as_int(x % 2 == target % 2)
     last = jnp.where(keep == 1, same, 1 - same)
-    return X * A_SEGS * 32 + ((keep * 2 + last) * (SEGS - A_SEGS) + segment - A_SEGS) * 32
-
-
-def weights_kernel(slots, info, xt_ref, pt_ref, ht_ref, *refs):
-    by_slot = [refs[i * slots : (i + 1) * slots] for i in range(4)]
-    keep_ref, send_ref, gi_ref, g3_s, g2_s, g1_s, sems = refs[4 * slots :]
+    return ((keep * 2 + last) * (SEGS - A_SEGS) + segment - A_SEGS) * 32
+
+
+def products(part, side, x, left, right, cols, out_ref, so_far):
+    first_ref, pt_ref = left
+    inner_w = pt_ref.shape[0] // 9
+    half = inner_w // CORES
+    first = first_ref.shape[0] // CORES
+    ks = range(A_SEGS - 4) if part == 0 else range(A_SEGS - 4, 9)
+
+    def put(target, segment, value):
+        rows = pl.ds(pl.multiple_of(place(segment, target, x), 32), value.shape[0])
+        if so_far is not None:
+            value = value + so_far[rows].astype(F32)
+        out_ref[rows] = value.astype(BF16)
+
+    total = dot(first_ref[pl.ds(pl.multiple_of(side * first, first), first), cols], right[0])
+    if part == 0:
+        for target in range(X):
+            put(target, 0, total[target * half : (target + 1) * half])
+    else:
+        for j in range(4):
+            for target in range(X):
+                put(target, 13 + j, total[target * 32 : target * 32 + 32, j * inner_w : (j + 1) * inner_w])
+    at = pl.multiple_of(side * 9 * half + ks[0] * half, half)
+    total = dot(pt_ref[pl.ds(at, len(ks) * half), cols], right[1])
+    for n, k in enumerate(ks):
+        for target in range(X):
+            put(target, 4 + k, total[n * half + target * 32 : n * half + target * 32 + 32])
+
+
+def weights_kernel(parts, rows, by_row, added, info, *refs):
+    count = len(parts)
+    lefts, refs = refs[: 2 * count], refs[2 * count :]
+    so_far, refs = (refs[: 2 * count], refs[2 * count :]) if added else ((None,) * (2 * count), refs)
+    kinds = 2 if count == 1 else 3
+    slots = []
+    for _ in range(kinds):
+        slots.append(refs[: len(by_row)])
+        refs = refs[len(by_row) :]
+    outs, stores, sems = refs[: 2 * count], refs[2 * count : 2 * count + kinds], refs[-1]
     core, x, section = info[0], info[1], info[2]
-    rows, kept, ch = gi_ref.shape
-    inner_w = ht_ref.shape[0]
-    half = inner_w // CORES
-    into = (g1_s, g2_s, g3_s, gi_ref)
-
-    def copy(which, r, slot):
-        return pltpu.make_async_copy(by_slot[which][slot], into[which].at[r], sems.at[which, r])
-
-    sections = (slots - rows) // LAG + 1
-    for s in range(sections):
+
+    def copy(kind, n, slot):
+        return pltpu.make_async_copy(slots[kind][by_row.index(slot)], stores[kind].at[n], sems.at[kind, n])
+
+    for s, used in enumerate(slots_of(rows)):
         @pl.when(section == s)
         def _():
-            for which in range(4):
-                for r in range(rows):
-                    copy(which, r, LAG * (sections - 1 - s) + r).start()
-
-    def arrived(which):
-        for r in range(rows):
-            copy(which, r, r).wait()
-        if which < 3:
-            return into[which][...].reshape(rows * kept, into[which].shape[2])
-
-    outs = ((keep_ref, core), (send_ref, 1 - core))
-
-    def put(ref, target, segment, value):
-        at = pl.multiple_of(place(segment, target, x), 32)
-        ref[pl.ds(at, value.shape[0])] = value.astype(BF16)
-
-    g1 = arrived(0)
-    for ref, side in outs:
-        total = dot(xt_ref[pl.ds(pl.multiple_of(side * (ch // CORES), half), ch // CORES)], g1)
-        for target in range(X):
-            put(ref, target, 0, total[target * half : (target + 1) * half])
-    g2 = arrived(1)
-    for ref, side in outs:
-        total = dot(pt_ref[pl.ds(pl.multiple_of(side * 9 * half, half), 9 * half)], g2)
-        for k in range(9):
-            for target in range(X):
-                at = k * half + target * 32
-                put(ref, target, 4 + k, total[at : at + 32])
-    g3 = arrived(2)
-    for ref, side in outs:
-        total = dot(ht_ref[pl.ds(pl.multiple_of(side * half, half), half)], g3)
-        for j in range(4):
-            for target in range(X):
-                part = total[target * 32 : target * 32 + 32, j * inner_w : (j + 1) * inner_w]
-                put(ref, target, 13 + j, part)
-    arrived(3)
-
-
-def weight_grads(info, xt, pt, ht, g1, g2, g3, gi, rows):
-    inner_w = ht.shape[0]
-    slots = len(gi)
-    kept, ch = gi[0].shape
-    shape = (SEGS * X * 32, inner_w)
-    args = (xt, pt, ht)
+            for kind in range(kinds):
+                for n, slot in enumerate(used):
+                    copy(kind, n, slot).start()
+
+    held = []
+    for kind in range(kinds):
+        for n in range(len(rows)):
+            copy(kind, n, by_row[0]).wait()
+        kept, lanes = stores[kind].shape[1:]
+        held.append(stores[kind][...].reshape(len(rows) * kept, lanes))
+    cols = slice(rows[0] * kept, (rows[-1] + 1) * kept)
+    for i, part in enumerate(parts):
+        right = (held[0], held[1]) if count == 1 or part == 0 else (held[2], held[1])
+        for n, side in enumerate((core, 1 - core)):
+            products(part, side, x, lefts[2 * i : 2 * i + 2], right, cols, outs[2 * i + n], so_far[2 * i + n])
+
+
+def slots_of(rows):
+    return [[LAG * (SECTIONS - 1 - s) + r for r in rows] for s in range(SECTIONS)]
+
+
+def weight_grads(info, parts, rows, lefts, saved, so_far, name):
+    by_row = sorted({slot for used in slots_of(rows) for slot in used})
+    kept = saved[0][0].shape[0]
+    inner_w = lefts[1].shape[0] // 9
+    sizes = [(A_SEGS if part == 0 else SEGS - A_SEGS) * X * 32 for part in parts]
+    out_shapes = [(size, inner_w) for size in sizes for _ in range(2)]
+    blocks = tuple(lefts) + tuple(so_far)
     return pl.pallas_call(
-        functools.partial(weights_kernel, slots),
-        out_shape=[jax.ShapeDtypeStruct(s, BF16) for s in (shape, shape, (rows, kept, ch))],
+        functools.partial(weights_kernel, parts, rows, by_row, len(so_far) > 0),
+        out_shape=[jax.ShapeDtypeStruct(s, BF16) for s in out_shapes],
         grid_spec=pltpu.PrefetchScalarGridSpec(
             num_scalar_prefetch=1,
             grid=(1,),
-            in_specs=[full(a.shape) for a in args] + [pl.BlockSpec(memory_space=pl.ANY)] * (4 * slots),
-            out_specs=[full(shape), full(shape), pl.BlockSpec(memory_space=pl.ANY)],
-            scratch_shapes=[
-                pltpu.VMEM((rows, kept, ch), BF16),
-                pltpu.VMEM((rows, kept, inner_w), BF16),
-                pltpu.VMEM((rows, kept, inner_w), BF16),
-                pltpu.SemaphoreType.DMA((4, rows)),
-            ],
+            in_specs=[full(a.shape) for a in blocks]
+            + [pl.BlockSpec(memory_space=pl.ANY)] * (len(by_row) * len(saved)),
+            out_specs=[full(s) for s in out_shapes],
+            scratch_shapes=[pltpu.VMEM((len(rows), kept, kind[0].shape[1]), BF16) for kind in saved]
+            + [pltpu.SemaphoreType.DMA((len(saved), len(rows)))],
         ),
         compiler_params=params(20),
-        cost_estimate=pl.CostEstimate(flops=1_200_000_000, bytes_accessed=8_000_000, transcendentals=0),
-        name="weight_gradients",
-    )(info, *args, *g1, *g2, *g3, *gi)
+        cost_estimate=pl.CostEstimate(
+            flops=300_000_000 * len(rows), bytes_accessed=2_000_000 * len(rows), transcendentals=0
+        ),
+        name=name,
+    )(info, *blocks, *[kind[slot] for kind in saved for slot in by_row])
+
+
+def collect_kernel(slots, info, *refs):
+    out_ref, sems = refs[slots], refs[slots + 1]
+    rows = range(out_ref.shape[0])
+
+    def copy(n, slot):
+        return pltpu.make_async_copy(refs[slot], out_ref.at[n], sems.at[n])
+
+    for s, used in enumerate(slots_of(rows)):
+        @pl.when(info[2] == s)
+        def _():
+            for n, slot in enumerate(used):
+                copy(n, slot).start()
+
+    for n in rows:
+        copy(n, n).wait()
+
+
+def collect(info, gi, rows):
+    return pl.pallas_call(
+        functools.partial(collect_kernel, len(gi)),
+        out_shape=jax.ShapeDtypeStruct((rows,) + gi[0].shape, BF16),
+        grid_spec=pltpu.PrefetchScalarGridSpec(
+            num_scalar_prefetch=1,
+            grid=(1,),
+            in_specs=[pl.BlockSpec(memory_space=pl.ANY)] * len(gi),
+            out_specs=pl.BlockSpec(memory_space=pl.ANY),
+            scratch_shapes=[pltpu.SemaphoreType.DMA((rows,))],
+        ),
+        compiler_params=params(4),
+        cost_estimate=pl.CostEstimate(flops=0, bytes_accessed=2_000_000, transcendentals=0),
+        name="collect_grad_inputs",
+    )(info, *gi)
 
 
 def tile_pairs(partner):
@@ -411,25 +470,23 @@
     return lax.ppermute(value.astype(BF16), "tile", tile_pairs(partner))
 
 
-def scatter_sum(keep, send):
-    lanes = keep.shape[-1]
-    got = swap(send, lambda x, z, c: (x, z, 1 - c))
+def scatter_sum(keep_a, send_a, keep_b, send_b):
+    lanes = keep_a.shape[-1]
+    other_core = lambda x, z, c: (x, z, 1 - c)
     inner_pair = lambda x, z, c: (x ^ 1, z, c)
     outer_pair = lambda x, z, c: (3 - x, z, c)
-    cut = X * A_SEGS * 32
-
-    def own(first, last):
-        return keep[first:last].astype(F32) + got[first:last].astype(F32)
-
-    half_a, half_b = cut // 2, (keep.shape[0] - cut) // 2
-    quart_a, quart_b = half_a // 2, half_b // 2
-    got_a = swap(own(0, half_a), inner_pair)
-    got_b = swap(own(cut, cut + half_b), outer_pair)
-    at_a, at_b = half_a, cut + half_b
-    got_a2 = swap(own(at_a, at_a + quart_a) + got_a[:quart_a].astype(F32), outer_pair)
-    got_b2 = swap(own(at_b, at_b + quart_b) + got_b[:quart_b].astype(F32), inner_pair)
-    part_a = own(at_a + quart_a, cut) + got_a[quart_a:].astype(F32) + got_a2.astype(F32)
-    part_b = own(at_b + quart_b, keep.shape[0]) + got_b[quart_b:].astype(F32) + got_b2.astype(F32)
+
+    def along_x(keep, send, pairs):
+        got = swap(send, other_core)
+        own = lambda first, last: keep[first:last].astype(F32) + got[first:last].astype(F32)
+        size = keep.shape[0]
+        half, quart = size // 2, size // 4
+        got_1 = swap(own(0, half), pairs[0])
+        got_2 = swap(own(half, half + quart) + got_1[:quart].astype(F32), pairs[1])
+        return own(half + quart, size) + got_1[quart:].astype(F32) + got_2.astype(F32)
+
+    part_a = along_x(keep_a, send_a, (inner_pair, outer_pair))
+    part_b = along_x(keep_b, send_b, (outer_pair, inner_pair))
     total = jnp.concatenate([part_a, part_b], axis=0).reshape(SEGS, Z * 4, lanes)
     count = Z * 4 // 2
     got = swap(total[:, :count], lambda x, z, c: (x, z ^ 1, c))
@@ -500,7 +557,7 @@
 
     back_one = [(i, i - 1) for i in range(1, sections)]
     slots = rows + LAG * (sections - 1)
-    arriving = [jnp.zeros((hgt * (width + 2 * RIM), ch), BF16)] * LAG
+    arriving = [jnp.zeros((hgt * (width + 2), ch), BF16)] * LAG
     per_slot = []
     for slot in range(slots):
         micro = slot - LAG * (sections - 1 - section)
@@ -508,8 +565,10 @@
             [jnp.clip(micro, 0, rows - 1), (section == sections - 1).astype(micro.dtype)]
         ).astype(jnp.int32)
         hand_on = slot + LAG < slots
+        senders = [s for s in range(1, sections) if 0 <= slot - LAG * (sections - 1 - s) < rows]
+        sent = width + 2 * max(senders, default=1)
         *saved, last = chain_step(
-            info, arriving[slot], seed, mz, h2, h1, at_hand[4], at_hand[3], at_hand[2], inner, outer, hgt, hand_on
+            info, arriving[slot], seed, mz, h2, h1, at_hand[4], at_hand[3], at_hand[2], inner, outer, hgt, hand_on, sent
         )
         if hand_on:
             arriving.append(lax.ppermute(last, "section", back_one))
@@ -518,8 +577,12 @@
         per_slot.append(saved)
     gi, g3, g2, g1 = zip(*per_slot)
     info = jnp.stack([tile % CORES, tile // (CORES * Z), section]).astype(jnp.int32)
-    keep, send, grad_inputs = weight_grads(info, xt, pt, ht, g1, g2, g3, gi, rows)
-    g_reduce, g_conv, g_expand = scatter_sum(keep, send)
+    early, late = range(rows - 1), range(rows - 1, rows)
+    so_far = weight_grads(info, (0, 1), early, (xt, pt, ht, pt), (g1, g2, g3), (), "weight_gradients_early")
+    sums_a = weight_grads(info, (0,), late, (xt, pt), (g1, g2), so_far[:2], "weight_gradients_a")
+    sums_b = weight_grads(info, (1,), late, (ht, pt), (g3, g2), so_far[2:], "weight_gradients_b")
+    g_reduce, g_conv, g_expand = scatter_sum(*sums_a, *sums_b)
+    grad_inputs = collect(info, gi, rows)
     grad_inputs = grad_inputs.reshape(rows, hgt, width, ch)
     return grad_inputs[None], g_reduce[None], g_conv[None], g_expand[None]
 

time: 130 us -> 125 us (0.962)
  waiting for transfers between devices: 51.8 us -> 44.3 us
  Pallas kernels: 34 us -> 38.2 us
    ppermute x8, waiting for transfers between devices: 22.6 us -> 16.2 us  [per_device(): arriving.append(lax.ppermute(last, 'section', back_one))]
    pallas_call x1 -> x4, Pallas kernels: 3.37 us -> 6.58 us  [the longest x3 5.04 us: weight_grads(): pl.pallas_call(functools.partial(weights_kernel, parts, rows, by_row, len...]
    ppermute x9 -> x10, starting transfers between devices: 9.78 us -> 8.83 us  [swap(): return lax.ppermute(value.astype(BF16), 'tile', tile_pairs(partner))]
    ppermute x9 -> x10, waiting for transfers between devices: 27.1 us -> 26.5 us  [swap(): return lax.ppermute(value.astype(BF16), 'tile', tile_pairs(partner))]
  transfers between devices with their start and end apart: 19 -> 20, of which waited for: 19 -> 17; matrix products, arithmetic and copies ran while one was open for 1% -> 1% of each run, Pallas kernels for 14% -> 20%
where the time goes in v3:
time: 125 us
  waiting for transfers between devices  44.3 us (35%)
  Pallas kernels  38.2 us (31%)
  starting transfers between devices  37.3 us (30%)
  local copies, waits for them, and re-layouts  2.2 us (2%)
  other arithmetic  1.55 us (1%)
    ppermute x10, waiting for transfers between devices, swap(): return lax.ppermute(value.astype(BF16), 'tile', tile_pairs(partner))  26.5 us
    pallas_call x10, Pallas kernels, chain_step(): pl.pallas_call(chain_kernel, out_shape=[jax.ShapeDtypeStruct(s, BF16) for...  21.6 us
    ppermute x8, starting transfers between devices, per_device(): arriving.append(lax.ppermute(last, 'section', back_one))  19.1 us
    ppermute x8, waiting for transfers between devices, per_device(): arriving.append(lax.ppermute(last, 'section', back_one))  16.2 us
    ppermute x10, starting transfers between devices, swap(): return lax.ppermute(value.astype(BF16), 'tile', tile_pairs(partner))  8.83 us
    ppermute x1, starting transfers between devices, neighbours(): high = lax.ppermute(first, 'tile', [(b, a) for a, b in pairs])  7.47 us
    pallas_call x3, Pallas kernels, weight_grads(): pl.pallas_call(functools.partial(weights_kernel, parts, rows, by_row, len...  5.04 us
    pallas_call x1, Pallas kernels, forward(): pl.pallas_call(forward_kernel, out_shape=[jax.ShapeDtypeStruct(s, BF16) f...  4.52 us
  transfers between devices with their start and end apart: 20, of which 17 were waited for; matrix products, arithmetic and copies ran while one was open for 1% of the time, Pallas kernels for 20%

profile of v3, /device:TPU:22, one launch (start us, length us, event | category | flops | bytes accessed | tf_op | source)
XLA Modules:
  0.0 124.8 jit_solution(15081355881128560862)
XLA Ops:
  0.7 3.1 %edge_columns.1 = (bf16[4,6,8,1024]{3,2,1,0:T(8,128)(2,1)}, bf16[4,6,8,1024]{3,2,1,0:T(8,128)(2,1)}) custom-call(s32[4,4]{1,0:T(4,128)} %tissue.3, bf16[4,4,32,1024]{3,2,1,0:T(8,128)(2,1)} %bitcast.29, bf16[4,4,32,1024]{3,2,1,0:T(8,128)(2,1)} %bitcast.30, bf16[4,4,32,1024]{3,2,1,0:T(8,128)(2,1)} %og_ref.1, bf16[4,4,32,1024]{3,2,1,0:T(8,128)(2,1)} %og_ref.1), custom_call_target="tpu_custom_call" | custom-call | tf_op jit(solution)/shard_map/edge_columns/pallas_call | solution.py:60
  5.7 7.5 %collective-permute-start.1 = (bf16[4,6,8,1024]{3,2,1,0:T(8,128)(2,1)}, bf16[4,6,8,1024]{3,2,1,0:T(8,128)(2,1)}, u32[]{:S(2)}, u32[]{:S(2)}) collective-permute-start(bf16[4,6,8,1024]{3,2,1,0:T(8,128)(2,1)} %get-tuple-element.80), channel_id=1, source_target_pairs={{4,0},{8,4},{12,8},{16,12},{20,16},{24,20},{28,24},{32,28},{36,32}... | collective-permute-start | bytes 1179656 | tf_op jit(solution)/shard_map/ppermute | solution.py:532
  18.8 4.5 %forward_all_rows.1 = (bf16[4,160,1024]{2,1,0:T(8,128)(2,1)S(1)}, bf16[4,160,256]{2,1,0:T(8,128)(2,1)S(1)}, bf16[4,160,256]{2,1,0:T(8,128)(2,1)S(1)}, bf16[4,6,4...) custom-call(s32[2]{0:T(128)S(1)} %add_convert_fusion.4.ends, s32[4,4]{1,0:T(4,128)S(1)} %copy-done.6, ...), custom_call_target="tpu_custom_call" | custom-call | flops 2000000000 | bytes 12000000 | tf_op jit(solution)/shard_map/forward_all_rows/pallas_call | solution.py:161
  23.3 2.2 %chain_row.10 = (bf16[128,1024]{1,0:T(8,128)(2,1)S(1)}, bf16[128,1024]{1,0:T(8,128)(2,1)S(1)}, bf16[128,256]{1,0:T(8,128)(2,1)S(1)}, bf16[128,256]{1,0:T(8,128)(2,1)S(1)}, bf16[152,1024]{1,0:T(8,128)(2,1)S(1)}) custom-call(s32[2]{0:T(128)S(1)} %get-tuple-element.161.info, bf16[136,1024]{1,0:T(8,128)(2,1)S(1)} %broadcast_in_dim.12.gy_ref, ...), custom_call_target="tpu_custom_call" | custom-call | flops 3600000000 | bytes 50000000 | tf_op jit(solution)/shard_map/chain_row/pallas_call | solution.py:243
  25.5 2.4 %collective-permute-start.2 = (bf16[152,1024]{1,0:T(8,128)(2,1)S(1)}, bf16[152,1024]{1,0:T(8,128)(2,1)S(1)}, u32[]{:S(2)}, u32[]{:S(2)}) collective-permute-start(bf16[152,1024]{1,0:T(8,128)(2,1)S(1)} %get-tuple-element.93), channel_id=1, source_target_pairs={{1,0},{2,1},{3,2},{5,4},{6,5},{7,6},{9,8},{10,9},{11,10},{13,12},{... | collective-permute-start | bytes 933896 | tf_op jit(solution)/shard_map/ppermute | solution.py:574
  27.9 2.2 %chain_row.11 = (bf16[128,1024]{1,0:T(8,128)(2,1)S(1)}, bf16[128,1024]{1,0:T(8,128)(2,1)S(1)}, bf16[128,256]{1,0:T(8,128)(2,1)S(1)}, bf16[128,256]{1,0:T(8,128)(2,1)S(1)}, bf16[152,1024]{1,0:T(8,128)(2,1)S(1)}) custom-call(s32[2]{0:T(128)S(1)} %get-tuple-element.162.info, bf16[136,1024]{1,0:T(8,128)(2,1)S(1)} %broadcast_in_dim.12.gy_ref, ...), custom_call_target="tpu_custom_call" | custom-call | flops 3600000000 | bytes 50000000 | tf_op jit(solution)/shard_map/chain_row/pallas_call | solution.py:243
  30.0 2.4 %collective-permute-start.3 = (bf16[152,1024]{1,0:T(8,128)(2,1)S(1)}, bf16[152,1024]{1,0:T(8,128)(2,1)S(1)}, u32[]{:S(2)}, u32[]{:S(2)}) collective-permute-start(bf16[152,1024]{1,0:T(8,128)(2,1)S(1)} %get-tuple-element.95), channel_id=1, source_target_pairs={{1,0},{2,1},{3,2},{5,4},{6,5},{7,6},{9,8},{10,9},{11,10},{13,12},{... | collective-permute-start | bytes 933896 | tf_op jit(solution)/shard_map/ppermute | solution.py:574
  33.6 3.8 %collective-permute-done.2.gy_ref = bf16[152,1024]{1,0:T(8,128)(2,1)S(1)} collective-permute-done((bf16[152,1024]{1,0:T(8,128)(2,1)S(1)}, bf16[152,1024]{1,0:T(8,128)(2,1)S(1)}, u32[]{:S(2)}, u32[]{:S(2)}) %collective-permute-start.2) | collective-permute-done | bytes 311328 | tf_op jit(solution)/shard_map/ppermute | solution.py:574
  37.4 2.2 %chain_row.12 = (bf16[128,1024]{1,0:T(8,128)(2,1)S(1)}, bf16[128,1024]{1,0:T(8,128)(2,1)S(1)}, bf16[128,256]{1,0:T(8,128)(2,1)S(1)}, bf16[128,256]{1,0:T(8,128)(2,1)S(1)}, bf16[152,1024]{1,0:T(8,128)(2,1)S(1)}) custom-call(s32[2]{0:T(128)S(1)} %pad_add_fusion.4.info, bf16[152,1024]{1,0:T(8,128)(2,1)S(1)} %collective-permute-done.2.gy_ref, ...), custom_call_target="tpu_custom_call" | custom-call | flops 3600000000 | bytes 50000000 | tf_op jit(solution)/shard_map/chain_row/pallas_call | solution.py:243
  39.5 2.4 %collective-permute-start.4 = (bf16[152,1024]{1,0:T(8,128)(2,1)S(1)}, bf16[152,1024]{1,0:T(8,128)(2,1)S(1)}, u32[]{:S(2)}, u32[]{:S(2)}) collective-permute-start(bf16[152,1024]{1,0:T(8,128)(2,1)S(1)} %get-tuple-element.97), channel_id=1, source_target_pairs={{1,0},{2,1},{3,2},{5,4},{6,5},{7,6},{9,8},{10,9},{11,10},{13,12},{... | collective-permute-start | bytes 933896 | tf_op jit(solution)/shard_map/ppermute | solution.py:574
  44.0 2.2 %chain_row.13 = (bf16[128,1024]{1,0:T(8,128)(2,1)S(1)}, bf16[128,1024]{1,0:T(8,128)(2,1)S(1)}, bf16[128,256]{1,0:T(8,128)(2,1)S(1)}, bf16[128,256]{1,0:T(8,128)(2,1)S(1)}, bf16[152,1024]{1,0:T(8,128)(2,1)S(1)}) custom-call(s32[2]{0:T(128)S(1)} %pad_add_fusion.5.info, bf16[152,1024]{1,0:T(8,128)(2,1)S(1)} %collective-permute-done.3.gy_ref, ...), custom_call_target="tpu_custom_call" | custom-call | flops 3600000000 | bytes 50000000 | tf_op jit(solution)/shard_map/chain_row/pallas_call | solution.py:243
  46.2 2.4 %collective-permute-start.5 = (bf16[152,1024]{1,0:T(8,128)(2,1)S(1)}, bf16[152,1024]{1,0:T(8,128)(2,1)S(1)}, u32[]{:S(2)}, u32[]{:S(2)}) collective-permute-start(bf16[152,1024]{1,0:T(8,128)(2,1)S(1)} %get-tuple-element.99), channel_id=1, source_target_pairs={{1,0},{2,1},{3,2},{5,4},{6,5},{7,6},{9,8},{10,9},{11,10},{13,12},{... | collective-permute-start | bytes 933896 | tf_op jit(solution)/shard_map/ppermute | solution.py:574
  50.6 2.2 %chain_row.14 = (bf16[128,1024]{1,0:T(8,128)(2,1)S(1)}, bf16[128,1024]{1,0:T(8,128)(2,1)S(1)}, bf16[128,256]{1,0:T(8,128)(2,1)S(1)}, bf16[128,256]{1,0:T(8,128)(2,1)S(1)}, bf16[144,1024]{1,0:T(8,128)(2,1)S(1)}) custom-call(s32[2]{0:T(128)S(1)} %pad_add_fusion.6.info, bf16[152,1024]{1,0:T(8,128)(2,1)S(1)} %collective-permute-done.4.gy_ref, ...), custom_call_target="tpu_custom_call" | custom-call | flops 3600000000 | bytes 50000000 | tf_op jit(solution)/shard_map/chain_row/pallas_call | solution.py:243
  52.8 2.6 %collective-permute-start.6 = (bf16[144,1024]{1,0:T(8,128)(2,1)S(1)}, bf16[144,1024]{1,0:T(8,128)(2,1)S(1)}, u32[]{:S(2)}, u32[]{:S(2)}) collective-permute-start(bf16[144,1024]{1,0:T(8,128)(2,1)S(1)} %get-tuple-element.101), channel_id=1, source_target_pairs={{1,0},{2,1},{3,2},{5,4},{6,5},{7,6},{9,8},{10,9},{11,10},{13,12},{... | collective-permute-start | bytes 884744 | tf_op jit(solution)/shard_map/ppermute | solution.py:574
  55.3 2.9 %collective-permute-done.5.gy_ref = bf16[152,1024]{1,0:T(8,128)(2,1)S(1)} collective-permute-done((bf16[152,1024]{1,0:T(8,128)(2,1)S(1)}, bf16[152,1024]{1,0:T(8,128)(2,1)S(1)}, u32[]{:S(2)}, u32[]{:S(2)}) %collective-permute-start.5) | collective-permute-done | bytes 311328 | tf_op jit(solution)/shard_map/ppermute | solution.py:574
  58.2 2.2 %chain_row.15 = (bf16[128,1024]{1,0:T(8,128)(2,1)S(1)}, bf16[128,1024]{1,0:T(8,128)(2,1)S(1)}, bf16[128,256]{1,0:T(8,128)(2,1)S(1)}, bf16[128,256]{1,0:T(8,128)(2,1)S(1)}, bf16[144,1024]{1,0:T(8,128)(2,1)S(1)}) custom-call(s32[2]{0:T(128)S(1)} %pad_add_fusion.7.info, bf16[152,1024]{1,0:T(8,128)(2,1)S(1)} %collective-permute-done.5.gy_ref, ...), custom_call_target="tpu_custom_call" | custom-call | flops 3600000000 | bytes 50000000 | tf_op jit(solution)/shard_map/chain_row/pallas_call | solution.py:243
  60.4 2.4 %collective-permute-start.7 = (bf16[144,1024]{1,0:T(8,128)(2,1)S(1)}, bf16[144,1024]{1,0:T(8,128)(2,1)S(1)}, u32[]{:S(2)}, u32[]{:S(2)}) collective-permute-start(bf16[144,1024]{1,0:T(8,128)(2,1)S(1)} %get-tuple-element.103), channel_id=1, source_target_pairs={{1,0},{2,1},{3,2},{5,4},{6,5},{7,6},{9,8},{10,9},{11,10},{13,12},{... | collective-permute-start | bytes 884744 | tf_op jit(solution)/shard_map/ppermute | solution.py:574
  64.5 2.2 %chain_row.16 = (bf16[128,1024]{1,0:T(8,128)(2,1)S(1)}, bf16[128,1024]{1,0:T(8,128)(2,1)S(1)}, bf16[128,256]{1,0:T(8,128)(2,1)S(1)}, bf16[128,256]{1,0:T(8,128)(2,1)S(1)}, bf16[136,1024]{1,0:T(8,128)(2,1)S(1)}) custom-call(s32[2]{0:T(128)S(1)} %pad_add_fusion.8.info, bf16[144,1024]{1,0:T(8,128)(2,1)S(1)} %collective-permute-done.6.gy_ref, ...), custom_call_target="tpu_custom_call" | custom-call | flops 3600000000 | bytes 50000000 | tf_op jit(solution)/shard_map/chain_row/pallas_call | solution.py:243
  66.7 2.4 %collective-permute-start.8 = (bf16[136,1024]{1,0:T(8,128)(2,1)S(1)}, bf16[136,1024]{1,0:T(8,128)(2,1)S(1)}, u32[]{:S(2)}, u32[]{:S(2)}) collective-permute-start(bf16[136,1024]{1,0:T(8,128)(2,1)S(1)} %get-tuple-element.105), channel_id=1, source_target_pairs={{1,0},{2,1},{3,2},{5,4},{6,5},{7,6},{9,8},{10,9},{11,10},{13,12},{... | collective-permute-start | bytes 835592 | tf_op jit(solution)/shard_map/ppermute | solution.py:574
  70.9 2.2 %chain_row.17 = (bf16[128,1024]{1,0:T(8,128)(2,1)S(1)}, bf16[128,1024]{1,0:T(8,128)(2,1)S(1)}, bf16[128,256]{1,0:T(8,128)(2,1)S(1)}, bf16[128,256]{1,0:T(8,128)(2,1)S(1)}, bf16[136,1024]{1,0:T(8,128)(2,1)S(1)}) custom-call(s32[2]{0:T(128)S(1)} %pad_add_fusion.9.info, bf16[144,1024]{1,0:T(8,128)(2,1)S(1)} %collective-permute-done.7.gy_ref, ...), custom_call_target="tpu_custom_call" | custom-call | flops 3600000000 | bytes 50000000 | tf_op jit(solution)/shard_map/chain_row/pallas_call | solution.py:243
  73.1 2.4 %collective-permute-start.9 = (bf16[136,1024]{1,0:T(8,128)(2,1)S(1)}, bf16[136,1024]{1,0:T(8,128)(2,1)S(1)}, u32[]{:S(2)}, u32[]{:S(2)}) collective-permute-start(bf16[136,1024]{1,0:T(8,128)(2,1)S(1)} %get-tuple-element.107), channel_id=1, source_target_pairs={{1,0},{2,1},{3,2},{5,4},{6,5},{7,6},{9,8},{10,9},{11,10},{13,12},{... | collective-permute-start | bytes 835592 | tf_op jit(solution)/shard_map/ppermute | solution.py:574
  77.2 2.1 %chain_row.18 = (bf16[128,1024]{1,0:T(8,128)(2,1)S(1)}, bf16[128,1024]{1,0:T(8,128)(2,1)S(1)}, bf16[128,256]{1,0:T(8,128)(2,1)S(1)}, bf16[128,256]{1,0:T(8,128)(2,1)S(1)}) custom-call(s32[2]{0:T(128)S(1)} %pad_add_fusion.10.info, bf16[136,1024]{1,0:T(8,128)(2,1)S(1)} %collective-permute-done.8.gy_ref, bf16[4,160,1024]{2,1,0:T(8,128)(2,1)S(1)} %get-tuple-element.87.seed_ref, ...), custom_call_target="tpu_custom_call" | custom-call | flops 3600000000 | bytes 50000000 | tf_op jit(solution)/shard_map/chain_row/pallas_call | solution.py:243
  79.4 2.7 %weight_gradients_early.1 = (bf16[1024,256]{1,0:T(8,128)(2,1)S(1)}, bf16[1024,256]{1,0:T(8,128)(2,1)S(1)}, bf16[1152,256]{1,0:T(8,128)(2,1)S(1)}, bf16[1152,256]{1,0:T(8,128)(2,1)S(1)}) custom-call(s32[3]{0:T(128)S(1)} %pad_add_fusion.1.info, bf16[1024,512]{1,0:T(8,128)(2,1)S(1)} %get-tuple-element.110.refs_0_, ...), custom_call_target="tpu_custom_call" | custom-call | flops 900000000 | bytes 6000000 | tf_op jit(solution)/shard_map/weight_gradients_early/pallas_call | solution.py:405
  82.1 2.1 %chain_row.19 = (bf16[128,1024]{1,0:T(8,128)(2,1)S(1)}, bf16[128,1024]{1,0:T(8,128)(2,1)S(1)}, bf16[128,256]{1,0:T(8,128)(2,1)S(1)}, bf16[128,256]{1,0:T(8,128)(2,1)S(1)}) custom-call(s32[2]{0:T(128)S(1)} %pad_add_fusion.11.info, bf16[136,1024]{1,0:T(8,128)(2,1)S(1)} %collective-permute-done.9.gy_ref, bf16[4,160,1024]{2,1,0:T(8,128)(2,1)S(1)} %get-tuple-element.87.seed_ref, ...), custom_call_target="tpu_custom_call" | custom-call | flops 3600000000 | bytes 50000000 | tf_op jit(solution)/shard_map/chain_row/pallas_call | solution.py:243
  89.5 6.4 %collective-permute-done.11 = bf16[512,256]{1,0:T(8,128)(2,1)S(1)} collective-permute-done((bf16[512,256]{1,0:T(8,128)(2,1)S(1)}, bf16[512,256]{1,0:T(8,128)(2,1)S(1)}, u32[]{:S(2)}, u32[]{:S(2)}) %collective-permute-start.11) | collective-permute-done | bytes 262176 | tf_op jit(solution)/shard_map/ppermute | solution.py:470
  96.1 3.8 %collective-permute-done.14 = bf16[576,256]{1,0:T(8,128)(2,1)S(1)} collective-permute-done((bf16[576,256]{1,0:T(8,128)(2,1)S(1)}, bf16[576,256]{1,0:T(8,128)(2,1)S(1)}, u32[]{:S(2)}, u32[]{:S(2)}) %collective-permute-start.14) | collective-permute-done | bytes 294944 | tf_op jit(solution)/shard_map/ppermute | solution.py:470
  100.0 2.3 %collective-permute-done.12 = bf16[256,256]{1,0:T(8,128)(2,1)S(1)} collective-permute-done((bf16[256,256]{1,0:T(8,128)(2,1)S(1)}, bf16[256,256]{1,0:T(8,128)(2,1)S(1)}, u32[]{:S(2)}, u32[]{:S(2)}) %collective-permute-start.12) | collective-permute-done | bytes 131104 | tf_op jit(solution)/shard_map/ppermute | solution.py:470
  102.4 2.7 %collective-permute-done.15 = bf16[288,256]{1,0:T(8,128)(2,1)S(1)} collective-permute-done((bf16[288,256]{1,0:T(8,128)(2,1)S(1)}, bf16[288,256]{1,0:T(8,128)(2,1)S(1)}, u32[]{:S(2)}, u32[]{:S(2)}) %collective-permute-start.15) | collective-permute-done | bytes 147488 | tf_op jit(solution)/shard_map/ppermute | solution.py:470
  105.4 5.0 %collective-permute-done.16 = bf16[17,16,256]{2,1,0:T(8,128)(2,1)S(1)} collective-permute-done((bf16[17,16,256]{2,1,0:T(8,128)(2,1)S(1)}, bf16[17,16,256]{2,1,0:T(8,128)(2,1)S(1)}, u32[]{:S(2)}, u32[]{:S(2)}) %collective-permute-start.16) | collective-permute-done | bytes 139296 | tf_op jit(solution)/shard_map/ppermute | solution.py:470
  110.5 3.3 %collective-permute-start.17 = (bf16[17,4,256]{2,1,0:T(4,128)(2,1)S(1)}, bf16[17,4,256]{2,1,0:T(4,128)(2,1)S(1)}, u32[]{:S(2)}, u32[]{:S(2)}) collective-permute-start(bf16[17,4,256]{2,1,0:T(4,128)(2,1)S(1)} %get-tuple-element.158), channel_id=1, source_target_pairs={{0,48},{4,52},{8,56},{12,60},{16,32},{20,36},{24,40},{28,44},{32,1... | collective-permute-start | bytes 104456 | tf_op jit(solution)/shard_map/ppermute | solution.py:470
  113.8 2.5 %collective-permute-start.18 = (bf16[17,4,256]{2,1,0:T(4,128)(2,1)S(1)}, bf16[17,4,256]{2,1,0:T(4,128)(2,1)S(1)}, u32[]{:S(2)}, u32[]{:S(2)}) collective-permute-start(bf16[17,4,256]{2,1,0:T(4,128)(2,1)S(1)} %get-tuple-element.157), channel_id=1, source_target_pairs={{0,16},{4,20},{8,24},{12,28},{16,0},{20,4},{24,8},{28,12},{32,48},... | collective-permute-start | bytes 104456 | tf_op jit(solution)/shard_map/ppermute | solution.py:470
  118.9 5.2 %collective-permute-done.19.refs_2_ = bf16[17,4,256]{2,1,0:T(4,128)(2,1)S(1)} collective-permute-done((bf16[17,4,256]{2,1,0:T(4,128)(2,1)S(1)}, bf16[17,4,256]{2,1,0:T(4,128)(2,1)S(1)}, u32[]{:S(2)}, u32[]{:S(2)}) %collective-permute-start.19) | collective-permute-done | bytes 34848 | tf_op jit(solution)/shard_map/ppermute | solution.py:470
  (72 shorter events, 27.3 us)
Async XLA Ops:
  0.6 13.6 %copy-start = (bf16[4,4,32,1024]{3,2,1,0:T(8,128)(2,1)S(1)}, bf16[4,4,32,1024]{3,2,1,0:T(8,128)(2,1)}, u32[]{:S(2)}) copy-start(bf16[4,4,32,1024]{3,2,1,0:T(8,128)(2,1)} %og_ref.1) | copy-start | bytes 3145732
  0.6 13.6 %copy-start.1 = (bf16[1,4,4,32,1024]{4,3,2,1,0:T(8,128)(2,1)S(1)}, bf16[1,4,4,32,1024]{4,3,2,1,0:T(8,128)(2,1)}, u32[]{:S(2)}) copy-start(bf16[1,4,4,32,1024]{4,3,2,1,0:T(8,128)(2,1)} %param.9) | copy-start | bytes 3145732
  0.7 13.5 %copy-start.2 = (bf16[1,3,3,256,256]{4,3,2,1,0:T(8,128)(2,1)S(1)}, bf16[1,3,3,256,256]{4,3,2,1,0:T(8,128)(2,1)}, u32[]{:S(2)}) copy-start(bf16[1,3,3,256,256]{4,3,2,1,0:T(8,128)(2,1)} %param.13) | copy-start | bytes 3538948
  0.7 13.5 %copy-start.5 = (f32[1,4,256]{2,1,0:T(4,128)S(1)}, f32[1,4,256]{2,1,0:T(4,128)}, u32[]{:S(2)}) copy-start(f32[1,4,256]{2,1,0:T(4,128)} %param.15) | copy-start | bytes 12292
  3.8 13.4 %collective-permute-start = (bf16[4,6,8,1024]{3,2,1,0:T(8,128)(2,1)}, bf16[4,6,8,1024]{3,2,1,0:T(8,128)(2,1)}, u32[]{:S(2)}, u32[]{:S(2)}) collective-permute-start(bf16[4,6,8,1024]{3,2,1,0:T(8,128)(2,1)} %get-tuple-element.79), channel_id=1, source_target_pairs={{0,4},{4,8},{8,12},{12,16},{16,20},{20,24},{24,28},{28,32},{32,36}... | collective-permute-start | bytes 1179656 | tf_op jit(solution)/shard_map/ppermute | solution.py:531
  5.7 13.1 %collective-permute-start.1 = (bf16[4,6,8,1024]{3,2,1,0:T(8,128)(2,1)}, bf16[4,6,8,1024]{3,2,1,0:T(8,128)(2,1)}, u32[]{:S(2)}, u32[]{:S(2)}) collective-permute-start(bf16[4,6,8,1024]{3,2,1,0:T(8,128)(2,1)} %get-tuple-element.80), channel_id=1, source_target_pairs={{4,0},{8,4},{12,8},{16,12},{20,16},{24,20},{28,24},{32,28},{36,32}... | collective-permute-start | bytes 1179656 | tf_op jit(solution)/shard_map/ppermute | solution.py:532
  14.2 1.0 copy-start.3
  15.3 1.0 copy-start.4
  16.3 2.5 %copy-start.6 = (s32[4,4]{1,0:T(4,128)S(1)}, s32[4,4]{1,0:T(4,128)}, u32[]{:S(2)}) copy-start(s32[4,4]{1,0:T(4,128)} %tissue.3) | copy-start | bytes 196
  16.3 2.5 %copy-start.7 = (f32[1,2,1024]{2,1,0:T(2,128)S(1)}, f32[1,2,1024]{2,1,0:T(2,128)}, u32[]{:S(2)}) copy-start(f32[1,2,1024]{2,1,0:T(2,128)} %param.16) | copy-start | bytes 24580
  25.5 11.9 %collective-permute-start.2 = (bf16[152,1024]{1,0:T(8,128)(2,1)S(1)}, bf16[152,1024]{1,0:T(8,128)(2,1)S(1)}, u32[]{:S(2)}, u32[]{:S(2)}) collective-permute-start(bf16[152,1024]{1,0:T(8,128)(2,1)S(1)} %get-tuple-element.93), channel_id=1, source_target_pairs={{1,0},{2,1},{3,2},{5,4},{6,5},{7,6},{9,8},{10,9},{11,10},{13,12},{... | collective-permute-start | bytes 933896 | tf_op jit(solution)/shard_map/ppermute | solution.py:574
  30.0 14.0 %collective-permute-start.3 = (bf16[152,1024]{1,0:T(8,128)(2,1)S(1)}, bf16[152,1024]{1,0:T(8,128)(2,1)S(1)}, u32[]{:S(2)}, u32[]{:S(2)}) collective-permute-start(bf16[152,1024]{1,0:T(8,128)(2,1)S(1)} %get-tuple-element.95), channel_id=1, source_target_pairs={{1,0},{2,1},{3,2},{5,4},{6,5},{7,6},{9,8},{10,9},{11,10},{13,12},{... | collective-permute-start | bytes 933896 | tf_op jit(solution)/shard_map/ppermute | solution.py:574
  39.5 11.1 %collective-permute-start.4 = (bf16[152,1024]{1,0:T(8,128)(2,1)S(1)}, bf16[152,1024]{1,0:T(8,128)(2,1)S(1)}, u32[]{:S(2)}, u32[]{:S(2)}) collective-permute-start(bf16[152,1024]{1,0:T(8,128)(2,1)S(1)} %get-tuple-element.97), channel_id=1, source_target_pairs={{1,0},{2,1},{3,2},{5,4},{6,5},{7,6},{9,8},{10,9},{11,10},{13,12},{... | collective-permute-start | bytes 933896 | tf_op jit(solution)/shard_map/ppermute | solution.py:574
  46.2 12.0 %collective-permute-start.5 = (bf16[152,1024]{1,0:T(8,128)(2,1)S(1)}, bf16[152,1024]{1,0:T(8,128)(2,1)S(1)}, u32[]{:S(2)}, u32[]{:S(2)}) collective-permute-start(bf16[152,1024]{1,0:T(8,128)(2,1)S(1)} %get-tuple-element.99), channel_id=1, source_target_pairs={{1,0},{2,1},{3,2},{5,4},{6,5},{7,6},{9,8},{10,9},{11,10},{13,12},{... | collective-permute-start | bytes 933896 | tf_op jit(solution)/shard_map/ppermute | solution.py:574
  52.8 11.8 %collective-permute-start.6 = (bf16[144,1024]{1,0:T(8,128)(2,1)S(1)}, bf16[144,1024]{1,0:T(8,128)(2,1)S(1)}, u32[]{:S(2)}, u32[]{:S(2)}) collective-permute-start(bf16[144,1024]{1,0:T(8,128)(2,1)S(1)} %get-tuple-element.101), channel_id=1, source_target_pairs={{1,0},{2,1},{3,2},{5,4},{6,5},{7,6},{9,8},{10,9},{11,10},{13,12},{... | collective-permute-start | bytes 884744 | tf_op jit(solution)/shard_map/ppermute | solution.py:574
  60.4 10.5 %collective-permute-start.7 = (bf16[144,1024]{1,0:T(8,128)(2,1)S(1)}, bf16[144,1024]{1,0:T(8,128)(2,1)S(1)}, u32[]{:S(2)}, u32[]{:S(2)}) collective-permute-start(bf16[144,1024]{1,0:T(8,128)(2,1)S(1)} %get-tuple-element.103), channel_id=1, source_target_pairs={{1,0},{2,1},{3,2},{5,4},{6,5},{7,6},{9,8},{10,9},{11,10},{13,12},{... | collective-permute-start | bytes 884744 | tf_op jit(solution)/shard_map/ppermute | solution.py:574
  66.7 10.5 %collective-permute-start.8 = (bf16[136,1024]{1,0:T(8,128)(2,1)S(1)}, bf16[136,1024]{1,0:T(8,128)(2,1)S(1)}, u32[]{:S(2)}, u32[]{:S(2)}) collective-permute-start(bf16[136,1024]{1,0:T(8,128)(2,1)S(1)} %get-tuple-element.105), channel_id=1, source_target_pairs={{1,0},{2,1},{3,2},{5,4},{6,5},{7,6},{9,8},{10,9},{11,10},{13,12},{... | collective-permute-start | bytes 835592 | tf_op jit(solution)/shard_map/ppermute | solution.py:574
  73.1 9.0 %collective-permute-start.9 = (bf16[136,1024]{1,0:T(8,128)(2,1)S(1)}, bf16[136,1024]{1,0:T(8,128)(2,1)S(1)}, u32[]{:S(2)}, u32[]{:S(2)}) collective-permute-start(bf16[136,1024]{1,0:T(8,128)(2,1)S(1)} %get-tuple-element.107), channel_id=1, source_target_pairs={{1,0},{2,1},{3,2},{5,4},{6,5},{7,6},{9,8},{10,9},{11,10},{13,12},{... | collective-permute-start | bytes 835592 | tf_op jit(solution)/shard_map/ppermute | solution.py:574
  85.4 2.0 %collective-permute-start.10 = (bf16[1024,256]{1,0:T(8,128)(2,1)S(1)}, bf16[1024,256]{1,0:T(8,128)(2,1)S(1)}, u32[]{:S(2)}, u32[]{:S(2)}) collective-permute-start(bf16[1024,256]{1,0:T(8,128)(2,1)S(1)} %get-tuple-element.145), channel_id=1, source_target_pairs={{0,4},{4,0},{8,12},{12,8},{16,20},{20,16},{24,28},{28,24},{32,36},... | collective-permute-start | bytes 1572872 | tf_op jit(solution)/shard_map/ppermute | solution.py:470
  86.7 2.2 %collective-permute-start.13 = (bf16[1152,256]{1,0:T(8,128)(2,1)S(1)}, bf16[1152,256]{1,0:T(8,128)(2,1)S(1)}, u32[]{:S(2)}, u32[]{:S(2)}) collective-permute-start(bf16[1152,256]{1,0:T(8,128)(2,1)S(1)} %get-tuple-element.150), channel_id=1, source_target_pairs={{0,4},{4,0},{8,12},{12,8},{16,20},{20,16},{24,28},{28,24},{32,36},... | collective-permute-start | bytes 1769480 | tf_op jit(solution)/shard_map/ppermute | solution.py:470
  87.5 8.4 %collective-permute-start.11 = (bf16[512,256]{1,0:T(8,128)(2,1)S(1)}, bf16[512,256]{1,0:T(8,128)(2,1)S(1)}, u32[]{:S(2)}, u32[]{:S(2)}) collective-permute-start(bf16[512,256]{1,0:T(8,128)(2,1)S(1)} %add_convert_fusion.1), channel_id=1, source_target_pairs={{0,64},{4,68},{8,72},{12,76},{16,80},{20,84},{24,88},{28,92},{32,9... | collective-permute-start | bytes 786440 | tf_op jit(solution)/shard_map/ppermute | solution.py:470
  89.0 10.9 %collective-permute-start.14 = (bf16[576,256]{1,0:T(8,128)(2,1)S(1)}, bf16[576,256]{1,0:T(8,128)(2,1)S(1)}, u32[]{:S(2)}, u32[]{:S(2)}) collective-permute-start(bf16[576,256]{1,0:T(8,128)(2,1)S(1)} %add_convert_fusion), channel_id=1, source_target_pairs={{0,192},{4,196},{8,200},{12,204},{16,208},{20,212},{24,216},{28,22... | collective-permute-start | bytes 884744 | tf_op jit(solution)/shard_map/ppermute | solution.py:470
  96.0 6.4 %collective-permute-start.12 = (bf16[256,256]{1,0:T(8,128)(2,1)S(1)}, bf16[256,256]{1,0:T(8,128)(2,1)S(1)}, u32[]{:S(2)}, u32[]{:S(2)}) collective-permute-start(bf16[256,256]{1,0:T(8,128)(2,1)S(1)} %add_convert_fusion.3), channel_id=1, source_target_pairs={{0,192},{4,196},{8,200},{12,204},{16,208},{20,212},{24,216},{28,22... | collective-permute-start | bytes 393224 | tf_op jit(solution)/shard_map/ppermute | solution.py:470
  99.9 5.2 %collective-permute-start.15 = (bf16[288,256]{1,0:T(8,128)(2,1)S(1)}, bf16[288,256]{1,0:T(8,128)(2,1)S(1)}, u32[]{:S(2)}, u32[]{:S(2)}) collective-permute-start(bf16[288,256]{1,0:T(8,128)(2,1)S(1)} %add_convert_fusion.2), channel_id=1, source_target_pairs={{0,64},{4,68},{8,72},{12,76},{16,80},{20,84},{24,88},{28,92},{32,9... | collective-permute-start | bytes 442376 | tf_op jit(solution)/shard_map/ppermute | solution.py:470
  105.3 5.1 %collective-permute-start.16 = (bf16[17,16,256]{2,1,0:T(8,128)(2,1)S(1)}, bf16[17,16,256]{2,1,0:T(8,128)(2,1)S(1)}, u32[]{:S(2)}, u32[]{:S(2)}) collective-permute-start(bf16[17,16,256]{2,1,0:T(8,128)(2,1)S(1)} %slice.135), channel_id=1, source_target_pairs={{0,8},{4,12},{8,0},{12,4},{16,24},{20,28},{24,16},{28,20},{32,40},... | collective-permute-start | bytes 417800 | tf_op jit(solution)/shard_map/ppermute | solution.py:470
  110.5 8.2 %collective-permute-start.17 = (bf16[17,4,256]{2,1,0:T(4,128)(2,1)S(1)}, bf16[17,4,256]{2,1,0:T(4,128)(2,1)S(1)}, u32[]{:S(2)}, u32[]{:S(2)}) collective-permute-start(bf16[17,4,256]{2,1,0:T(4,128)(2,1)S(1)} %get-tuple-element.158), channel_id=1, source_target_pairs={{0,48},{4,52},{8,56},{12,60},{16,32},{20,36},{24,40},{28,44},{32,1... | collective-permute-start | bytes 104456 | tf_op jit(solution)/shard_map/ppermute | solution.py:470
  113.8 5.1 %collective-permute-start.18 = (bf16[17,4,256]{2,1,0:T(4,128)(2,1)S(1)}, bf16[17,4,256]{2,1,0:T(4,128)(2,1)S(1)}, u32[]{:S(2)}, u32[]{:S(2)}) collective-permute-start(bf16[17,4,256]{2,1,0:T(4,128)(2,1)S(1)} %get-tuple-element.157), channel_id=1, source_target_pairs={{0,16},{4,20},{8,24},{12,28},{16,0},{20,4},{24,8},{28,12},{32,48},... | collective-permute-start | bytes 104456 | tf_op jit(solution)/shard_map/ppermute | solution.py:470
  116.3 7.8 %collective-permute-start.19 = (bf16[17,4,256]{2,1,0:T(4,128)(2,1)S(1)}, bf16[17,4,256]{2,1,0:T(4,128)(2,1)S(1)}, u32[]{:S(2)}, u32[]{:S(2)}) collective-permute-start(bf16[17,4,256]{2,1,0:T(4,128)(2,1)S(1)} %get-tuple-element.156), channel_id=1, source_target_pairs={{0,32},{4,36},{8,40},{12,44},{16,48},{20,52},{24,56},{28,60},{32,0... | collective-permute-start | bytes 104456 | tf_op jit(solution)/shard_map/ppermute | solution.py:470

commit v4 on v3

--- a/solution.py
+++ b/solution.py
@@ -15,7 +15,7 @@
 BF16, F32 = jnp.bfloat16, jnp.float32
 LAG = 2
 SEGS, A_SEGS = 17, 8
-Z_ORDER = (7, 3, 5, 1, 6, 2, 4, 0)
+Z_ORDER = (5, 3, 7, 1, 4, 2, 6, 0)
 
 
 def params(mib):
@@ -100,22 +100,28 @@
 
 
 def forward_kernel(
-    ends, tissue, lo_ref, hi_ref, own_ref, inner_ref, outer_ref, x_ref, og_ref, wr_ref, wc_ref, we_ref,
-    mz_ref, h2_ref, h1_ref, pad_ref, seed_ref,
-    xs, hs, patches, ss,
+    some, held, ends, tissue, lo_ref, hi_ref, own_ref, inner_ref, outer_ref, x_ref, og_ref, wr_ref, wc_ref, we_ref, *refs,
 ):
-    rows, hgt, width, ch = x_ref.shape
+    before, refs = refs[:held], refs[held:]
+    mz_ref, h2_ref, h1_ref, pad_ref, seed_ref, xs, hs, patches, ss = refs
+    hgt, width, ch = x_ref.shape[1:]
     inner_w = wr_ref.shape[1]
     wide = width + 2 * RIM
     per_row = hgt * wide
-    hs[:, 0] = jnp.zeros((rows, width + 2 * EDGE, inner_w), F32)
-    hs[:, hgt + 1] = jnp.zeros((rows, width + 2 * EDGE, inner_w), F32)
-    hs[:, 1 : hgt + 1, EDGE : EDGE + width] = own_ref[...].astype(F32)
+    count, start = len(some), some[0]
+    these = slice(start, start + count)
+    for ref, out in zip(before, (mz_ref, h2_ref, h1_ref, pad_ref, seed_ref)):
+        out[:start] = ref[...]
+    into = pl.ds(start if held else 0, count)
+    hs[:, 0] = jnp.zeros((count, width + 2 * EDGE, inner_w), F32)
+    hs[:, hgt + 1] = jnp.zeros((count, width + 2 * EDGE, inner_w), F32)
+    hs[:, 1 : hgt + 1, EDGE : EDGE + width] = own_ref[these].astype(F32)
+    xs[:, :, EDGE : EDGE + width] = x_ref[these].astype(F32)
     for ref, at, keep in ((lo_ref, 0, ends[0]), (hi_ref, EDGE + width, ends[1])):
-        part = ref[:, :hgt]
+        part = ref[these, :hgt]
         xs[:, :, at : at + EDGE] = part.astype(F32)
         hs[:, 1 : hgt + 1, at : at + EDGE] = hidden_one(part, wr_ref[...], inner_ref) * keep.astype(F32)
-    pad_ref[...] = hs[...].astype(BF16)
+    pad_ref[into] = hs[...].astype(BF16)
     first = EDGE - RIM - 1
     for k in range(9):
         dr, dc = divmod(k, 3)
@@ -123,16 +129,16 @@
         piece = piece.reshape(-1, inner_w).astype(BF16)
         patches[:, k * inner_w : (k + 1) * inner_w] = piece
         if k == 4:
-            h1_ref[...] = piece.reshape(rows, hgt * wide, inner_w)
+            h1_ref[into] = piece.reshape(count, per_row, inner_w)
     pre = dot(patches[...], wc_ref[...]) * inner_ref[2:3] + inner_ref[3:4]
     hid = jnp.maximum(pre, 0.0).astype(BF16)
-    h2_ref[...] = hid.reshape(rows, hgt * wide, inner_w)
-    xs[:, :, EDGE : EDGE + width] = x_ref[...].astype(F32)
-    for r in range(rows):
-        part = hid[r * per_row : (r + 1) * per_row]
+    h2_ref[into] = hid.reshape(count, per_row, inner_w)
+    for n, r in enumerate(some):
+        out = r if held else n
+        part = hid[n * per_row : (n + 1) * per_row]
         z = dot(part, we_ref[...]) * outer_ref[0:1] + outer_ref[1:2]
-        z = z + xs[r, :, EDGE - RIM : EDGE - RIM + wide].reshape(per_row, ch)
-        mz_ref[r] = jnp.where(z > 0, 1.0, 0.0).astype(BF16)
+        z = z + xs[n, :, EDGE - RIM : EDGE - RIM + wide].reshape(per_row, ch)
+        mz_ref[out] = jnp.where(z > 0, 1.0, 0.0).astype(BF16)
         for ref, at in ((lo_ref, 0), (hi_ref, RIM + width)):
             for pair in range(hgt // 2):
                 both = ref[r, hgt + pair].astype(F32)
@@ -142,24 +148,26 @@
         for tile in range(width // TILE_W):
             cols = og[:, tile * TILE_W : (tile + 1) * TILE_W] * tissue[r, tile].astype(F32)
             ss[:, RIM + tile * TILE_W : RIM + (tile + 1) * TILE_W] = cols
-        seed_ref[r] = ss[...].reshape(per_row, ch).astype(BF16)
-
-
-def forward(ends, tissue, lo, hi, own, inner, outer, x, og, wr, wc, we):
+        seed_ref[out] = ss[...].reshape(per_row, ch).astype(BF16)
+
+
+def forward(some, before, ends, tissue, lo, hi, own, inner, outer, x, og, wr, wc, we):
     rows, hgt, width, ch = x.shape
     inner_w = wr.shape[1]
     wide = width + 2 * RIM
     pos = hgt * wide
+    count = len(some)
+    out_rows = rows if before else count
     out_shapes = (
-        (rows, pos, ch),
-        (rows, pos, inner_w),
-        (rows, pos, inner_w),
-        (rows, hgt + 2, width + 2 * EDGE, inner_w),
-        (rows, pos, ch),
+        (out_rows, pos, ch),
+        (out_rows, pos, inner_w),
+        (out_rows, pos, inner_w),
+        (out_rows, hgt + 2, width + 2 * EDGE, inner_w),
+        (out_rows, pos, ch),
     )
-    blocks = (lo, hi, own, inner, outer, x, og, wr, wc, we)
+    blocks = (lo, hi, own, inner, outer, x, og, wr, wc, we, *before)
     return pl.pallas_call(
-        forward_kernel,
+        functools.partial(forward_kernel, some, len(before)),
         out_shape=[jax.ShapeDtypeStruct(s, BF16) for s in out_shapes],
         grid_spec=pltpu.PrefetchScalarGridSpec(
             num_scalar_prefetch=2,
@@ -167,15 +175,17 @@
             in_specs=[full(a.shape) for a in blocks],
             out_specs=[full(s) for s in out_shapes],
             scratch_shapes=[
-                pltpu.VMEM((rows, hgt, width + 2 * EDGE, ch), F32),
-                pltpu.VMEM((rows, hgt + 2, width + 2 * EDGE, inner_w), F32),
-                pltpu.VMEM((rows * pos, 9 * inner_w), BF16),
+                pltpu.VMEM((count, hgt, width + 2 * EDGE, ch), F32),
+                pltpu.VMEM((count, hgt + 2, width + 2 * EDGE, inner_w), F32),
+                pltpu.VMEM((count * pos, 9 * inner_w), BF16),
                 pltpu.VMEM((hgt, wide, ch), F32),
             ],
         ),
         compiler_params=params(20),
-        cost_estimate=pl.CostEstimate(flops=2_000_000_000, bytes_accessed=12_000_000, transcendentals=0),
-        name="forward_all_rows",
+        cost_estimate=pl.CostEstimate(
+            flops=600_000_000 * count, bytes_accessed=4_000_000 * count, transcendentals=0
+        ),
+        name="forward_rows",
     )(ends, tissue, *blocks)
 
 
@@ -488,14 +498,11 @@
     part_a = along_x(keep_a, send_a, (inner_pair, outer_pair))
     part_b = along_x(keep_b, send_b, (outer_pair, inner_pair))
     total = jnp.concatenate([part_a, part_b], axis=0).reshape(SEGS, Z * 4, lanes)
-    count = Z * 4 // 2
-    got = swap(total[:, :count], lambda x, z, c: (x, z ^ 1, c))
-    total = total[:, count:] + got.astype(F32)
-    shares = [
-        swap(total[:, 4 * i : 4 * i + 4], lambda x, z, c, b=Z_ORDER[Z // 2 + i]: (x, z ^ b, c))
-        for i in range(Z // 2 - 1)
-    ]
-    return finish(total[:, count - 4 :], shares)
+    for bits in (1, 2):
+        count = total.shape[1] // 2
+        got = swap(total[:, :count], lambda x, z, c, b=bits: (x, z ^ b, c))
+        total = total[:, count:] + got.astype(F32)
+    return finish(total[:, 4:], [swap(total[:, :4], lambda x, z, c: (x, z ^ 6, c))])
 
 
 def finish_kernel(own_ref, *refs):
@@ -549,9 +556,10 @@
     own, *at_hand = inside(x, wr, inner, out_grad, wc, we)
 
     ends = jnp.stack([tile > 0, tile < tiles - 1]).astype(jnp.int32)
-    mz, h2, h1, pad, seed = forward(
-        ends, tissue, lo, hi, own, inner, outer, *at_hand
-    )
+    ahead = (ends, tissue, lo, hi, own, inner, outer, *at_hand)
+    first_row = forward(range(1), (), *ahead)
+    all_rows = forward(range(1, rows), first_row, *ahead)
+    mz, h2, h1, pad, seed = all_rows
     z_now = (tile // CORES) % Z
     xt, pt, ht = turn(x, pad, h2, picks(inner_w, z_now))
 
@@ -567,8 +575,11 @@
         hand_on = slot + LAG < slots
         senders = [s for s in range(1, sections) if 0 <= slot - LAG * (sections - 1 - s) < rows]
         sent = width + 2 * max(senders, default=1)
+        mz_s, h2_s, h1_s, _, seed_s = all_rows if slot else first_row
+        if slot == 0:
+            info = info.at[0].set(0)
         *saved, last = chain_step(
-            info, arriving[slot], seed, mz, h2, h1, at_hand[4], at_hand[3], at_hand[2], inner, outer, hgt, hand_on, sent
+            info, arriving[slot], seed_s, mz_s, h2_s, h1_s, *at_hand[:1:-1], inner, outer, hgt, hand_on, sent
         )
         if hand_on:
             arriving.append(lax.ppermute(last, "section", back_one))

time: 125 us -> 122 us (0.976)
  waiting for transfers between devices: 44.3 us -> 41.8 us
  starting transfers between devices: 37.3 us -> 34.9 us
  Pallas kernels: 38.2 us -> 40.4 us
    pallas_call x1 -> x2, Pallas kernels: 4.52 us -> 6.76 us  [forward(): pl.pallas_call(functools.partial(forward_kernel, some, len(before)), out_...]
    ppermute x8, waiting for transfers between devices: 16.2 us -> 14.4 us  [per_device(): arriving.append(lax.ppermute(last, 'section', back_one))]
    ppermute x8, starting transfers between devices: 19.1 us -> 17.6 us  [per_device(): arriving.append(lax.ppermute(last, 'section', back_one))]
    ppermute x10 -> x9, starting transfers between devices: 8.83 us -> 7.89 us  [swap(): return lax.ppermute(value.astype(BF16), 'tile', tile_pairs(partner))]
    ppermute x10 -> x9, waiting for transfers between devices: 26.5 us -> 25.8 us  [swap(): return lax.ppermute(value.astype(BF16), 'tile', tile_pairs(partner))]
  transfers between devices with their start and end apart: 20 -> 19, of which waited for: 17 -> 16; matrix products, arithmetic and copies ran while one was open for 1% -> 1% of each run, Pallas kernels for 20% -> 23%
where the time goes in v4:
time: 122 us
  waiting for transfers between devices  41.8 us (34%)
  Pallas kernels  40.4 us (33%)
  starting transfers between devices  34.9 us (29%)
  local copies, waits for them, and re-layouts  2.2 us (2%)
  other arithmetic  1.54 us (1%)
    ppermute x9, waiting for transfers between devices, swap(): return lax.ppermute(value.astype(BF16), 'tile', tile_pairs(partner))  25.8 us
    pallas_call x10, Pallas kernels, chain_step(): pl.pallas_call(chain_kernel, out_shape=[jax.ShapeDtypeStruct(s, BF16) for...  21.5 us
    ppermute x8, starting transfers between devices, per_device(): arriving.append(lax.ppermute(last, 'section', back_one))  17.6 us
    ppermute x8, waiting for transfers between devices, per_device(): arriving.append(lax.ppermute(last, 'section', back_one))  14.4 us
    ppermute x9, starting transfers between devices, swap(): return lax.ppermute(value.astype(BF16), 'tile', tile_pairs(partner))  7.89 us
    ppermute x1, starting transfers between devices, neighbours(): high = lax.ppermute(first, 'tile', [(b, a) for a, b in pairs])  7.47 us
    pallas_call x2, Pallas kernels, forward(): pl.pallas_call(functools.partial(forward_kernel, some, len(before)), out_...  6.76 us
    pallas_call x3, Pallas kernels, weight_grads(): pl.pallas_call(functools.partial(weights_kernel, parts, rows, by_row, len...  5.04 us
  transfers between devices with their start and end apart: 19, of which 16 were waited for; matrix products, arithmetic and copies ran while one was open for 1% of the time, Pallas kernels for 23%

profile of v4, /device:TPU:22, one launch (start us, length us, event | category | flops | bytes accessed | tf_op | source)
XLA Modules:
  0.0 121.9 jit_solution(4133882671221496174)
XLA Ops:
  0.7 3.1 %edge_columns.1 = (bf16[4,6,8,1024]{3,2,1,0:T(8,128)(2,1)}, bf16[4,6,8,1024]{3,2,1,0:T(8,128)(2,1)}) custom-call(s32[4,4]{1,0:T(4,128)} %tissue.5, bf16[4,4,32,1024]{3,2,1,0:T(8,128)(2,1)} %bitcast.29, bf16[4,4,32,1024]{3,2,1,0:T(8,128)(2,1)} %bitcast.30, bf16[4,4,32,1024]{3,2,1,0:T(8,128)(2,1)} %og_ref.1, bf16[4,4,32,1024]{3,2,1,0:T(8,128)(2,1)} %og_ref.1), custom_call_target="tpu_custom_call" | custom-call | tf_op jit(solution)/shard_map/edge_columns/pallas_call | solution.py:60
  5.7 7.5 %collective-permute-start.1 = (bf16[4,6,8,1024]{3,2,1,0:T(8,128)(2,1)}, bf16[4,6,8,1024]{3,2,1,0:T(8,128)(2,1)}, u32[]{:S(2)}, u32[]{:S(2)}) collective-permute-start(bf16[4,6,8,1024]{3,2,1,0:T(8,128)(2,1)} %get-tuple-element.97), channel_id=1, source_target_pairs={{4,0},{8,4},{12,8},{16,12},{20,16},{24,20},{28,24},{32,28},{36,32}... | collective-permute-start | bytes 1179656 | tf_op jit(solution)/shard_map/ppermute | solution.py:539
  18.8 2.8 %forward_rows.2 = (bf16[1,160,1024]{2,1,0:T(8,128)(2,1)S(1)}, bf16[1,160,256]{2,1,0:T(8,128)(2,1)S(1)}, bf16[1,160,256]{2,1,0:T(8,128)(2,1)S(1)}, bf16[1,6,48,25...) custom-call(s32[2]{0:T(128)S(1)} %add_convert_fusion.4.ends, s32[4,4]{1,0:T(4,128)S(1)} %copy-done.7, ...), custom_call_target="tpu_custom_call" | custom-call | flops 600000000 | bytes 4000000 | tf_op jit(solution)/shard_map/forward_rows/pallas_call | solution.py:169
  21.6 2.2 %chain_row.10 = (bf16[128,1024]{1,0:T(8,128)(2,1)S(1)}, bf16[128,1024]{1,0:T(8,128)(2,1)S(1)}, bf16[128,256]{1,0:T(8,128)(2,1)S(1)}, bf16[128,256]{1,0:T(8,128)(2,1)S(1)}, bf16[152,1024]{1,0:T(8,128)(2,1)S(1)}) custom-call(s32[2]{0:T(128)S(1)} %constant_dynamic-update-slice_fusion.info, bf16[136,1024]{1,0:T(8,128)(2,1)S(1)} %broadcast_in_dim.12.gy_ref, ...), custom_call_target="tpu_custom_call" | custom-call | flops 3600000000 | bytes 50000000 | tf_op jit(solution)/shard_map/chain_row/pallas_call | solution.py:253
  23.7 2.4 %collective-permute-start.2 = (bf16[152,1024]{1,0:T(8,128)(2,1)S(1)}, bf16[152,1024]{1,0:T(8,128)(2,1)S(1)}, u32[]{:S(2)}, u32[]{:S(2)}) collective-permute-start(bf16[152,1024]{1,0:T(8,128)(2,1)S(1)} %get-tuple-element.115), channel_id=1, source_target_pairs={{1,0},{2,1},{3,2},{5,4},{6,5},{7,6},{9,8},{10,9},{11,10},{13,12},{... | collective-permute-start | bytes 933896 | tf_op jit(solution)/shard_map/ppermute | solution.py:585
  26.1 4.0 %forward_rows.3 = (bf16[4,160,1024]{2,1,0:T(8,128)(2,1)S(1)}, bf16[4,160,256]{2,1,0:T(8,128)(2,1)S(1)}, bf16[4,160,256]{2,1,0:T(8,128)(2,1)S(1)}, bf16[4,6,48,25...) custom-call(s32[2]{0:T(128)S(1)} %add_convert_fusion.4.ends, s32[4,4]{1,0:T(4,128)S(1)} %copy-done.7, ...), custom_call_target="tpu_custom_call" | custom-call | flops 1800000000 | bytes 12000000 | tf_op jit(solution)/shard_map/forward_rows/pallas_call | solution.py:169
  30.1 2.2 %chain_row.11 = (bf16[128,1024]{1,0:T(8,128)(2,1)S(1)}, bf16[128,1024]{1,0:T(8,128)(2,1)S(1)}, bf16[128,256]{1,0:T(8,128)(2,1)S(1)}, bf16[128,256]{1,0:T(8,128)(2,1)S(1)}, bf16[152,1024]{1,0:T(8,128)(2,1)S(1)}) custom-call(s32[2]{0:T(128)S(1)} %get-tuple-element.179.info, bf16[136,1024]{1,0:T(8,128)(2,1)S(1)} %broadcast_in_dim.12.gy_ref, ...), custom_call_target="tpu_custom_call" | custom-call | flops 3600000000 | bytes 50000000 | tf_op jit(solution)/shard_map/chain_row/pallas_call | solution.py:253
  32.3 2.4 %collective-permute-start.3 = (bf16[152,1024]{1,0:T(8,128)(2,1)S(1)}, bf16[152,1024]{1,0:T(8,128)(2,1)S(1)}, u32[]{:S(2)}, u32[]{:S(2)}) collective-permute-start(bf16[152,1024]{1,0:T(8,128)(2,1)S(1)} %get-tuple-element.117), channel_id=1, source_target_pairs={{1,0},{2,1},{3,2},{5,4},{6,5},{7,6},{9,8},{10,9},{11,10},{13,12},{... | collective-permute-start | bytes 933896 | tf_op jit(solution)/shard_map/ppermute | solution.py:585
  35.8 2.2 %chain_row.12 = (bf16[128,1024]{1,0:T(8,128)(2,1)S(1)}, bf16[128,1024]{1,0:T(8,128)(2,1)S(1)}, bf16[128,256]{1,0:T(8,128)(2,1)S(1)}, bf16[128,256]{1,0:T(8,128)(2,1)S(1)}, bf16[152,1024]{1,0:T(8,128)(2,1)S(1)}) custom-call(s32[2]{0:T(128)S(1)} %pad_add_fusion.4.info, bf16[152,1024]{1,0:T(8,128)(2,1)S(1)} %collective-permute-done.2.gy_ref, ...), custom_call_target="tpu_custom_call" | custom-call | flops 3600000000 | bytes 50000000 | tf_op jit(solution)/shard_map/chain_row/pallas_call | solution.py:253
  39.9 2.8 %collective-permute-done.3.gy_ref = bf16[152,1024]{1,0:T(8,128)(2,1)S(1)} collective-permute-done((bf16[152,1024]{1,0:T(8,128)(2,1)S(1)}, bf16[152,1024]{1,0:T(8,128)(2,1)S(1)}, u32[]{:S(2)}, u32[]{:S(2)}) %collective-permute-start.3) | collective-permute-done | bytes 311328 | tf_op jit(solution)/shard_map/ppermute | solution.py:585
  42.7 2.2 %chain_row.13 = (bf16[128,1024]{1,0:T(8,128)(2,1)S(1)}, bf16[128,1024]{1,0:T(8,128)(2,1)S(1)}, bf16[128,256]{1,0:T(8,128)(2,1)S(1)}, bf16[128,256]{1,0:T(8,128)(2,1)S(1)}, bf16[152,1024]{1,0:T(8,128)(2,1)S(1)}) custom-call(s32[2]{0:T(128)S(1)} %pad_add_fusion.5.info, bf16[152,1024]{1,0:T(8,128)(2,1)S(1)} %collective-permute-done.3.gy_ref, ...), custom_call_target="tpu_custom_call" | custom-call | flops 3600000000 | bytes 50000000 | tf_op jit(solution)/shard_map/chain_row/pallas_call | solution.py:253
  44.8 2.5 %collective-permute-start.5 = (bf16[152,1024]{1,0:T(8,128)(2,1)S(1)}, bf16[152,1024]{1,0:T(8,128)(2,1)S(1)}, u32[]{:S(2)}, u32[]{:S(2)}) collective-permute-start(bf16[152,1024]{1,0:T(8,128)(2,1)S(1)} %get-tuple-element.121), channel_id=1, source_target_pairs={{1,0},{2,1},{3,2},{5,4},{6,5},{7,6},{9,8},{10,9},{11,10},{13,12},{... | collective-permute-start | bytes 933896 | tf_op jit(solution)/shard_map/ppermute | solution.py:585
  47.3 2.8 %collective-permute-done.4.gy_ref = bf16[152,1024]{1,0:T(8,128)(2,1)S(1)} collective-permute-done((bf16[152,1024]{1,0:T(8,128)(2,1)S(1)}, bf16[152,1024]{1,0:T(8,128)(2,1)S(1)}, u32[]{:S(2)}, u32[]{:S(2)}) %collective-permute-start.4) | collective-permute-done | bytes 311328 | tf_op jit(solution)/shard_map/ppermute | solution.py:585
  50.2 2.2 %chain_row.14 = (bf16[128,1024]{1,0:T(8,128)(2,1)S(1)}, bf16[128,1024]{1,0:T(8,128)(2,1)S(1)}, bf16[128,256]{1,0:T(8,128)(2,1)S(1)}, bf16[128,256]{1,0:T(8,128)(2,1)S(1)}, bf16[144,1024]{1,0:T(8,128)(2,1)S(1)}) custom-call(s32[2]{0:T(128)S(1)} %pad_add_fusion.6.info, bf16[152,1024]{1,0:T(8,128)(2,1)S(1)} %collective-permute-done.4.gy_ref, ...), custom_call_target="tpu_custom_call" | custom-call | flops 3600000000 | bytes 50000000 | tf_op jit(solution)/shard_map/chain_row/pallas_call | solution.py:253
  52.3 2.1 %collective-permute-start.6 = (bf16[144,1024]{1,0:T(8,128)(2,1)S(1)}, bf16[144,1024]{1,0:T(8,128)(2,1)S(1)}, u32[]{:S(2)}, u32[]{:S(2)}) collective-permute-start(bf16[144,1024]{1,0:T(8,128)(2,1)S(1)} %get-tuple-element.123), channel_id=1, source_target_pairs={{1,0},{2,1},{3,2},{5,4},{6,5},{7,6},{9,8},{10,9},{11,10},{13,12},{... | collective-permute-start | bytes 884744 | tf_op jit(solution)/shard_map/ppermute | solution.py:585
  54.4 2.2 %collective-permute-done.5.gy_ref = bf16[152,1024]{1,0:T(8,128)(2,1)S(1)} collective-permute-done((bf16[152,1024]{1,0:T(8,128)(2,1)S(1)}, bf16[152,1024]{1,0:T(8,128)(2,1)S(1)}, u32[]{:S(2)}, u32[]{:S(2)}) %collective-permute-start.5) | collective-permute-done | bytes 311328 | tf_op jit(solution)/shard_map/ppermute | solution.py:585
  56.7 2.2 %chain_row.15 = (bf16[128,1024]{1,0:T(8,128)(2,1)S(1)}, bf16[128,1024]{1,0:T(8,128)(2,1)S(1)}, bf16[128,256]{1,0:T(8,128)(2,1)S(1)}, bf16[128,256]{1,0:T(8,128)(2,1)S(1)}, bf16[144,1024]{1,0:T(8,128)(2,1)S(1)}) custom-call(s32[2]{0:T(128)S(1)} %pad_add_fusion.7.info, bf16[152,1024]{1,0:T(8,128)(2,1)S(1)} %collective-permute-done.5.gy_ref, ...), custom_call_target="tpu_custom_call" | custom-call | flops 3600000000 | bytes 50000000 | tf_op jit(solution)/shard_map/chain_row/pallas_call | solution.py:253
  62.8 2.2 %chain_row.16 = (bf16[128,1024]{1,0:T(8,128)(2,1)S(1)}, bf16[128,1024]{1,0:T(8,128)(2,1)S(1)}, bf16[128,256]{1,0:T(8,128)(2,1)S(1)}, bf16[128,256]{1,0:T(8,128)(2,1)S(1)}, bf16[136,1024]{1,0:T(8,128)(2,1)S(1)}) custom-call(s32[2]{0:T(128)S(1)} %pad_add_fusion.8.info, bf16[144,1024]{1,0:T(8,128)(2,1)S(1)} %collective-permute-done.6.gy_ref, ...), custom_call_target="tpu_custom_call" | custom-call | flops 3600000000 | bytes 50000000 | tf_op jit(solution)/shard_map/chain_row/pallas_call | solution.py:253
  65.0 2.5 %collective-permute-start.8 = (bf16[136,1024]{1,0:T(8,128)(2,1)S(1)}, bf16[136,1024]{1,0:T(8,128)(2,1)S(1)}, u32[]{:S(2)}, u32[]{:S(2)}) collective-permute-start(bf16[136,1024]{1,0:T(8,128)(2,1)S(1)} %get-tuple-element.127), channel_id=1, source_target_pairs={{1,0},{2,1},{3,2},{5,4},{6,5},{7,6},{9,8},{10,9},{11,10},{13,12},{... | collective-permute-start | bytes 835592 | tf_op jit(solution)/shard_map/ppermute | solution.py:585
  67.5 2.6 %collective-permute-done.7.gy_ref = bf16[144,1024]{1,0:T(8,128)(2,1)S(1)} collective-permute-done((bf16[144,1024]{1,0:T(8,128)(2,1)S(1)}, bf16[144,1024]{1,0:T(8,128)(2,1)S(1)}, u32[]{:S(2)}, u32[]{:S(2)}) %collective-permute-start.7) | collective-permute-done | bytes 294944 | tf_op jit(solution)/shard_map/ppermute | solution.py:585
  70.1 2.2 %chain_row.17 = (bf16[128,1024]{1,0:T(8,128)(2,1)S(1)}, bf16[128,1024]{1,0:T(8,128)(2,1)S(1)}, bf16[128,256]{1,0:T(8,128)(2,1)S(1)}, bf16[128,256]{1,0:T(8,128)(2,1)S(1)}, bf16[136,1024]{1,0:T(8,128)(2,1)S(1)}) custom-call(s32[2]{0:T(128)S(1)} %pad_add_fusion.9.info, bf16[144,1024]{1,0:T(8,128)(2,1)S(1)} %collective-permute-done.7.gy_ref, ...), custom_call_target="tpu_custom_call" | custom-call | flops 3600000000 | bytes 50000000 | tf_op jit(solution)/shard_map/chain_row/pallas_call | solution.py:253
  76.1 2.1 %chain_row.18 = (bf16[128,1024]{1,0:T(8,128)(2,1)S(1)}, bf16[128,1024]{1,0:T(8,128)(2,1)S(1)}, bf16[128,256]{1,0:T(8,128)(2,1)S(1)}, bf16[128,256]{1,0:T(8,128)(2,1)S(1)}) custom-call(s32[2]{0:T(128)S(1)} %pad_add_fusion.10.info, bf16[136,1024]{1,0:T(8,128)(2,1)S(1)} %collective-permute-done.8.gy_ref, bf16[4,160,1024]{2,1,0:T(8,128)(2,1)S(1)} %get-tuple-element.110.seed_ref, ...), custom_call_target="tpu_custom_call" | custom-call | flops 3600000000 | bytes 50000000 | tf_op jit(solution)/shard_map/chain_row/pallas_call | solution.py:253
  78.2 2.7 %weight_gradients_early.1 = (bf16[1024,256]{1,0:T(8,128)(2,1)S(1)}, bf16[1024,256]{1,0:T(8,128)(2,1)S(1)}, bf16[1152,256]{1,0:T(8,128)(2,1)S(1)}, bf16[1152,256]{1,0:T(8,128)(2,1)S(1)}) custom-call(s32[3]{0:T(128)S(1)} %pad_add_fusion.1.info, bf16[1024,512]{1,0:T(8,128)(2,1)S(1)} %get-tuple-element.132.refs_0_, ...), custom_call_target="tpu_custom_call" | custom-call | flops 900000000 | bytes 6000000 | tf_op jit(solution)/shard_map/weight_gradients_early/pallas_call | solution.py:415
  80.9 2.1 %chain_row.19 = (bf16[128,1024]{1,0:T(8,128)(2,1)S(1)}, bf16[128,1024]{1,0:T(8,128)(2,1)S(1)}, bf16[128,256]{1,0:T(8,128)(2,1)S(1)}, bf16[128,256]{1,0:T(8,128)(2,1)S(1)}) custom-call(s32[2]{0:T(128)S(1)} %pad_add_fusion.11.info, bf16[136,1024]{1,0:T(8,128)(2,1)S(1)} %collective-permute-done.9.gy_ref, bf16[4,160,1024]{2,1,0:T(8,128)(2,1)S(1)} %get-tuple-element.110.seed_ref, ...), custom_call_target="tpu_custom_call" | custom-call | flops 3600000000 | bytes 50000000 | tf_op jit(solution)/shard_map/chain_row/pallas_call | solution.py:253
  88.1 6.7 %collective-permute-done.11 = bf16[512,256]{1,0:T(8,128)(2,1)S(1)} collective-permute-done((bf16[512,256]{1,0:T(8,128)(2,1)S(1)}, bf16[512,256]{1,0:T(8,128)(2,1)S(1)}, u32[]{:S(2)}, u32[]{:S(2)}) %collective-permute-start.11) | collective-permute-done | bytes 262176 | tf_op jit(solution)/shard_map/ppermute | solution.py:480
  94.9 3.8 %collective-permute-done.14 = bf16[576,256]{1,0:T(8,128)(2,1)S(1)} collective-permute-done((bf16[576,256]{1,0:T(8,128)(2,1)S(1)}, bf16[576,256]{1,0:T(8,128)(2,1)S(1)}, u32[]{:S(2)}, u32[]{:S(2)}) %collective-permute-start.14) | collective-permute-done | bytes 294944 | tf_op jit(solution)/shard_map/ppermute | solution.py:480
  98.9 2.3 %collective-permute-done.12 = bf16[256,256]{1,0:T(8,128)(2,1)S(1)} collective-permute-done((bf16[256,256]{1,0:T(8,128)(2,1)S(1)}, bf16[256,256]{1,0:T(8,128)(2,1)S(1)}, u32[]{:S(2)}, u32[]{:S(2)}) %collective-permute-start.12) | collective-permute-done | bytes 131104 | tf_op jit(solution)/shard_map/ppermute | solution.py:480
  101.3 2.7 %collective-permute-done.15 = bf16[288,256]{1,0:T(8,128)(2,1)S(1)} collective-permute-done((bf16[288,256]{1,0:T(8,128)(2,1)S(1)}, bf16[288,256]{1,0:T(8,128)(2,1)S(1)}, u32[]{:S(2)}, u32[]{:S(2)}) %collective-permute-start.15) | collective-permute-done | bytes 147488 | tf_op jit(solution)/shard_map/ppermute | solution.py:480
  104.5 4.8 %collective-permute-done.16 = bf16[17,16,256]{2,1,0:T(8,128)(2,1)S(1)} collective-permute-done((bf16[17,16,256]{2,1,0:T(8,128)(2,1)S(1)}, bf16[17,16,256]{2,1,0:T(8,128)(2,1)S(1)}, u32[]{:S(2)}, u32[]{:S(2)}) %collective-permute-start.16) | collective-permute-done | bytes 139296 | tf_op jit(solution)/shard_map/ppermute | solution.py:480
  109.4 2.5 %collective-permute-start.17 = (bf16[17,8,256]{2,1,0:T(8,128)(2,1)S(1)}, bf16[17,8,256]{2,1,0:T(8,128)(2,1)S(1)}, u32[]{:S(2)}, u32[]{:S(2)}) collective-permute-start(bf16[17,8,256]{2,1,0:T(8,128)(2,1)S(1)} %slice.148), channel_id=1, source_target_pairs={{0,16},{4,20},{8,24},{12,28},{16,0},{20,4},{24,8},{28,12},{32,48},... | collective-permute-start | bytes 208904 | tf_op jit(solution)/shard_map/ppermute | solution.py:480
  111.8 3.3 %collective-permute-done.17 = bf16[17,8,256]{2,1,0:T(8,128)(2,1)S(1)} collective-permute-done((bf16[17,8,256]{2,1,0:T(8,128)(2,1)S(1)}, bf16[17,8,256]{2,1,0:T(8,128)(2,1)S(1)}, u32[]{:S(2)}, u32[]{:S(2)}) %collective-permute-start.17) | collective-permute-done | bytes 69664 | tf_op jit(solution)/shard_map/ppermute | solution.py:480
  115.2 3.6 %collective-permute-start.18 = (bf16[17,4,256]{2,1,0:T(4,128)(2,1)S(1)}, bf16[17,4,256]{2,1,0:T(4,128)(2,1)S(1)}, u32[]{:S(2)}, u32[]{:S(2)}) collective-permute-start(bf16[17,4,256]{2,1,0:T(4,128)(2,1)S(1)} %slice.149), channel_id=1, source_target_pairs={{0,48},{4,52},{8,56},{12,60},{16,32},{20,36},{24,40},{28,44},{32,1... | collective-permute-start | bytes 104456 | tf_op jit(solution)/shard_map/ppermute | solution.py:480
  (74 shorter events, 27.3 us)
Async XLA Ops:
  0.6 13.6 %copy-start = (bf16[4,4,32,1024]{3,2,1,0:T(8,128)(2,1)S(1)}, bf16[4,4,32,1024]{3,2,1,0:T(8,128)(2,1)}, u32[]{:S(2)}) copy-start(bf16[4,4,32,1024]{3,2,1,0:T(8,128)(2,1)} %og_ref.1) | copy-start | bytes 3145732
  0.6 13.6 %copy-start.1 = (bf16[1,4,4,32,1024]{4,3,2,1,0:T(8,128)(2,1)S(1)}, bf16[1,4,4,32,1024]{4,3,2,1,0:T(8,128)(2,1)}, u32[]{:S(2)}) copy-start(bf16[1,4,4,32,1024]{4,3,2,1,0:T(8,128)(2,1)} %param.11) | copy-start | bytes 3145732
  0.7 13.6 %copy-start.2 = (bf16[1,3,3,256,256]{4,3,2,1,0:T(8,128)(2,1)S(1)}, bf16[1,3,3,256,256]{4,3,2,1,0:T(8,128)(2,1)}, u32[]{:S(2)}) copy-start(bf16[1,3,3,256,256]{4,3,2,1,0:T(8,128)(2,1)} %param.15) | copy-start | bytes 3538948
  0.7 13.6 %copy-start.5 = (f32[1,4,256]{2,1,0:T(4,128)S(1)}, f32[1,4,256]{2,1,0:T(4,128)}, u32[]{:S(2)}) copy-start(f32[1,4,256]{2,1,0:T(4,128)} %param.17) | copy-start | bytes 12292
  3.8 13.4 %collective-permute-start = (bf16[4,6,8,1024]{3,2,1,0:T(8,128)(2,1)}, bf16[4,6,8,1024]{3,2,1,0:T(8,128)(2,1)}, u32[]{:S(2)}, u32[]{:S(2)}) collective-permute-start(bf16[4,6,8,1024]{3,2,1,0:T(8,128)(2,1)} %get-tuple-element.96), channel_id=1, source_target_pairs={{0,4},{4,8},{8,12},{12,16},{16,20},{20,24},{24,28},{28,32},{32,36}... | collective-permute-start | bytes 1179656 | tf_op jit(solution)/shard_map/ppermute | solution.py:538
  5.7 13.1 %collective-permute-start.1 = (bf16[4,6,8,1024]{3,2,1,0:T(8,128)(2,1)}, bf16[4,6,8,1024]{3,2,1,0:T(8,128)(2,1)}, u32[]{:S(2)}, u32[]{:S(2)}) collective-permute-start(bf16[4,6,8,1024]{3,2,1,0:T(8,128)(2,1)} %get-tuple-element.97), channel_id=1, source_target_pairs={{4,0},{8,4},{12,8},{16,12},{20,16},{24,20},{28,24},{32,28},{36,32}... | collective-permute-start | bytes 1179656 | tf_op jit(solution)/shard_map/ppermute | solution.py:539
  14.2 1.0 copy-start.3
  15.3 1.0 copy-start.4
  16.3 2.4 %copy-start.6 = (f32[1,2,1024]{2,1,0:T(2,128)S(1)}, f32[1,2,1024]{2,1,0:T(2,128)}, u32[]{:S(2)}) copy-start(f32[1,2,1024]{2,1,0:T(2,128)} %param.18) | copy-start | bytes 24580
  16.3 2.4 %copy-start.7 = (s32[4,4]{1,0:T(4,128)S(1)}, s32[4,4]{1,0:T(4,128)}, u32[]{:S(2)}) copy-start(s32[4,4]{1,0:T(4,128)} %tissue.5) | copy-start | bytes 196
  23.7 12.0 %collective-permute-start.2 = (bf16[152,1024]{1,0:T(8,128)(2,1)S(1)}, bf16[152,1024]{1,0:T(8,128)(2,1)S(1)}, u32[]{:S(2)}, u32[]{:S(2)}) collective-permute-start(bf16[152,1024]{1,0:T(8,128)(2,1)S(1)} %get-tuple-element.115), channel_id=1, source_target_pairs={{1,0},{2,1},{3,2},{5,4},{6,5},{7,6},{9,8},{10,9},{11,10},{13,12},{... | collective-permute-start | bytes 933896 | tf_op jit(solution)/shard_map/ppermute | solution.py:585
  32.3 10.4 %collective-permute-start.3 = (bf16[152,1024]{1,0:T(8,128)(2,1)S(1)}, bf16[152,1024]{1,0:T(8,128)(2,1)S(1)}, u32[]{:S(2)}, u32[]{:S(2)}) collective-permute-start(bf16[152,1024]{1,0:T(8,128)(2,1)S(1)} %get-tuple-element.117), channel_id=1, source_target_pairs={{1,0},{2,1},{3,2},{5,4},{6,5},{7,6},{9,8},{10,9},{11,10},{13,12},{... | collective-permute-start | bytes 933896 | tf_op jit(solution)/shard_map/ppermute | solution.py:585
  38.0 12.2 %collective-permute-start.4 = (bf16[152,1024]{1,0:T(8,128)(2,1)S(1)}, bf16[152,1024]{1,0:T(8,128)(2,1)S(1)}, u32[]{:S(2)}, u32[]{:S(2)}) collective-permute-start(bf16[152,1024]{1,0:T(8,128)(2,1)S(1)} %get-tuple-element.119), channel_id=1, source_target_pairs={{1,0},{2,1},{3,2},{5,4},{6,5},{7,6},{9,8},{10,9},{11,10},{13,12},{... | collective-permute-start | bytes 933896 | tf_op jit(solution)/shard_map/ppermute | solution.py:585
  44.8 11.8 %collective-permute-start.5 = (bf16[152,1024]{1,0:T(8,128)(2,1)S(1)}, bf16[152,1024]{1,0:T(8,128)(2,1)S(1)}, u32[]{:S(2)}, u32[]{:S(2)}) collective-permute-start(bf16[152,1024]{1,0:T(8,128)(2,1)S(1)} %get-tuple-element.121), channel_id=1, source_target_pairs={{1,0},{2,1},{3,2},{5,4},{6,5},{7,6},{9,8},{10,9},{11,10},{13,12},{... | collective-permute-start | bytes 933896 | tf_op jit(solution)/shard_map/ppermute | solution.py:585
  52.3 10.5 %collective-permute-start.6 = (bf16[144,1024]{1,0:T(8,128)(2,1)S(1)}, bf16[144,1024]{1,0:T(8,128)(2,1)S(1)}, u32[]{:S(2)}, u32[]{:S(2)}) collective-permute-start(bf16[144,1024]{1,0:T(8,128)(2,1)S(1)} %get-tuple-element.123), channel_id=1, source_target_pairs={{1,0},{2,1},{3,2},{5,4},{6,5},{7,6},{9,8},{10,9},{11,10},{13,12},{... | collective-permute-start | bytes 884744 | tf_op jit(solution)/shard_map/ppermute | solution.py:585
  58.8 11.3 %collective-permute-start.7 = (bf16[144,1024]{1,0:T(8,128)(2,1)S(1)}, bf16[144,1024]{1,0:T(8,128)(2,1)S(1)}, u32[]{:S(2)}, u32[]{:S(2)}) collective-permute-start(bf16[144,1024]{1,0:T(8,128)(2,1)S(1)} %get-tuple-element.125), channel_id=1, source_target_pairs={{1,0},{2,1},{3,2},{5,4},{6,5},{7,6},{9,8},{10,9},{11,10},{13,12},{... | collective-permute-start | bytes 884744 | tf_op jit(solution)/shard_map/ppermute | solution.py:585
  65.0 11.1 %collective-permute-start.8 = (bf16[136,1024]{1,0:T(8,128)(2,1)S(1)}, bf16[136,1024]{1,0:T(8,128)(2,1)S(1)}, u32[]{:S(2)}, u32[]{:S(2)}) collective-permute-start(bf16[136,1024]{1,0:T(8,128)(2,1)S(1)} %get-tuple-element.127), channel_id=1, source_target_pairs={{1,0},{2,1},{3,2},{5,4},{6,5},{7,6},{9,8},{10,9},{11,10},{13,12},{... | collective-permute-start | bytes 835592 | tf_op jit(solution)/shard_map/ppermute | solution.py:585
  72.3 8.7 %collective-permute-start.9 = (bf16[136,1024]{1,0:T(8,128)(2,1)S(1)}, bf16[136,1024]{1,0:T(8,128)(2,1)S(1)}, u32[]{:S(2)}, u32[]{:S(2)}) collective-permute-start(bf16[136,1024]{1,0:T(8,128)(2,1)S(1)} %get-tuple-element.129), channel_id=1, source_target_pairs={{1,0},{2,1},{3,2},{5,4},{6,5},{7,6},{9,8},{10,9},{11,10},{13,12},{... | collective-permute-start | bytes 835592 | tf_op jit(solution)/shard_map/ppermute | solution.py:585
  84.3 2.0 %collective-permute-start.10 = (bf16[1024,256]{1,0:T(8,128)(2,1)S(1)}, bf16[1024,256]{1,0:T(8,128)(2,1)S(1)}, u32[]{:S(2)}, u32[]{:S(2)}) collective-permute-start(bf16[1024,256]{1,0:T(8,128)(2,1)S(1)} %get-tuple-element.167), channel_id=1, source_target_pairs={{0,4},{4,0},{8,12},{12,8},{16,20},{20,16},{24,28},{28,24},{32,36},... | collective-permute-start | bytes 1572872 | tf_op jit(solution)/shard_map/ppermute | solution.py:480
  85.5 2.2 %collective-permute-start.13 = (bf16[1152,256]{1,0:T(8,128)(2,1)S(1)}, bf16[1152,256]{1,0:T(8,128)(2,1)S(1)}, u32[]{:S(2)}, u32[]{:S(2)}) collective-permute-start(bf16[1152,256]{1,0:T(8,128)(2,1)S(1)} %get-tuple-element.172), channel_id=1, source_target_pairs={{0,4},{4,0},{8,12},{12,8},{16,20},{20,16},{24,28},{28,24},{32,36},... | collective-permute-start | bytes 1769480 | tf_op jit(solution)/shard_map/ppermute | solution.py:480
  86.3 8.4 %collective-permute-start.11 = (bf16[512,256]{1,0:T(8,128)(2,1)S(1)}, bf16[512,256]{1,0:T(8,128)(2,1)S(1)}, u32[]{:S(2)}, u32[]{:S(2)}) collective-permute-start(bf16[512,256]{1,0:T(8,128)(2,1)S(1)} %add_convert_fusion.1), channel_id=1, source_target_pairs={{0,64},{4,68},{8,72},{12,76},{16,80},{20,84},{24,88},{28,92},{32,9... | collective-permute-start | bytes 786440 | tf_op jit(solution)/shard_map/ppermute | solution.py:480
  87.8 10.9 %collective-permute-start.14 = (bf16[576,256]{1,0:T(8,128)(2,1)S(1)}, bf16[576,256]{1,0:T(8,128)(2,1)S(1)}, u32[]{:S(2)}, u32[]{:S(2)}) collective-permute-start(bf16[576,256]{1,0:T(8,128)(2,1)S(1)} %add_convert_fusion), channel_id=1, source_target_pairs={{0,192},{4,196},{8,200},{12,204},{16,208},{20,212},{24,216},{28,22... | collective-permute-start | bytes 884744 | tf_op jit(solution)/shard_map/ppermute | solution.py:480
  94.8 6.4 %collective-permute-start.12 = (bf16[256,256]{1,0:T(8,128)(2,1)S(1)}, bf16[256,256]{1,0:T(8,128)(2,1)S(1)}, u32[]{:S(2)}, u32[]{:S(2)}) collective-permute-start(bf16[256,256]{1,0:T(8,128)(2,1)S(1)} %add_convert_fusion.3), channel_id=1, source_target_pairs={{0,192},{4,196},{8,200},{12,204},{16,208},{20,212},{24,216},{28,22... | collective-permute-start | bytes 393224 | tf_op jit(solution)/shard_map/ppermute | solution.py:480
  98.8 5.2 %collective-permute-start.15 = (bf16[288,256]{1,0:T(8,128)(2,1)S(1)}, bf16[288,256]{1,0:T(8,128)(2,1)S(1)}, u32[]{:S(2)}, u32[]{:S(2)}) collective-permute-start(bf16[288,256]{1,0:T(8,128)(2,1)S(1)} %add_convert_fusion.2), channel_id=1, source_target_pairs={{0,64},{4,68},{8,72},{12,76},{16,80},{20,84},{24,88},{28,92},{32,9... | collective-permute-start | bytes 442376 | tf_op jit(solution)/shard_map/ppermute | solution.py:480
  104.2 5.1 %collective-permute-start.16 = (bf16[17,16,256]{2,1,0:T(8,128)(2,1)S(1)}, bf16[17,16,256]{2,1,0:T(8,128)(2,1)S(1)}, u32[]{:S(2)}, u32[]{:S(2)}) collective-permute-start(bf16[17,16,256]{2,1,0:T(8,128)(2,1)S(1)} %slice.147), channel_id=1, source_target_pairs={{0,8},{4,12},{8,0},{12,4},{16,24},{20,28},{24,16},{28,20},{32,40},... | collective-permute-start | bytes 417800 | tf_op jit(solution)/shard_map/ppermute | solution.py:480
  109.4 5.7 %collective-permute-start.17 = (bf16[17,8,256]{2,1,0:T(8,128)(2,1)S(1)}, bf16[17,8,256]{2,1,0:T(8,128)(2,1)S(1)}, u32[]{:S(2)}, u32[]{:S(2)}) collective-permute-start(bf16[17,8,256]{2,1,0:T(8,128)(2,1)S(1)} %slice.148), channel_id=1, source_target_pairs={{0,16},{4,20},{8,24},{12,28},{16,0},{20,4},{24,8},{28,12},{32,48},... | collective-permute-start | bytes 208904 | tf_op jit(solution)/shard_map/ppermute | solution.py:480
  115.2 6.1 %collective-permute-start.18 = (bf16[17,4,256]{2,1,0:T(4,128)(2,1)S(1)}, bf16[17,4,256]{2,1,0:T(4,128)(2,1)S(1)}, u32[]{:S(2)}, u32[]{:S(2)}) collective-permute-start(bf16[17,4,256]{2,1,0:T(4,128)(2,1)S(1)} %slice.149), channel_id=1, source_target_pairs={{0,48},{4,52},{8,56},{12,60},{16,32},{20,36},{24,40},{28,44},{32,1... | collective-permute-start | bytes 104456 | tf_op jit(solution)/shard_map/ppermute | solution.py:480

commit v5 on v4

--- a/solution.py
+++ b/solution.py
@@ -34,41 +34,52 @@
     return pl.BlockSpec(shape, lambda *_: (0,) * len(shape), pipeline_mode=pl.Buffered(1))
 
 
-def edges_kernel(tissue, x0_ref, x1_ref, og0_ref, og1_ref, first_ref, last_ref):
-    rows, hgt = x0_ref.shape[:2]
-    for x_ref, og_ref, out, tile, at in (
-        (x0_ref, og0_ref, first_ref, 0, 0),
-        (x1_ref, og1_ref, last_ref, tissue.shape[1] - 1, EDGE - RIM),
-    ):
-        out[:, :hgt] = x_ref[...]
+def edges_kernel(tissue, x_ref, og_ref, first_ref, last_ref, og_s, seed_s, sems):
+    rows, hgt, width, ch = x_ref.shape
+    sides = (
+        (first_ref, 0, 0, 0),
+        (last_ref, width - EDGE, tissue.shape[1] - 1, EDGE - RIM),
+    )
+    plain, fetched, handed = [], [], []
+    for n, (out, start, _, _) in enumerate(sides):
+        cols = pl.ds(start, EDGE)
+        fetched.append(pltpu.make_async_copy(og_ref.at[:, :, cols], og_s.at[n], sems.at[n]))
+        plain.append(pltpu.make_async_copy(x_ref.at[:, :, cols], out.at[:, pl.ds(0, hgt)], sems.at[2 + n]))
+        handed.append(pltpu.make_async_copy(seed_s.at[n], out.at[:, pl.ds(hgt, hgt // 2)], sems.at[4 + n]))
+    for copy in fetched + plain:
+        copy.start()
+    for n, (_, _, tile, at) in enumerate(sides):
+        fetched[n].wait()
         for r in range(rows):
-            seed = og_ref[r].astype(F32)[:, at : at + RIM] * tissue[r, tile].astype(F32)
+            seed = og_s[n, r].astype(F32)[:, at : at + RIM] * tissue[r, tile].astype(F32)
             for pair in range(hgt // 2):
                 both = jnp.concatenate([seed[2 * pair], seed[2 * pair + 1]], axis=0)
-                out[r, hgt + pair] = both.astype(BF16)
+                seed_s[n, r, pair] = both.astype(BF16)
+        handed[n].start()
+    for copy in plain + handed:
+        copy.wait()
 
 
 def edges(tissue, x, og):
     rows, hgt, width, ch = x.shape
-    part = (rows, hgt, EDGE, ch)
     out = (rows, hgt + hgt // 2, EDGE, ch)
-    end = width // EDGE - 1
-
-    def at(block):
-        return pl.BlockSpec(part, lambda i, tissue: (0, 0, block, 0))
-
     return pl.pallas_call(
         edges_kernel,
         out_shape=[jax.ShapeDtypeStruct(out, BF16)] * 2,
         grid_spec=pltpu.PrefetchScalarGridSpec(
             num_scalar_prefetch=1,
             grid=(1,),
-            in_specs=[at(0), at(end), at(0), at(end)],
-            out_specs=[full(out)] * 2,
+            in_specs=[pl.BlockSpec(memory_space=pl.ANY)] * 2,
+            out_specs=[pl.BlockSpec(memory_space=pl.ANY)] * 2,
+            scratch_shapes=[
+                pltpu.VMEM((2, rows, hgt, EDGE, ch), BF16),
+                pltpu.VMEM((2, rows, hgt // 2, EDGE, ch), BF16),
+                pltpu.SemaphoreType.DMA((6,)),
+            ],
         ),
         compiler_params=params(60),
         name="edge_columns",
-    )(tissue, x, x, og, og)
+    )(tissue, x, og)
 
 
 def hidden_one(part, wr, inner_ref):
@@ -172,7 +183,7 @@
         grid_spec=pltpu.PrefetchScalarGridSpec(
             num_scalar_prefetch=2,
             grid=(1,),
-            in_specs=[full(a.shape) for a in blocks],
+            in_specs=[full((some[-1] + 1,) + a.shape[1:]) for a in blocks[:2]] + [full(a.shape) for a in blocks[2:]],
             out_specs=[full(s) for s in out_shapes],
             scratch_shapes=[
                 pltpu.VMEM((count, hgt, width + 2 * EDGE, ch), F32),
@@ -191,8 +202,9 @@
 
 def chain_kernel(
     info, gy_ref, seed_ref, mz_ref, h2_ref, h1_ref, we_ref, wc_ref, wr_ref, inner_ref, outer_ref,
-    gi_ref, g3_ref, g2_ref, g1_ref, *more,
+    g3_ref, g2_ref, g1_ref, *more, with_gi,
 ):
+    gi_ref, more = (more[0], more[1:]) if with_gi else (None, more)
     *wire_ref, wide_s, pad_s, flat_s = more
     inner_w = we_ref.shape[0]
     hgt, wide, ch = wide_s.shape
@@ -229,6 +241,8 @@
         back = back + dot_t(piece.reshape(pos, inner_w).astype(BF16), wc_ref[k * inner_w : (k + 1) * inner_w])
     g1 = jnp.where(h1_ref[0].astype(F32) > 0, back * inner_ref[0:1], 0.0).astype(BF16)
     g1_ref[...] = center(g1.astype(F32))
+    if gi_ref is None:
+        return
     gi = gz + dot_t(g1, wr_ref[...])
     gi_ref[...] = center(gi)
     if wire_ref:
@@ -239,7 +253,7 @@
         wire_ref[0][...] = flat_s[: hgt * cols].astype(BF16)
 
 
-def chain_step(info, gy, seed, mz, h2, h1, we, wc, wr, inner, outer, hgt, hand_on, sent):
+def chain_step(info, gy, seed, mz, h2, h1, we, wc, wr, inner, outer, hgt, hand_on, sent, with_gi=True):
     pos, ch = seed.shape[1:]
     inner_w = we.shape[0]
     wide = pos // hgt
@@ -249,9 +263,9 @@
         return pl.BlockSpec((1, pos, lanes), lambda i, info: (info[0], 0, 0))
 
     const = (we, wc, wr, inner, outer)
-    out_shapes = [(kept, ch), (kept, ch), (kept, inner_w), (kept, inner_w)] + [(hgt * sent, ch)] * hand_on
+    out_shapes = [(kept, ch), (kept, inner_w), (kept, inner_w)] + [(kept, ch)] * with_gi + [(hgt * sent, ch)] * hand_on
     return pl.pallas_call(
-        chain_kernel,
+        functools.partial(chain_kernel, with_gi=with_gi),
         out_shape=[jax.ShapeDtypeStruct(s, BF16) for s in out_shapes],
         grid_spec=pltpu.PrefetchScalarGridSpec(
             num_scalar_prefetch=1,
@@ -480,7 +494,7 @@
     return lax.ppermute(value.astype(BF16), "tile", tile_pairs(partner))
 
 
-def scatter_sum(keep_a, send_a, keep_b, send_b):
+def scatter_sum(beside, keep_a, send_a, keep_b, send_b):
     lanes = keep_a.shape[-1]
     other_core = lambda x, z, c: (x, z, 1 - c)
     inner_pair = lambda x, z, c: (x ^ 1, z, c)
@@ -498,11 +512,13 @@
     part_a = along_x(keep_a, send_a, (inner_pair, outer_pair))
     part_b = along_x(keep_b, send_b, (outer_pair, inner_pair))
     total = jnp.concatenate([part_a, part_b], axis=0).reshape(SEGS, Z * 4, lanes)
+    total, beside = lax.optimization_barrier((total, beside))
     for bits in (1, 2):
         count = total.shape[1] // 2
         got = swap(total[:, :count], lambda x, z, c, b=bits: (x, z ^ b, c))
         total = total[:, count:] + got.astype(F32)
-    return finish(total[:, 4:], [swap(total[:, :4], lambda x, z, c: (x, z ^ 6, c))])
+    shares = finish(total[:, 4:], [swap(total[:, :4], lambda x, z, c: (x, z ^ 6, c))])
+    return (*shares, beside)
 
 
 def finish_kernel(own_ref, *refs):
@@ -578,22 +594,22 @@
         mz_s, h2_s, h1_s, _, seed_s = all_rows if slot else first_row
         if slot == 0:
             info = info.at[0].set(0)
-        *saved, last = chain_step(
-            info, arriving[slot], seed_s, mz_s, h2_s, h1_s, *at_hand[:1:-1], inner, outer, hgt, hand_on, sent
+        step = functools.partial(
+            chain_step, info, arriving[slot], seed_s, mz_s, h2_s, h1_s, *at_hand[:1:-1], inner, outer, hgt, hand_on, sent
         )
+        saved = step()
         if hand_on:
-            arriving.append(lax.ppermute(last, "section", back_one))
-        else:
-            saved.append(last)
-        per_slot.append(saved)
-    gi, g3, g2, g1 = zip(*per_slot)
+            arriving.append(lax.ppermute(saved[4], "section", back_one))
+        if slot == slots - 1:
+            saved = [*step(with_gi=False), saved[3]]
+        per_slot.append(saved[:4])
+    g3, g2, g1, gi = zip(*per_slot)
     info = jnp.stack([tile % CORES, tile // (CORES * Z), section]).astype(jnp.int32)
     early, late = range(rows - 1), range(rows - 1, rows)
     so_far = weight_grads(info, (0, 1), early, (xt, pt, ht, pt), (g1, g2, g3), (), "weight_gradients_early")
     sums_a = weight_grads(info, (0,), late, (xt, pt), (g1, g2), so_far[:2], "weight_gradients_a")
     sums_b = weight_grads(info, (1,), late, (ht, pt), (g3, g2), so_far[2:], "weight_gradients_b")
-    g_reduce, g_conv, g_expand = scatter_sum(*sums_a, *sums_b)
-    grad_inputs = collect(info, gi, rows)
+    g_reduce, g_conv, g_expand, grad_inputs = scatter_sum(collect(info, gi, rows), *sums_a, *sums_b)
     grad_inputs = grad_inputs.reshape(rows, hgt, width, ch)
     return grad_inputs[None], g_reduce[None], g_conv[None], g_expand[None]
 

time: 122 us -> 134 us (1.098)
  Pallas kernels: 40.4 us -> 55.3 us
  waiting for transfers between devices: 41.8 us -> 37.5 us
    pallas_call x1, Pallas kernels: 3.1 us -> 17.9 us  [edges(): pl.pallas_call(edges_kernel, out_shape=[jax.ShapeDtypeStruct(out, BF16)]...]
    ppermute x9, waiting for transfers between devices: 25.8 us -> 22.8 us  [swap(): return lax.ppermute(value.astype(BF16), 'tile', tile_pairs(partner))]
    pallas_call x10 -> x11, Pallas kernels: 21.5 us -> 23.8 us  [chain_step(): pl.pallas_call(functools.partial(chain_kernel, with_gi=with_gi), out_shap...]
    pallas_call x2, Pallas kernels: 6.76 us -> 4.56 us  [forward(): pl.pallas_call(functools.partial(forward_kernel, some, len(before)), out_...]
  transfers between devices with their start and end apart: 19 -> 19, of which waited for: 16 -> 16; matrix products, arithmetic and copies ran while one was open for 1% -> 1% of each run, Pallas kernels for 23% -> 22%
where the time goes in v5:
time: 134 us
  Pallas kernels  55.3 us (41%)
  waiting for transfers between devices  37.5 us (28%)
  starting transfers between devices  35 us (26%)
  local copies, waits for them, and re-layouts  3.47 us (3%)
  other arithmetic  1.55 us (1%)
    pallas_call x11, Pallas kernels, chain_step(): pl.pallas_call(functools.partial(chain_kernel, with_gi=with_gi), out_shap...  23.8 us
    ppermute x9, waiting for transfers between devices, swap(): return lax.ppermute(value.astype(BF16), 'tile', tile_pairs(partner))  22.8 us
    pallas_call x1, Pallas kernels, edges(): pl.pallas_call(edges_kernel, out_shape=[jax.ShapeDtypeStruct(out, BF16)]...  17.9 us
    ppermute x8, starting transfers between devices, per_device(): arriving.append(lax.ppermute(saved[4], 'section', back_one))  17.6 us
    ppermute x8, waiting for transfers between devices, per_device(): arriving.append(lax.ppermute(saved[4], 'section', back_one))  14.4 us
    ppermute x9, starting transfers between devices, swap(): return lax.ppermute(value.astype(BF16), 'tile', tile_pairs(partner))  8 us
    ppermute x1, starting transfers between devices, neighbours(): high = lax.ppermute(first, 'tile', [(b, a) for a, b in pairs])  7.47 us
    pallas_call x3, Pallas kernels, weight_grads(): pl.pallas_call(functools.partial(weights_kernel, parts, rows, by_row, len...  5.05 us
  transfers between devices with their start and end apart: 19, of which 16 were waited for; matrix products, arithmetic and copies ran while one was open for 1% of the time, Pallas kernels for 22%

profile of v5, /device:TPU:22, one launch (start us, length us, event | category | flops | bytes accessed | tf_op | source)
XLA Modules:
  0.0 134.0 jit_solution(5523726866899210172)
XLA Ops:
  0.7 17.9 %edge_columns.1 = (bf16[4,6,8,1024]{3,2,1,0:T(8,128)(2,1)}, bf16[4,6,8,1024]{3,2,1,0:T(8,128)(2,1)}) custom-call(s32[4,4]{1,0:T(4,128)} %tissue.5, bf16[4,4,32,1024]{3,2,1,0:T(8,128)(2,1)} %bitcast.29, bf16[4,4,32,1024]{3,2,1,0:T(8,128)(2,1)} %og_ref.3), custom_call_target="tpu_custom_call" | custom-call | tf_op jit(solution)/shard_map/edge_columns/pallas_call | solution.py:66
  20.5 7.5 %collective-permute-start.1 = (bf16[4,6,8,1024]{3,2,1,0:T(8,128)(2,1)}, bf16[4,6,8,1024]{3,2,1,0:T(8,128)(2,1)S(1)}, u32[]{:S(2)}, u32[]{:S(2)}) collective-permute-start(bf16[4,6,8,1024]{3,2,1,0:T(8,128)(2,1)} %get-tuple-element.99), channel_id=1, source_target_pairs={{4,0},{8,4},{12,8},{16,12},{20,16},{24,20},{28,24},{32,28},{36,32}... | collective-permute-start | bytes 1179656 | tf_op jit(solution)/shard_map/ppermute | solution.py:555
  35.2 2.2 %chain_row.11 = (bf16[128,1024]{1,0:T(8,128)(2,1)S(1)}, bf16[128,256]{1,0:T(8,128)(2,1)S(1)}, bf16[128,256]{1,0:T(8,128)(2,1)S(1)}, bf16[128,1024]{1,0:T(8,128)(2,1)S(1)}, bf16[152,1024]{1,0:T(8,128)(2,1)S(1)}) custom-call(s32[2]{0:T(128)S(1)} %constant_dynamic-update-slice_fusion.info, bf16[136,1024]{1,0:T(8,128)(2,1)S(1)} %broadcast_in_dim.12.gy_ref, ...), custom_call_target="tpu_custom_call" | custom-call | flops 3600000000 | bytes 50000000 | tf_op jit(solution)/shard_map/chain_row/pallas_call | solution.py:267
  37.4 2.4 %collective-permute-start.2 = (bf16[152,1024]{1,0:T(8,128)(2,1)S(1)}, bf16[152,1024]{1,0:T(8,128)(2,1)S(1)}, u32[]{:S(2)}, u32[]{:S(2)}) collective-permute-start(bf16[152,1024]{1,0:T(8,128)(2,1)S(1)} %get-tuple-element.121), channel_id=1, source_target_pairs={{1,0},{2,1},{3,2},{5,4},{6,5},{7,6},{9,8},{10,9},{11,10},{13,12},{... | collective-permute-start | bytes 933896 | tf_op jit(solution)/shard_map/ppermute | solution.py:602
  39.8 2.9 %forward_rows.3 = (bf16[4,160,1024]{2,1,0:T(8,128)(2,1)S(1)}, bf16[4,160,256]{2,1,0:T(8,128)(2,1)S(1)}, bf16[4,160,256]{2,1,0:T(8,128)(2,1)S(1)}, bf16[4,6,48,25...) custom-call(s32[2]{0:T(128)S(1)} %add_convert_fusion.4.ends, s32[4,4]{1,0:T(4,128)S(1)} %copy-done.7, ...), custom_call_target="tpu_custom_call" | custom-call | flops 1800000000 | bytes 12000000 | tf_op jit(solution)/shard_map/forward_rows/pallas_call | solution.py:180
  42.7 2.2 %chain_row.12 = (bf16[128,1024]{1,0:T(8,128)(2,1)S(1)}, bf16[128,256]{1,0:T(8,128)(2,1)S(1)}, bf16[128,256]{1,0:T(8,128)(2,1)S(1)}, bf16[128,1024]{1,0:T(8,128)(2,1)S(1)}, bf16[152,1024]{1,0:T(8,128)(2,1)S(1)}) custom-call(s32[2]{0:T(128)S(1)} %get-tuple-element.183.info, bf16[136,1024]{1,0:T(8,128)(2,1)S(1)} %broadcast_in_dim.12.gy_ref, ...), custom_call_target="tpu_custom_call" | custom-call | flops 3600000000 | bytes 50000000 | tf_op jit(solution)/shard_map/chain_row/pallas_call | solution.py:267
  44.8 2.4 %collective-permute-start.3 = (bf16[152,1024]{1,0:T(8,128)(2,1)S(1)}, bf16[152,1024]{1,0:T(8,128)(2,1)S(1)}, u32[]{:S(2)}, u32[]{:S(2)}) collective-permute-start(bf16[152,1024]{1,0:T(8,128)(2,1)S(1)} %get-tuple-element.123), channel_id=1, source_target_pairs={{1,0},{2,1},{3,2},{5,4},{6,5},{7,6},{9,8},{10,9},{11,10},{13,12},{... | collective-permute-start | bytes 933896 | tf_op jit(solution)/shard_map/ppermute | solution.py:602
  48.4 2.2 %chain_row.13 = (bf16[128,1024]{1,0:T(8,128)(2,1)S(1)}, bf16[128,256]{1,0:T(8,128)(2,1)S(1)}, bf16[128,256]{1,0:T(8,128)(2,1)S(1)}, bf16[128,1024]{1,0:T(8,128)(2,1)S(1)}, bf16[152,1024]{1,0:T(8,128)(2,1)S(1)}) custom-call(s32[2]{0:T(128)S(1)} %pad_add_fusion.4.info, bf16[152,1024]{1,0:T(8,128)(2,1)S(1)} %collective-permute-done.2.gy_ref, ...), custom_call_target="tpu_custom_call" | custom-call | flops 3600000000 | bytes 50000000 | tf_op jit(solution)/shard_map/chain_row/pallas_call | solution.py:267
  52.5 2.6 %collective-permute-done.3.gy_ref = bf16[152,1024]{1,0:T(8,128)(2,1)S(1)} collective-permute-done((bf16[152,1024]{1,0:T(8,128)(2,1)S(1)}, bf16[152,1024]{1,0:T(8,128)(2,1)S(1)}, u32[]{:S(2)}, u32[]{:S(2)}) %collective-permute-start.3) | collective-permute-done | bytes 311328 | tf_op jit(solution)/shard_map/ppermute | solution.py:602
  55.1 2.2 %chain_row.14 = (bf16[128,1024]{1,0:T(8,128)(2,1)S(1)}, bf16[128,256]{1,0:T(8,128)(2,1)S(1)}, bf16[128,256]{1,0:T(8,128)(2,1)S(1)}, bf16[128,1024]{1,0:T(8,128)(2,1)S(1)}, bf16[152,1024]{1,0:T(8,128)(2,1)S(1)}) custom-call(s32[2]{0:T(128)S(1)} %pad_add_fusion.5.info, bf16[152,1024]{1,0:T(8,128)(2,1)S(1)} %collective-permute-done.3.gy_ref, ...), custom_call_target="tpu_custom_call" | custom-call | flops 3600000000 | bytes 50000000 | tf_op jit(solution)/shard_map/chain_row/pallas_call | solution.py:267
  57.3 2.5 %collective-permute-start.5 = (bf16[152,1024]{1,0:T(8,128)(2,1)S(1)}, bf16[152,1024]{1,0:T(8,128)(2,1)S(1)}, u32[]{:S(2)}, u32[]{:S(2)}) collective-permute-start(bf16[152,1024]{1,0:T(8,128)(2,1)S(1)} %get-tuple-element.127), channel_id=1, source_target_pairs={{1,0},{2,1},{3,2},{5,4},{6,5},{7,6},{9,8},{10,9},{11,10},{13,12},{... | collective-permute-start | bytes 933896 | tf_op jit(solution)/shard_map/ppermute | solution.py:602
  59.8 2.9 %collective-permute-done.4.gy_ref = bf16[152,1024]{1,0:T(8,128)(2,1)S(1)} collective-permute-done((bf16[152,1024]{1,0:T(8,128)(2,1)S(1)}, bf16[152,1024]{1,0:T(8,128)(2,1)S(1)}, u32[]{:S(2)}, u32[]{:S(2)}) %collective-permute-start.4) | collective-permute-done | bytes 311328 | tf_op jit(solution)/shard_map/ppermute | solution.py:602
  62.8 2.2 %chain_row.15 = (bf16[128,1024]{1,0:T(8,128)(2,1)S(1)}, bf16[128,256]{1,0:T(8,128)(2,1)S(1)}, bf16[128,256]{1,0:T(8,128)(2,1)S(1)}, bf16[128,1024]{1,0:T(8,128)(2,1)S(1)}, bf16[144,1024]{1,0:T(8,128)(2,1)S(1)}) custom-call(s32[2]{0:T(128)S(1)} %pad_add_fusion.6.info, bf16[152,1024]{1,0:T(8,128)(2,1)S(1)} %collective-permute-done.4.gy_ref, ...), custom_call_target="tpu_custom_call" | custom-call | flops 3600000000 | bytes 50000000 | tf_op jit(solution)/shard_map/chain_row/pallas_call | solution.py:267
  64.9 2.1 %collective-permute-start.6 = (bf16[144,1024]{1,0:T(8,128)(2,1)S(1)}, bf16[144,1024]{1,0:T(8,128)(2,1)S(1)}, u32[]{:S(2)}, u32[]{:S(2)}) collective-permute-start(bf16[144,1024]{1,0:T(8,128)(2,1)S(1)} %get-tuple-element.129), channel_id=1, source_target_pairs={{1,0},{2,1},{3,2},{5,4},{6,5},{7,6},{9,8},{10,9},{11,10},{13,12},{... | collective-permute-start | bytes 884744 | tf_op jit(solution)/shard_map/ppermute | solution.py:602
  67.0 2.2 %collective-permute-done.5.gy_ref = bf16[152,1024]{1,0:T(8,128)(2,1)S(1)} collective-permute-done((bf16[152,1024]{1,0:T(8,128)(2,1)S(1)}, bf16[152,1024]{1,0:T(8,128)(2,1)S(1)}, u32[]{:S(2)}, u32[]{:S(2)}) %collective-permute-start.5) | collective-permute-done | bytes 311328 | tf_op jit(solution)/shard_map/ppermute | solution.py:602
  69.3 2.2 %chain_row.16 = (bf16[128,1024]{1,0:T(8,128)(2,1)S(1)}, bf16[128,256]{1,0:T(8,128)(2,1)S(1)}, bf16[128,256]{1,0:T(8,128)(2,1)S(1)}, bf16[128,1024]{1,0:T(8,128)(2,1)S(1)}, bf16[144,1024]{1,0:T(8,128)(2,1)S(1)}) custom-call(s32[2]{0:T(128)S(1)} %pad_add_fusion.7.info, bf16[152,1024]{1,0:T(8,128)(2,1)S(1)} %collective-permute-done.5.gy_ref, ...), custom_call_target="tpu_custom_call" | custom-call | flops 3600000000 | bytes 50000000 | tf_op jit(solution)/shard_map/chain_row/pallas_call | solution.py:267
  75.3 2.2 %chain_row.17 = (bf16[128,1024]{1,0:T(8,128)(2,1)S(1)}, bf16[128,256]{1,0:T(8,128)(2,1)S(1)}, bf16[128,256]{1,0:T(8,128)(2,1)S(1)}, bf16[128,1024]{1,0:T(8,128)(2,1)S(1)}, bf16[136,1024]{1,0:T(8,128)(2,1)S(1)}) custom-call(s32[2]{0:T(128)S(1)} %pad_add_fusion.8.info, bf16[144,1024]{1,0:T(8,128)(2,1)S(1)} %collective-permute-done.6.gy_ref, ...), custom_call_target="tpu_custom_call" | custom-call | flops 3600000000 | bytes 50000000 | tf_op jit(solution)/shard_map/chain_row/pallas_call | solution.py:267
  77.5 2.5 %collective-permute-start.8 = (bf16[136,1024]{1,0:T(8,128)(2,1)S(1)}, bf16[136,1024]{1,0:T(8,128)(2,1)S(1)}, u32[]{:S(2)}, u32[]{:S(2)}) collective-permute-start(bf16[136,1024]{1,0:T(8,128)(2,1)S(1)} %get-tuple-element.133), channel_id=1, source_target_pairs={{1,0},{2,1},{3,2},{5,4},{6,5},{7,6},{9,8},{10,9},{11,10},{13,12},{... | collective-permute-start | bytes 835592 | tf_op jit(solution)/shard_map/ppermute | solution.py:602
  80.0 2.9 %collective-permute-done.7.gy_ref = bf16[144,1024]{1,0:T(8,128)(2,1)S(1)} collective-permute-done((bf16[144,1024]{1,0:T(8,128)(2,1)S(1)}, bf16[144,1024]{1,0:T(8,128)(2,1)S(1)}, u32[]{:S(2)}, u32[]{:S(2)}) %collective-permute-start.7) | collective-permute-done | bytes 294944 | tf_op jit(solution)/shard_map/ppermute | solution.py:602
  82.9 2.2 %chain_row.18 = (bf16[128,1024]{1,0:T(8,128)(2,1)S(1)}, bf16[128,256]{1,0:T(8,128)(2,1)S(1)}, bf16[128,256]{1,0:T(8,128)(2,1)S(1)}, bf16[128,1024]{1,0:T(8,128)(2,1)S(1)}, bf16[136,1024]{1,0:T(8,128)(2,1)S(1)}) custom-call(s32[2]{0:T(128)S(1)} %pad_add_fusion.9.info, bf16[144,1024]{1,0:T(8,128)(2,1)S(1)} %collective-permute-done.7.gy_ref, ...), custom_call_target="tpu_custom_call" | custom-call | flops 3600000000 | bytes 50000000 | tf_op jit(solution)/shard_map/chain_row/pallas_call | solution.py:267
  88.8 2.1 %chain_row.19 = (bf16[128,1024]{1,0:T(8,128)(2,1)S(1)}, bf16[128,256]{1,0:T(8,128)(2,1)S(1)}, bf16[128,256]{1,0:T(8,128)(2,1)S(1)}, bf16[128,1024]{1,0:T(8,128)(2,1)S(1)}) custom-call(s32[2]{0:T(128)S(1)} %pad_add_fusion.10.info, bf16[136,1024]{1,0:T(8,128)(2,1)S(1)} %collective-permute-done.8.gy_ref, bf16[4,160,1024]{2,1,0:T(8,128)(2,1)S(1)} %get-tuple-element.117.seed_ref, ...), custom_call_target="tpu_custom_call" | custom-call | flops 3600000000 | bytes 50000000 | tf_op jit(solution)/shard_map/chain_row/pallas_call | solution.py:267
  90.9 2.7 %weight_gradients_early.1 = (bf16[1024,256]{1,0:T(8,128)(2,1)S(1)}, bf16[1024,256]{1,0:T(8,128)(2,1)S(1)}, bf16[1152,256]{1,0:T(8,128)(2,1)S(1)}, bf16[1152,256]{1,0:T(8,128)(2,1)S(1)}) custom-call(s32[3]{0:T(128)S(1)} %pad_add_fusion.1.info, bf16[1024,512]{1,0:T(8,128)(2,1)S(1)} %get-tuple-element.113.refs_0_, ...), custom_call_target="tpu_custom_call" | custom-call | flops 900000000 | bytes 6000000 | tf_op jit(solution)/shard_map/weight_gradients_early/pallas_call | solution.py:429
  100.2 2.8 %chain_row.21 = (bf16[128,1024]{1,0:T(8,128)(2,1)}, bf16[128,256]{1,0:T(8,128)(2,1)}, bf16[128,256]{1,0:T(8,128)(2,1)}, bf16[128,1024]{1,0:T(8,128)(2,1)S(1)}) custom-call(s32[2]{0:T(128)S(1)} %pad_add_fusion.11.info, bf16[136,1024]{1,0:T(8,128)(2,1)S(1)} %collective-permute-done.9.gy_ref, bf16[4,160,1024]{2,1,0:T(8,128)(2,1)S(1)} %get-tuple-element.117.seed_ref, ...), custom_call_target="tpu_custom_call" | custom-call | flops 3600000000 | bytes 50000000 | tf_op jit(solution)/shard_map/chain_row/pallas_call | solution.py:267
  104.5 2.5 %collective-permute-done.11 = bf16[512,256]{1,0:T(8,128)(2,1)S(1)} collective-permute-done((bf16[512,256]{1,0:T(8,128)(2,1)S(1)}, bf16[512,256]{1,0:T(8,128)(2,1)S(1)}, u32[]{:S(2)}, u32[]{:S(2)}) %collective-permute-start.11) | collective-permute-done | bytes 262176 | tf_op jit(solution)/shard_map/ppermute | solution.py:494
  107.8 3.1 %collective-permute-done.14 = bf16[576,256]{1,0:T(8,128)(2,1)S(1)} collective-permute-done((bf16[576,256]{1,0:T(8,128)(2,1)S(1)}, bf16[576,256]{1,0:T(8,128)(2,1)S(1)}, u32[]{:S(2)}, u32[]{:S(2)}) %collective-permute-start.14) | collective-permute-done | bytes 294944 | tf_op jit(solution)/shard_map/ppermute | solution.py:494
  111.1 2.3 %collective-permute-done.12 = bf16[256,256]{1,0:T(8,128)(2,1)S(1)} collective-permute-done((bf16[256,256]{1,0:T(8,128)(2,1)S(1)}, bf16[256,256]{1,0:T(8,128)(2,1)S(1)}, u32[]{:S(2)}, u32[]{:S(2)}) %collective-permute-start.12) | collective-permute-done | bytes 131104 | tf_op jit(solution)/shard_map/ppermute | solution.py:494
  113.5 2.7 %collective-permute-done.15 = bf16[288,256]{1,0:T(8,128)(2,1)S(1)} collective-permute-done((bf16[288,256]{1,0:T(8,128)(2,1)S(1)}, bf16[288,256]{1,0:T(8,128)(2,1)S(1)}, u32[]{:S(2)}, u32[]{:S(2)}) %collective-permute-start.15) | collective-permute-done | bytes 147488 | tf_op jit(solution)/shard_map/ppermute | solution.py:494
  116.6 4.9 %collective-permute-done.16 = bf16[17,16,256]{2,1,0:T(8,128)(2,1)S(1)} collective-permute-done((bf16[17,16,256]{2,1,0:T(8,128)(2,1)S(1)}, bf16[17,16,256]{2,1,0:T(8,128)(2,1)S(1)}, u32[]{:S(2)}, u32[]{:S(2)}) %collective-permute-start.16) | collective-permute-done | bytes 139296 | tf_op jit(solution)/shard_map/ppermute | solution.py:494
  121.5 2.2 %collective-permute-start.17 = (bf16[17,8,256]{2,1,0:T(8,128)(2,1)S(1)}, bf16[17,8,256]{2,1,0:T(8,128)(2,1)S(1)}, u32[]{:S(2)}, u32[]{:S(2)}) collective-permute-start(bf16[17,8,256]{2,1,0:T(8,128)(2,1)S(1)} %slice.147), channel_id=1, source_target_pairs={{0,16},{4,20},{8,24},{12,28},{16,0},{20,4},{24,8},{28,12},{32,48},... | collective-permute-start | bytes 208904 | tf_op jit(solution)/shard_map/ppermute | solution.py:494
  123.8 3.4 %collective-permute-done.17 = bf16[17,8,256]{2,1,0:T(8,128)(2,1)S(1)} collective-permute-done((bf16[17,8,256]{2,1,0:T(8,128)(2,1)S(1)}, bf16[17,8,256]{2,1,0:T(8,128)(2,1)S(1)}, u32[]{:S(2)}, u32[]{:S(2)}) %collective-permute-start.17) | collective-permute-done | bytes 69664 | tf_op jit(solution)/shard_map/ppermute | solution.py:494
  127.2 3.5 %collective-permute-start.18 = (bf16[17,4,256]{2,1,0:T(4,128)(2,1)S(1)}, bf16[17,4,256]{2,1,0:T(4,128)(2,1)S(1)}, u32[]{:S(2)}, u32[]{:S(2)}) collective-permute-start(bf16[17,4,256]{2,1,0:T(4,128)(2,1)S(1)} %slice.148), channel_id=1, source_target_pairs={{0,48},{4,52},{8,56},{12,60},{16,32},{20,36},{24,40},{28,44},{32,1... | collective-permute-start | bytes 104456 | tf_op jit(solution)/shard_map/ppermute | solution.py:494
  130.7 2.6 %collective-permute-done.18.refs_0_ = bf16[17,4,256]{2,1,0:T(4,128)(2,1)S(1)} collective-permute-done((bf16[17,4,256]{2,1,0:T(4,128)(2,1)S(1)}, bf16[17,4,256]{2,1,0:T(4,128)(2,1)S(1)}, u32[]{:S(2)}, u32[]{:S(2)}) %collective-permute-start.18) | collective-permute-done | bytes 34848 | tf_op jit(solution)/shard_map/ppermute | solution.py:494
  (75 shorter events, 29.9 us)
Async XLA Ops:
  0.6 28.4 %copy-start = (bf16[4,4,32,1024]{3,2,1,0:T(8,128)(2,1)S(1)}, bf16[4,4,32,1024]{3,2,1,0:T(8,128)(2,1)}, u32[]{:S(2)}) copy-start(bf16[4,4,32,1024]{3,2,1,0:T(8,128)(2,1)} %og_ref.3) | copy-start | bytes 3145732
  0.6 28.4 %copy-start.1 = (bf16[1,4,4,32,1024]{4,3,2,1,0:T(8,128)(2,1)S(1)}, bf16[1,4,4,32,1024]{4,3,2,1,0:T(8,128)(2,1)}, u32[]{:S(2)}) copy-start(bf16[1,4,4,32,1024]{4,3,2,1,0:T(8,128)(2,1)} %param.11) | copy-start | bytes 3145732
  0.7 28.4 %copy-start.5 = (f32[1,4,256]{2,1,0:T(4,128)S(1)}, f32[1,4,256]{2,1,0:T(4,128)}, u32[]{:S(2)}) copy-start(f32[1,4,256]{2,1,0:T(4,128)} %param.17) | copy-start | bytes 12292
  18.5 14.7 %collective-permute-start = (bf16[4,6,8,1024]{3,2,1,0:T(8,128)(2,1)}, bf16[4,6,8,1024]{3,2,1,0:T(8,128)(2,1)S(1)}, u32[]{:S(2)}, u32[]{:S(2)}) collective-permute-start(bf16[4,6,8,1024]{3,2,1,0:T(8,128)(2,1)} %get-tuple-element.98), channel_id=1, source_target_pairs={{0,4},{4,8},{8,12},{12,16},{16,20},{20,24},{24,28},{28,32},{32,36}... | collective-permute-start | bytes 1179656 | tf_op jit(solution)/shard_map/ppermute | solution.py:554
  20.5 13.1 %collective-permute-start.1 = (bf16[4,6,8,1024]{3,2,1,0:T(8,128)(2,1)}, bf16[4,6,8,1024]{3,2,1,0:T(8,128)(2,1)S(1)}, u32[]{:S(2)}, u32[]{:S(2)}) collective-permute-start(bf16[4,6,8,1024]{3,2,1,0:T(8,128)(2,1)} %get-tuple-element.99), channel_id=1, source_target_pairs={{4,0},{8,4},{12,8},{16,12},{20,16},{24,20},{28,24},{32,28},{36,32}... | collective-permute-start | bytes 1179656 | tf_op jit(solution)/shard_map/ppermute | solution.py:555
  29.0 1.3 copy-start.2
  30.3 1.0 copy-start.3
  31.3 1.0 copy-start.4
  32.4 1.2 copy-start.6
  32.4 1.2 copy-start.7
  37.4 11.0 %collective-permute-start.2 = (bf16[152,1024]{1,0:T(8,128)(2,1)S(1)}, bf16[152,1024]{1,0:T(8,128)(2,1)S(1)}, u32[]{:S(2)}, u32[]{:S(2)}) collective-permute-start(bf16[152,1024]{1,0:T(8,128)(2,1)S(1)} %get-tuple-element.121), channel_id=1, source_target_pairs={{1,0},{2,1},{3,2},{5,4},{6,5},{7,6},{9,8},{10,9},{11,10},{13,12},{... | collective-permute-start | bytes 933896 | tf_op jit(solution)/shard_map/ppermute | solution.py:602
  44.8 10.3 %collective-permute-start.3 = (bf16[152,1024]{1,0:T(8,128)(2,1)S(1)}, bf16[152,1024]{1,0:T(8,128)(2,1)S(1)}, u32[]{:S(2)}, u32[]{:S(2)}) collective-permute-start(bf16[152,1024]{1,0:T(8,128)(2,1)S(1)} %get-tuple-element.123), channel_id=1, source_target_pairs={{1,0},{2,1},{3,2},{5,4},{6,5},{7,6},{9,8},{10,9},{11,10},{13,12},{... | collective-permute-start | bytes 933896 | tf_op jit(solution)/shard_map/ppermute | solution.py:602
  50.6 12.2 %collective-permute-start.4 = (bf16[152,1024]{1,0:T(8,128)(2,1)S(1)}, bf16[152,1024]{1,0:T(8,128)(2,1)S(1)}, u32[]{:S(2)}, u32[]{:S(2)}) collective-permute-start(bf16[152,1024]{1,0:T(8,128)(2,1)S(1)} %get-tuple-element.125), channel_id=1, source_target_pairs={{1,0},{2,1},{3,2},{5,4},{6,5},{7,6},{9,8},{10,9},{11,10},{13,12},{... | collective-permute-start | bytes 933896 | tf_op jit(solution)/shard_map/ppermute | solution.py:602
  57.3 12.0 %collective-permute-start.5 = (bf16[152,1024]{1,0:T(8,128)(2,1)S(1)}, bf16[152,1024]{1,0:T(8,128)(2,1)S(1)}, u32[]{:S(2)}, u32[]{:S(2)}) collective-permute-start(bf16[152,1024]{1,0:T(8,128)(2,1)S(1)} %get-tuple-element.127), channel_id=1, source_target_pairs={{1,0},{2,1},{3,2},{5,4},{6,5},{7,6},{9,8},{10,9},{11,10},{13,12},{... | collective-permute-start | bytes 933896 | tf_op jit(solution)/shard_map/ppermute | solution.py:602
  64.9 10.4 %collective-permute-start.6 = (bf16[144,1024]{1,0:T(8,128)(2,1)S(1)}, bf16[144,1024]{1,0:T(8,128)(2,1)S(1)}, u32[]{:S(2)}, u32[]{:S(2)}) collective-permute-start(bf16[144,1024]{1,0:T(8,128)(2,1)S(1)} %get-tuple-element.129), channel_id=1, source_target_pairs={{1,0},{2,1},{3,2},{5,4},{6,5},{7,6},{9,8},{10,9},{11,10},{13,12},{... | collective-permute-start | bytes 884744 | tf_op jit(solution)/shard_map/ppermute | solution.py:602
  71.4 11.5 %collective-permute-start.7 = (bf16[144,1024]{1,0:T(8,128)(2,1)S(1)}, bf16[144,1024]{1,0:T(8,128)(2,1)S(1)}, u32[]{:S(2)}, u32[]{:S(2)}) collective-permute-start(bf16[144,1024]{1,0:T(8,128)(2,1)S(1)} %get-tuple-element.131), channel_id=1, source_target_pairs={{1,0},{2,1},{3,2},{5,4},{6,5},{7,6},{9,8},{10,9},{11,10},{13,12},{... | collective-permute-start | bytes 884744 | tf_op jit(solution)/shard_map/ppermute | solution.py:602
  77.5 11.3 %collective-permute-start.8 = (bf16[136,1024]{1,0:T(8,128)(2,1)S(1)}, bf16[136,1024]{1,0:T(8,128)(2,1)S(1)}, u32[]{:S(2)}, u32[]{:S(2)}) collective-permute-start(bf16[136,1024]{1,0:T(8,128)(2,1)S(1)} %get-tuple-element.133), channel_id=1, source_target_pairs={{1,0},{2,1},{3,2},{5,4},{6,5},{7,6},{9,8},{10,9},{11,10},{13,12},{... | collective-permute-start | bytes 835592 | tf_op jit(solution)/shard_map/ppermute | solution.py:602
  85.1 8.5 %collective-permute-start.9 = (bf16[136,1024]{1,0:T(8,128)(2,1)S(1)}, bf16[136,1024]{1,0:T(8,128)(2,1)S(1)}, u32[]{:S(2)}, u32[]{:S(2)}) collective-permute-start(bf16[136,1024]{1,0:T(8,128)(2,1)S(1)} %get-tuple-element.155), channel_id=1, source_target_pairs={{1,0},{2,1},{3,2},{5,4},{6,5},{7,6},{9,8},{10,9},{11,10},{13,12},{... | collective-permute-start | bytes 835592 | tf_op jit(solution)/shard_map/ppermute | solution.py:602
  96.4 2.0 %collective-permute-start.10 = (bf16[1024,256]{1,0:T(8,128)(2,1)S(1)}, bf16[1024,256]{1,0:T(8,128)(2,1)S(1)}, u32[]{:S(2)}, u32[]{:S(2)}) collective-permute-start(bf16[1024,256]{1,0:T(8,128)(2,1)S(1)} %get-tuple-element.159), channel_id=1, source_target_pairs={{0,4},{4,0},{8,12},{12,8},{16,20},{20,16},{24,28},{28,24},{32,36},... | collective-permute-start | bytes 1572872 | tf_op jit(solution)/shard_map/ppermute | solution.py:494
  97.7 2.2 %collective-permute-start.13 = (bf16[1152,256]{1,0:T(8,128)(2,1)S(1)}, bf16[1152,256]{1,0:T(8,128)(2,1)S(1)}, u32[]{:S(2)}, u32[]{:S(2)}) collective-permute-start(bf16[1152,256]{1,0:T(8,128)(2,1)S(1)} %get-tuple-element.164), channel_id=1, source_target_pairs={{0,4},{4,0},{8,12},{12,8},{16,20},{20,16},{24,28},{28,24},{32,36},... | collective-permute-start | bytes 1769480 | tf_op jit(solution)/shard_map/ppermute | solution.py:494
  98.5 8.4 %collective-permute-start.11 = (bf16[512,256]{1,0:T(8,128)(2,1)S(1)}, bf16[512,256]{1,0:T(8,128)(2,1)S(1)}, u32[]{:S(2)}, u32[]{:S(2)}) collective-permute-start(bf16[512,256]{1,0:T(8,128)(2,1)S(1)} %add_convert_fusion.1), channel_id=1, source_target_pairs={{0,64},{4,68},{8,72},{12,76},{16,80},{20,84},{24,88},{28,92},{32,9... | collective-permute-start | bytes 786440 | tf_op jit(solution)/shard_map/ppermute | solution.py:494
  100.0 10.9 %collective-permute-start.14 = (bf16[576,256]{1,0:T(8,128)(2,1)S(1)}, bf16[576,256]{1,0:T(8,128)(2,1)S(1)}, u32[]{:S(2)}, u32[]{:S(2)}) collective-permute-start(bf16[576,256]{1,0:T(8,128)(2,1)S(1)} %add_convert_fusion), channel_id=1, source_target_pairs={{0,192},{4,196},{8,200},{12,204},{16,208},{20,212},{24,216},{28,22... | collective-permute-start | bytes 884744 | tf_op jit(solution)/shard_map/ppermute | solution.py:494
  107.0 6.4 %collective-permute-start.12 = (bf16[256,256]{1,0:T(8,128)(2,1)S(1)}, bf16[256,256]{1,0:T(8,128)(2,1)S(1)}, u32[]{:S(2)}, u32[]{:S(2)}) collective-permute-start(bf16[256,256]{1,0:T(8,128)(2,1)S(1)} %add_convert_fusion.3), channel_id=1, source_target_pairs={{0,192},{4,196},{8,200},{12,204},{16,208},{20,212},{24,216},{28,22... | collective-permute-start | bytes 393224 | tf_op jit(solution)/shard_map/ppermute | solution.py:494
  111.0 5.2 %collective-permute-start.15 = (bf16[288,256]{1,0:T(8,128)(2,1)S(1)}, bf16[288,256]{1,0:T(8,128)(2,1)S(1)}, u32[]{:S(2)}, u32[]{:S(2)}) collective-permute-start(bf16[288,256]{1,0:T(8,128)(2,1)S(1)} %add_convert_fusion.2), channel_id=1, source_target_pairs={{0,64},{4,68},{8,72},{12,76},{16,80},{20,84},{24,88},{28,92},{32,9... | collective-permute-start | bytes 442376 | tf_op jit(solution)/shard_map/ppermute | solution.py:494
  116.3 5.1 %collective-permute-start.16 = (bf16[17,16,256]{2,1,0:T(8,128)(2,1)S(1)}, bf16[17,16,256]{2,1,0:T(8,128)(2,1)S(1)}, u32[]{:S(2)}, u32[]{:S(2)}) collective-permute-start(bf16[17,16,256]{2,1,0:T(8,128)(2,1)S(1)} %slice.146), channel_id=1, source_target_pairs={{0,8},{4,12},{8,0},{12,4},{16,24},{20,28},{24,16},{28,20},{32,40},... | collective-permute-start | bytes 417800 | tf_op jit(solution)/shard_map/ppermute | solution.py:494
  121.5 5.6 %collective-permute-start.17 = (bf16[17,8,256]{2,1,0:T(8,128)(2,1)S(1)}, bf16[17,8,256]{2,1,0:T(8,128)(2,1)S(1)}, u32[]{:S(2)}, u32[]{:S(2)}) collective-permute-start(bf16[17,8,256]{2,1,0:T(8,128)(2,1)S(1)} %slice.147), channel_id=1, source_target_pairs={{0,16},{4,20},{8,24},{12,28},{16,0},{20,4},{24,8},{28,12},{32,48},... | collective-permute-start | bytes 208904 | tf_op jit(solution)/shard_map/ppermute | solution.py:494
  127.2 6.1 %collective-permute-start.18 = (bf16[17,4,256]{2,1,0:T(4,128)(2,1)S(1)}, bf16[17,4,256]{2,1,0:T(4,128)(2,1)S(1)}, u32[]{:S(2)}, u32[]{:S(2)}) collective-permute-start(bf16[17,4,256]{2,1,0:T(4,128)(2,1)S(1)} %slice.148), channel_id=1, source_target_pairs={{0,48},{4,52},{8,56},{12,60},{16,32},{20,36},{24,40},{28,44},{32,1... | collective-permute-start | bytes 104456 | tf_op jit(solution)/shard_map/ppermute | solution.py:494

commit v6 on v5

--- a/solution.py
+++ b/solution.py
@@ -34,29 +34,32 @@
     return pl.BlockSpec(shape, lambda *_: (0,) * len(shape), pipeline_mode=pl.Buffered(1))
 
 
-def edges_kernel(tissue, x_ref, og_ref, first_ref, last_ref, og_s, seed_s, sems):
+def edges_kernel(tissue, x_ref, og_ref, first_ref, last_ref, og_s, stage, sems):
     rows, hgt, width, ch = x_ref.shape
     sides = (
         (first_ref, 0, 0, 0),
         (last_ref, width - EDGE, tissue.shape[1] - 1, EDGE - RIM),
     )
-    plain, fetched, handed = [], [], []
+    from_og, from_x, handed = [], [], []
     for n, (out, start, _, _) in enumerate(sides):
         cols = pl.ds(start, EDGE)
-        fetched.append(pltpu.make_async_copy(og_ref.at[:, :, cols], og_s.at[n], sems.at[n]))
-        plain.append(pltpu.make_async_copy(x_ref.at[:, :, cols], out.at[:, pl.ds(0, hgt)], sems.at[2 + n]))
-        handed.append(pltpu.make_async_copy(seed_s.at[n], out.at[:, pl.ds(hgt, hgt // 2)], sems.at[4 + n]))
-    for copy in fetched + plain:
+        from_og.append(pltpu.make_async_copy(og_ref.at[:, :, cols], og_s.at[n], sems.at[n]))
+        from_x.append(
+            pltpu.make_async_copy(x_ref.at[:, :, cols], stage.at[n, :, pl.ds(0, hgt)], sems.at[2 + n])
+        )
+        handed.append(pltpu.make_async_copy(stage.at[n], out, sems.at[4 + n]))
+    for copy in from_og + from_x:
         copy.start()
     for n, (_, _, tile, at) in enumerate(sides):
-        fetched[n].wait()
+        from_og[n].wait()
         for r in range(rows):
             seed = og_s[n, r].astype(F32)[:, at : at + RIM] * tissue[r, tile].astype(F32)
             for pair in range(hgt // 2):
                 both = jnp.concatenate([seed[2 * pair], seed[2 * pair + 1]], axis=0)
-                seed_s[n, r, pair] = both.astype(BF16)
+                stage[n, r, hgt + pair] = both.astype(BF16)
+        from_x[n].wait()
         handed[n].start()
-    for copy in plain + handed:
+    for copy in handed:
         copy.wait()
 
 
@@ -73,7 +76,7 @@
             out_specs=[pl.BlockSpec(memory_space=pl.ANY)] * 2,
             scratch_shapes=[
                 pltpu.VMEM((2, rows, hgt, EDGE, ch), BF16),
-                pltpu.VMEM((2, rows, hgt // 2, EDGE, ch), BF16),
+                pltpu.VMEM((2,) + out, BF16),
                 pltpu.SemaphoreType.DMA((6,)),
             ],
         ),

time: 134 us -> 119 us (0.89)
  Pallas kernels: 55.3 us -> 40.3 us
    pallas_call x1, Pallas kernels: 17.9 us -> 2.87 us  [edges(): pl.pallas_call(edges_kernel, out_shape=[jax.ShapeDtypeStruct(out, BF16)]...]
  transfers between devices with their start and end apart: 19 -> 19, of which waited for: 16 -> 16; matrix products, arithmetic and copies ran while one was open for 1% -> 1% of each run, Pallas kernels for 22% -> 25%
where the time goes in v6:
time: 119 us
  Pallas kernels  40.3 us (34%)
  waiting for transfers between devices  37.2 us (31%)
  starting transfers between devices  35.4 us (30%)
  local copies, waits for them, and re-layouts  3.47 us (3%)
  other arithmetic  1.55 us (1%)
    pallas_call x11, Pallas kernels, chain_step(): pl.pallas_call(functools.partial(chain_kernel, with_gi=with_gi), out_shap...  23.8 us
    ppermute x9, waiting for transfers between devices, swap(): return lax.ppermute(value.astype(BF16), 'tile', tile_pairs(partner))  22.5 us
    ppermute x8, starting transfers between devices, per_device(): arriving.append(lax.ppermute(saved[4], 'section', back_one))  17.6 us
    ppermute x8, waiting for transfers between devices, per_device(): arriving.append(lax.ppermute(saved[4], 'section', back_one))  14.3 us
    ppermute x9, starting transfers between devices, swap(): return lax.ppermute(value.astype(BF16), 'tile', tile_pairs(partner))  8.34 us
    ppermute x1, starting transfers between devices, neighbours(): high = lax.ppermute(first, 'tile', [(b, a) for a, b in pairs])  7.47 us
    pallas_call x3, Pallas kernels, weight_grads(): pl.pallas_call(functools.partial(weights_kernel, parts, rows, by_row, len...  5.04 us
    pallas_call x2, Pallas kernels, forward(): pl.pallas_call(functools.partial(forward_kernel, some, len(before)), out_...  4.56 us
  transfers between devices with their start and end apart: 19, of which 16 were waited for; matrix products, arithmetic and copies ran while one was open for 1% of the time, Pallas kernels for 25%

profile of v6, /device:TPU:22, one launch (start us, length us, event | category | flops | bytes accessed | tf_op | source)
XLA Modules:
  0.0 119.0 jit_solution(4567697350555122792)
XLA Ops:
  0.7 2.9 %edge_columns.1 = (bf16[4,6,8,1024]{3,2,1,0:T(8,128)(2,1)}, bf16[4,6,8,1024]{3,2,1,0:T(8,128)(2,1)}) custom-call(s32[4,4]{1,0:T(4,128)} %tissue.5, bf16[4,4,32,1024]{3,2,1,0:T(8,128)(2,1)} %bitcast.29, bf16[4,4,32,1024]{3,2,1,0:T(8,128)(2,1)} %og_ref.3), custom_call_target="tpu_custom_call" | custom-call | tf_op jit(solution)/shard_map/edge_columns/pallas_call | solution.py:69
  5.5 7.5 %collective-permute-start.1 = (bf16[4,6,8,1024]{3,2,1,0:T(8,128)(2,1)}, bf16[4,6,8,1024]{3,2,1,0:T(8,128)(2,1)S(1)}, u32[]{:S(2)}, u32[]{:S(2)}) collective-permute-start(bf16[4,6,8,1024]{3,2,1,0:T(8,128)(2,1)} %get-tuple-element.99), channel_id=1, source_target_pairs={{4,0},{8,4},{12,8},{16,12},{20,16},{24,20},{28,24},{32,28},{36,32}... | collective-permute-start | bytes 1179656 | tf_op jit(solution)/shard_map/ppermute | solution.py:558
  20.2 2.2 %chain_row.11 = (bf16[128,1024]{1,0:T(8,128)(2,1)S(1)}, bf16[128,256]{1,0:T(8,128)(2,1)S(1)}, bf16[128,256]{1,0:T(8,128)(2,1)S(1)}, bf16[128,1024]{1,0:T(8,128)(2,1)S(1)}, bf16[152,1024]{1,0:T(8,128)(2,1)S(1)}) custom-call(s32[2]{0:T(128)S(1)} %constant_dynamic-update-slice_fusion.info, bf16[136,1024]{1,0:T(8,128)(2,1)S(1)} %broadcast_in_dim.12.gy_ref, ...), custom_call_target="tpu_custom_call" | custom-call | flops 3600000000 | bytes 50000000 | tf_op jit(solution)/shard_map/chain_row/pallas_call | solution.py:270
  22.4 2.4 %collective-permute-start.2 = (bf16[152,1024]{1,0:T(8,128)(2,1)S(1)}, bf16[152,1024]{1,0:T(8,128)(2,1)S(1)}, u32[]{:S(2)}, u32[]{:S(2)}) collective-permute-start(bf16[152,1024]{1,0:T(8,128)(2,1)S(1)} %get-tuple-element.121), channel_id=1, source_target_pairs={{1,0},{2,1},{3,2},{5,4},{6,5},{7,6},{9,8},{10,9},{11,10},{13,12},{... | collective-permute-start | bytes 933896 | tf_op jit(solution)/shard_map/ppermute | solution.py:605
  24.8 2.9 %forward_rows.3 = (bf16[4,160,1024]{2,1,0:T(8,128)(2,1)S(1)}, bf16[4,160,256]{2,1,0:T(8,128)(2,1)S(1)}, bf16[4,160,256]{2,1,0:T(8,128)(2,1)S(1)}, bf16[4,6,48,25...) custom-call(s32[2]{0:T(128)S(1)} %add_convert_fusion.4.ends, s32[4,4]{1,0:T(4,128)S(1)} %copy-done.7, ...), custom_call_target="tpu_custom_call" | custom-call | flops 1800000000 | bytes 12000000 | tf_op jit(solution)/shard_map/forward_rows/pallas_call | solution.py:183
  27.7 2.2 %chain_row.12 = (bf16[128,1024]{1,0:T(8,128)(2,1)S(1)}, bf16[128,256]{1,0:T(8,128)(2,1)S(1)}, bf16[128,256]{1,0:T(8,128)(2,1)S(1)}, bf16[128,1024]{1,0:T(8,128)(2,1)S(1)}, bf16[152,1024]{1,0:T(8,128)(2,1)S(1)}) custom-call(s32[2]{0:T(128)S(1)} %get-tuple-element.183.info, bf16[136,1024]{1,0:T(8,128)(2,1)S(1)} %broadcast_in_dim.12.gy_ref, ...), custom_call_target="tpu_custom_call" | custom-call | flops 3600000000 | bytes 50000000 | tf_op jit(solution)/shard_map/chain_row/pallas_call | solution.py:270
  29.8 2.4 %collective-permute-start.3 = (bf16[152,1024]{1,0:T(8,128)(2,1)S(1)}, bf16[152,1024]{1,0:T(8,128)(2,1)S(1)}, u32[]{:S(2)}, u32[]{:S(2)}) collective-permute-start(bf16[152,1024]{1,0:T(8,128)(2,1)S(1)} %get-tuple-element.123), channel_id=1, source_target_pairs={{1,0},{2,1},{3,2},{5,4},{6,5},{7,6},{9,8},{10,9},{11,10},{13,12},{... | collective-permute-start | bytes 933896 | tf_op jit(solution)/shard_map/ppermute | solution.py:605
  33.4 2.2 %chain_row.13 = (bf16[128,1024]{1,0:T(8,128)(2,1)S(1)}, bf16[128,256]{1,0:T(8,128)(2,1)S(1)}, bf16[128,256]{1,0:T(8,128)(2,1)S(1)}, bf16[128,1024]{1,0:T(8,128)(2,1)S(1)}, bf16[152,1024]{1,0:T(8,128)(2,1)S(1)}) custom-call(s32[2]{0:T(128)S(1)} %pad_add_fusion.4.info, bf16[152,1024]{1,0:T(8,128)(2,1)S(1)} %collective-permute-done.2.gy_ref, ...), custom_call_target="tpu_custom_call" | custom-call | flops 3600000000 | bytes 50000000 | tf_op jit(solution)/shard_map/chain_row/pallas_call | solution.py:270
  37.5 2.6 %collective-permute-done.3.gy_ref = bf16[152,1024]{1,0:T(8,128)(2,1)S(1)} collective-permute-done((bf16[152,1024]{1,0:T(8,128)(2,1)S(1)}, bf16[152,1024]{1,0:T(8,128)(2,1)S(1)}, u32[]{:S(2)}, u32[]{:S(2)}) %collective-permute-start.3) | collective-permute-done | bytes 311328 | tf_op jit(solution)/shard_map/ppermute | solution.py:605
  40.1 2.2 %chain_row.14 = (bf16[128,1024]{1,0:T(8,128)(2,1)S(1)}, bf16[128,256]{1,0:T(8,128)(2,1)S(1)}, bf16[128,256]{1,0:T(8,128)(2,1)S(1)}, bf16[128,1024]{1,0:T(8,128)(2,1)S(1)}, bf16[152,1024]{1,0:T(8,128)(2,1)S(1)}) custom-call(s32[2]{0:T(128)S(1)} %pad_add_fusion.5.info, bf16[152,1024]{1,0:T(8,128)(2,1)S(1)} %collective-permute-done.3.gy_ref, ...), custom_call_target="tpu_custom_call" | custom-call | flops 3600000000 | bytes 50000000 | tf_op jit(solution)/shard_map/chain_row/pallas_call | solution.py:270
  42.3 2.5 %collective-permute-start.5 = (bf16[152,1024]{1,0:T(8,128)(2,1)S(1)}, bf16[152,1024]{1,0:T(8,128)(2,1)S(1)}, u32[]{:S(2)}, u32[]{:S(2)}) collective-permute-start(bf16[152,1024]{1,0:T(8,128)(2,1)S(1)} %get-tuple-element.127), channel_id=1, source_target_pairs={{1,0},{2,1},{3,2},{5,4},{6,5},{7,6},{9,8},{10,9},{11,10},{13,12},{... | collective-permute-start | bytes 933896 | tf_op jit(solution)/shard_map/ppermute | solution.py:605
  44.8 2.9 %collective-permute-done.4.gy_ref = bf16[152,1024]{1,0:T(8,128)(2,1)S(1)} collective-permute-done((bf16[152,1024]{1,0:T(8,128)(2,1)S(1)}, bf16[152,1024]{1,0:T(8,128)(2,1)S(1)}, u32[]{:S(2)}, u32[]{:S(2)}) %collective-permute-start.4) | collective-permute-done | bytes 311328 | tf_op jit(solution)/shard_map/ppermute | solution.py:605
  47.8 2.2 %chain_row.15 = (bf16[128,1024]{1,0:T(8,128)(2,1)S(1)}, bf16[128,256]{1,0:T(8,128)(2,1)S(1)}, bf16[128,256]{1,0:T(8,128)(2,1)S(1)}, bf16[128,1024]{1,0:T(8,128)(2,1)S(1)}, bf16[144,1024]{1,0:T(8,128)(2,1)S(1)}) custom-call(s32[2]{0:T(128)S(1)} %pad_add_fusion.6.info, bf16[152,1024]{1,0:T(8,128)(2,1)S(1)} %collective-permute-done.4.gy_ref, ...), custom_call_target="tpu_custom_call" | custom-call | flops 3600000000 | bytes 50000000 | tf_op jit(solution)/shard_map/chain_row/pallas_call | solution.py:270
  49.9 2.1 %collective-permute-start.6 = (bf16[144,1024]{1,0:T(8,128)(2,1)S(1)}, bf16[144,1024]{1,0:T(8,128)(2,1)S(1)}, u32[]{:S(2)}, u32[]{:S(2)}) collective-permute-start(bf16[144,1024]{1,0:T(8,128)(2,1)S(1)} %get-tuple-element.129), channel_id=1, source_target_pairs={{1,0},{2,1},{3,2},{5,4},{6,5},{7,6},{9,8},{10,9},{11,10},{13,12},{... | collective-permute-start | bytes 884744 | tf_op jit(solution)/shard_map/ppermute | solution.py:605
  52.0 2.2 %collective-permute-done.5.gy_ref = bf16[152,1024]{1,0:T(8,128)(2,1)S(1)} collective-permute-done((bf16[152,1024]{1,0:T(8,128)(2,1)S(1)}, bf16[152,1024]{1,0:T(8,128)(2,1)S(1)}, u32[]{:S(2)}, u32[]{:S(2)}) %collective-permute-start.5) | collective-permute-done | bytes 311328 | tf_op jit(solution)/shard_map/ppermute | solution.py:605
  54.3 2.2 %chain_row.16 = (bf16[128,1024]{1,0:T(8,128)(2,1)S(1)}, bf16[128,256]{1,0:T(8,128)(2,1)S(1)}, bf16[128,256]{1,0:T(8,128)(2,1)S(1)}, bf16[128,1024]{1,0:T(8,128)(2,1)S(1)}, bf16[144,1024]{1,0:T(8,128)(2,1)S(1)}) custom-call(s32[2]{0:T(128)S(1)} %pad_add_fusion.7.info, bf16[152,1024]{1,0:T(8,128)(2,1)S(1)} %collective-permute-done.5.gy_ref, ...), custom_call_target="tpu_custom_call" | custom-call | flops 3600000000 | bytes 50000000 | tf_op jit(solution)/shard_map/chain_row/pallas_call | solution.py:270
  60.2 2.2 %chain_row.17 = (bf16[128,1024]{1,0:T(8,128)(2,1)S(1)}, bf16[128,256]{1,0:T(8,128)(2,1)S(1)}, bf16[128,256]{1,0:T(8,128)(2,1)S(1)}, bf16[128,1024]{1,0:T(8,128)(2,1)S(1)}, bf16[136,1024]{1,0:T(8,128)(2,1)S(1)}) custom-call(s32[2]{0:T(128)S(1)} %pad_add_fusion.8.info, bf16[144,1024]{1,0:T(8,128)(2,1)S(1)} %collective-permute-done.6.gy_ref, ...), custom_call_target="tpu_custom_call" | custom-call | flops 3600000000 | bytes 50000000 | tf_op jit(solution)/shard_map/chain_row/pallas_call | solution.py:270
  62.4 2.5 %collective-permute-start.8 = (bf16[136,1024]{1,0:T(8,128)(2,1)S(1)}, bf16[136,1024]{1,0:T(8,128)(2,1)S(1)}, u32[]{:S(2)}, u32[]{:S(2)}) collective-permute-start(bf16[136,1024]{1,0:T(8,128)(2,1)S(1)} %get-tuple-element.133), channel_id=1, source_target_pairs={{1,0},{2,1},{3,2},{5,4},{6,5},{7,6},{9,8},{10,9},{11,10},{13,12},{... | collective-permute-start | bytes 835592 | tf_op jit(solution)/shard_map/ppermute | solution.py:605
  64.9 3.0 %collective-permute-done.7.gy_ref = bf16[144,1024]{1,0:T(8,128)(2,1)S(1)} collective-permute-done((bf16[144,1024]{1,0:T(8,128)(2,1)S(1)}, bf16[144,1024]{1,0:T(8,128)(2,1)S(1)}, u32[]{:S(2)}, u32[]{:S(2)}) %collective-permute-start.7) | collective-permute-done | bytes 294944 | tf_op jit(solution)/shard_map/ppermute | solution.py:605
  67.9 2.2 %chain_row.18 = (bf16[128,1024]{1,0:T(8,128)(2,1)S(1)}, bf16[128,256]{1,0:T(8,128)(2,1)S(1)}, bf16[128,256]{1,0:T(8,128)(2,1)S(1)}, bf16[128,1024]{1,0:T(8,128)(2,1)S(1)}, bf16[136,1024]{1,0:T(8,128)(2,1)S(1)}) custom-call(s32[2]{0:T(128)S(1)} %pad_add_fusion.9.info, bf16[144,1024]{1,0:T(8,128)(2,1)S(1)} %collective-permute-done.7.gy_ref, ...), custom_call_target="tpu_custom_call" | custom-call | flops 3600000000 | bytes 50000000 | tf_op jit(solution)/shard_map/chain_row/pallas_call | solution.py:270
  73.7 2.1 %chain_row.19 = (bf16[128,1024]{1,0:T(8,128)(2,1)S(1)}, bf16[128,256]{1,0:T(8,128)(2,1)S(1)}, bf16[128,256]{1,0:T(8,128)(2,1)S(1)}, bf16[128,1024]{1,0:T(8,128)(2,1)S(1)}) custom-call(s32[2]{0:T(128)S(1)} %pad_add_fusion.10.info, bf16[136,1024]{1,0:T(8,128)(2,1)S(1)} %collective-permute-done.8.gy_ref, bf16[4,160,1024]{2,1,0:T(8,128)(2,1)S(1)} %get-tuple-element.117.seed_ref, ...), custom_call_target="tpu_custom_call" | custom-call | flops 3600000000 | bytes 50000000 | tf_op jit(solution)/shard_map/chain_row/pallas_call | solution.py:270
  75.8 2.7 %weight_gradients_early.1 = (bf16[1024,256]{1,0:T(8,128)(2,1)S(1)}, bf16[1024,256]{1,0:T(8,128)(2,1)S(1)}, bf16[1152,256]{1,0:T(8,128)(2,1)S(1)}, bf16[1152,256]{1,0:T(8,128)(2,1)S(1)}) custom-call(s32[3]{0:T(128)S(1)} %pad_add_fusion.1.info, bf16[1024,512]{1,0:T(8,128)(2,1)S(1)} %get-tuple-element.113.refs_0_, ...), custom_call_target="tpu_custom_call" | custom-call | flops 900000000 | bytes 6000000 | tf_op jit(solution)/shard_map/weight_gradients_early/pallas_call | solution.py:432
  85.2 2.8 %chain_row.21 = (bf16[128,1024]{1,0:T(8,128)(2,1)}, bf16[128,256]{1,0:T(8,128)(2,1)}, bf16[128,256]{1,0:T(8,128)(2,1)}, bf16[128,1024]{1,0:T(8,128)(2,1)S(1)}) custom-call(s32[2]{0:T(128)S(1)} %pad_add_fusion.11.info, bf16[136,1024]{1,0:T(8,128)(2,1)S(1)} %collective-permute-done.9.gy_ref, bf16[4,160,1024]{2,1,0:T(8,128)(2,1)S(1)} %get-tuple-element.117.seed_ref, ...), custom_call_target="tpu_custom_call" | custom-call | flops 3600000000 | bytes 50000000 | tf_op jit(solution)/shard_map/chain_row/pallas_call | solution.py:270
  89.5 2.4 %collective-permute-done.11 = bf16[512,256]{1,0:T(8,128)(2,1)S(1)} collective-permute-done((bf16[512,256]{1,0:T(8,128)(2,1)S(1)}, bf16[512,256]{1,0:T(8,128)(2,1)S(1)}, u32[]{:S(2)}, u32[]{:S(2)}) %collective-permute-start.11) | collective-permute-done | bytes 262176 | tf_op jit(solution)/shard_map/ppermute | solution.py:497
  92.7 3.1 %collective-permute-done.14 = bf16[576,256]{1,0:T(8,128)(2,1)S(1)} collective-permute-done((bf16[576,256]{1,0:T(8,128)(2,1)S(1)}, bf16[576,256]{1,0:T(8,128)(2,1)S(1)}, u32[]{:S(2)}, u32[]{:S(2)}) %collective-permute-start.14) | collective-permute-done | bytes 294944 | tf_op jit(solution)/shard_map/ppermute | solution.py:497
  96.0 2.3 %collective-permute-done.12 = bf16[256,256]{1,0:T(8,128)(2,1)S(1)} collective-permute-done((bf16[256,256]{1,0:T(8,128)(2,1)S(1)}, bf16[256,256]{1,0:T(8,128)(2,1)S(1)}, u32[]{:S(2)}, u32[]{:S(2)}) %collective-permute-start.12) | collective-permute-done | bytes 131104 | tf_op jit(solution)/shard_map/ppermute | solution.py:497
  98.4 2.7 %collective-permute-done.15 = bf16[288,256]{1,0:T(8,128)(2,1)S(1)} collective-permute-done((bf16[288,256]{1,0:T(8,128)(2,1)S(1)}, bf16[288,256]{1,0:T(8,128)(2,1)S(1)}, u32[]{:S(2)}, u32[]{:S(2)}) %collective-permute-start.15) | collective-permute-done | bytes 147488 | tf_op jit(solution)/shard_map/ppermute | solution.py:497
  101.6 4.9 %collective-permute-done.16 = bf16[17,16,256]{2,1,0:T(8,128)(2,1)S(1)} collective-permute-done((bf16[17,16,256]{2,1,0:T(8,128)(2,1)S(1)}, bf16[17,16,256]{2,1,0:T(8,128)(2,1)S(1)}, u32[]{:S(2)}, u32[]{:S(2)}) %collective-permute-start.16) | collective-permute-done | bytes 139296 | tf_op jit(solution)/shard_map/ppermute | solution.py:497
  106.5 2.4 %collective-permute-start.17 = (bf16[17,8,256]{2,1,0:T(8,128)(2,1)S(1)}, bf16[17,8,256]{2,1,0:T(8,128)(2,1)S(1)}, u32[]{:S(2)}, u32[]{:S(2)}) collective-permute-start(bf16[17,8,256]{2,1,0:T(8,128)(2,1)S(1)} %slice.147), channel_id=1, source_target_pairs={{0,16},{4,20},{8,24},{12,28},{16,0},{20,4},{24,8},{28,12},{32,48},... | collective-permute-start | bytes 208904 | tf_op jit(solution)/shard_map/ppermute | solution.py:497
  108.8 3.3 %collective-permute-done.17 = bf16[17,8,256]{2,1,0:T(8,128)(2,1)S(1)} collective-permute-done((bf16[17,8,256]{2,1,0:T(8,128)(2,1)S(1)}, bf16[17,8,256]{2,1,0:T(8,128)(2,1)S(1)}, u32[]{:S(2)}, u32[]{:S(2)}) %collective-permute-start.17) | collective-permute-done | bytes 69664 | tf_op jit(solution)/shard_map/ppermute | solution.py:497
  112.2 3.5 %collective-permute-start.18 = (bf16[17,4,256]{2,1,0:T(4,128)(2,1)S(1)}, bf16[17,4,256]{2,1,0:T(4,128)(2,1)S(1)}, u32[]{:S(2)}, u32[]{:S(2)}) collective-permute-start(bf16[17,4,256]{2,1,0:T(4,128)(2,1)S(1)} %slice.148), channel_id=1, source_target_pairs={{0,48},{4,52},{8,56},{12,60},{16,32},{20,36},{24,40},{28,44},{32,1... | collective-permute-start | bytes 104456 | tf_op jit(solution)/shard_map/ppermute | solution.py:497
  115.7 2.6 %collective-permute-done.18.refs_0_ = bf16[17,4,256]{2,1,0:T(4,128)(2,1)S(1)} collective-permute-done((bf16[17,4,256]{2,1,0:T(4,128)(2,1)S(1)}, bf16[17,4,256]{2,1,0:T(4,128)(2,1)S(1)}, u32[]{:S(2)}, u32[]{:S(2)}) %collective-permute-start.18) | collective-permute-done | bytes 34848 | tf_op jit(solution)/shard_map/ppermute | solution.py:497
  (75 shorter events, 29.9 us)
Async XLA Ops:
  0.6 13.4 %copy-start = (bf16[4,4,32,1024]{3,2,1,0:T(8,128)(2,1)S(1)}, bf16[4,4,32,1024]{3,2,1,0:T(8,128)(2,1)}, u32[]{:S(2)}) copy-start(bf16[4,4,32,1024]{3,2,1,0:T(8,128)(2,1)} %og_ref.3) | copy-start | bytes 3145732
  0.6 13.4 %copy-start.1 = (bf16[1,4,4,32,1024]{4,3,2,1,0:T(8,128)(2,1)S(1)}, bf16[1,4,4,32,1024]{4,3,2,1,0:T(8,128)(2,1)}, u32[]{:S(2)}) copy-start(bf16[1,4,4,32,1024]{4,3,2,1,0:T(8,128)(2,1)} %param.11) | copy-start | bytes 3145732
  0.7 13.4 %copy-start.5 = (f32[1,4,256]{2,1,0:T(4,128)S(1)}, f32[1,4,256]{2,1,0:T(4,128)}, u32[]{:S(2)}) copy-start(f32[1,4,256]{2,1,0:T(4,128)} %param.17) | copy-start | bytes 12292
  3.5 14.7 %collective-permute-start = (bf16[4,6,8,1024]{3,2,1,0:T(8,128)(2,1)}, bf16[4,6,8,1024]{3,2,1,0:T(8,128)(2,1)S(1)}, u32[]{:S(2)}, u32[]{:S(2)}) collective-permute-start(bf16[4,6,8,1024]{3,2,1,0:T(8,128)(2,1)} %get-tuple-element.98), channel_id=1, source_target_pairs={{0,4},{4,8},{8,12},{12,16},{16,20},{20,24},{24,28},{28,32},{32,36}... | collective-permute-start | bytes 1179656 | tf_op jit(solution)/shard_map/ppermute | solution.py:557
  5.5 13.1 %collective-permute-start.1 = (bf16[4,6,8,1024]{3,2,1,0:T(8,128)(2,1)}, bf16[4,6,8,1024]{3,2,1,0:T(8,128)(2,1)S(1)}, u32[]{:S(2)}, u32[]{:S(2)}) collective-permute-start(bf16[4,6,8,1024]{3,2,1,0:T(8,128)(2,1)} %get-tuple-element.99), channel_id=1, source_target_pairs={{4,0},{8,4},{12,8},{16,12},{20,16},{24,20},{28,24},{32,28},{36,32}... | collective-permute-start | bytes 1179656 | tf_op jit(solution)/shard_map/ppermute | solution.py:558
  14.0 1.3 %copy-start.2 = (bf16[1,3,3,256,256]{4,3,2,1,0:T(8,128)(2,1)S(1)}, bf16[1,3,3,256,256]{4,3,2,1,0:T(8,128)(2,1)}, u32[]{:S(2)}) copy-start(bf16[1,3,3,256,256]{4,3,2,1,0:T(8,128)(2,1)} %param.15) | copy-start | bytes 3538948
  15.3 1.0 copy-start.3
  16.3 1.0 copy-start.4
  17.4 1.2 copy-start.6
  17.4 1.2 copy-start.7
  22.4 11.0 %collective-permute-start.2 = (bf16[152,1024]{1,0:T(8,128)(2,1)S(1)}, bf16[152,1024]{1,0:T(8,128)(2,1)S(1)}, u32[]{:S(2)}, u32[]{:S(2)}) collective-permute-start(bf16[152,1024]{1,0:T(8,128)(2,1)S(1)} %get-tuple-element.121), channel_id=1, source_target_pairs={{1,0},{2,1},{3,2},{5,4},{6,5},{7,6},{9,8},{10,9},{11,10},{13,12},{... | collective-permute-start | bytes 933896 | tf_op jit(solution)/shard_map/ppermute | solution.py:605
  29.8 10.3 %collective-permute-start.3 = (bf16[152,1024]{1,0:T(8,128)(2,1)S(1)}, bf16[152,1024]{1,0:T(8,128)(2,1)S(1)}, u32[]{:S(2)}, u32[]{:S(2)}) collective-permute-start(bf16[152,1024]{1,0:T(8,128)(2,1)S(1)} %get-tuple-element.123), channel_id=1, source_target_pairs={{1,0},{2,1},{3,2},{5,4},{6,5},{7,6},{9,8},{10,9},{11,10},{13,12},{... | collective-permute-start | bytes 933896 | tf_op jit(solution)/shard_map/ppermute | solution.py:605
  35.6 12.2 %collective-permute-start.4 = (bf16[152,1024]{1,0:T(8,128)(2,1)S(1)}, bf16[152,1024]{1,0:T(8,128)(2,1)S(1)}, u32[]{:S(2)}, u32[]{:S(2)}) collective-permute-start(bf16[152,1024]{1,0:T(8,128)(2,1)S(1)} %get-tuple-element.125), channel_id=1, source_target_pairs={{1,0},{2,1},{3,2},{5,4},{6,5},{7,6},{9,8},{10,9},{11,10},{13,12},{... | collective-permute-start | bytes 933896 | tf_op jit(solution)/shard_map/ppermute | solution.py:605
  42.3 12.0 %collective-permute-start.5 = (bf16[152,1024]{1,0:T(8,128)(2,1)S(1)}, bf16[152,1024]{1,0:T(8,128)(2,1)S(1)}, u32[]{:S(2)}, u32[]{:S(2)}) collective-permute-start(bf16[152,1024]{1,0:T(8,128)(2,1)S(1)} %get-tuple-element.127), channel_id=1, source_target_pairs={{1,0},{2,1},{3,2},{5,4},{6,5},{7,6},{9,8},{10,9},{11,10},{13,12},{... | collective-permute-start | bytes 933896 | tf_op jit(solution)/shard_map/ppermute | solution.py:605
  49.9 10.3 %collective-permute-start.6 = (bf16[144,1024]{1,0:T(8,128)(2,1)S(1)}, bf16[144,1024]{1,0:T(8,128)(2,1)S(1)}, u32[]{:S(2)}, u32[]{:S(2)}) collective-permute-start(bf16[144,1024]{1,0:T(8,128)(2,1)S(1)} %get-tuple-element.129), channel_id=1, source_target_pairs={{1,0},{2,1},{3,2},{5,4},{6,5},{7,6},{9,8},{10,9},{11,10},{13,12},{... | collective-permute-start | bytes 884744 | tf_op jit(solution)/shard_map/ppermute | solution.py:605
  56.4 11.5 %collective-permute-start.7 = (bf16[144,1024]{1,0:T(8,128)(2,1)S(1)}, bf16[144,1024]{1,0:T(8,128)(2,1)S(1)}, u32[]{:S(2)}, u32[]{:S(2)}) collective-permute-start(bf16[144,1024]{1,0:T(8,128)(2,1)S(1)} %get-tuple-element.131), channel_id=1, source_target_pairs={{1,0},{2,1},{3,2},{5,4},{6,5},{7,6},{9,8},{10,9},{11,10},{13,12},{... | collective-permute-start | bytes 884744 | tf_op jit(solution)/shard_map/ppermute | solution.py:605
  62.4 11.3 %collective-permute-start.8 = (bf16[136,1024]{1,0:T(8,128)(2,1)S(1)}, bf16[136,1024]{1,0:T(8,128)(2,1)S(1)}, u32[]{:S(2)}, u32[]{:S(2)}) collective-permute-start(bf16[136,1024]{1,0:T(8,128)(2,1)S(1)} %get-tuple-element.133), channel_id=1, source_target_pairs={{1,0},{2,1},{3,2},{5,4},{6,5},{7,6},{9,8},{10,9},{11,10},{13,12},{... | collective-permute-start | bytes 835592 | tf_op jit(solution)/shard_map/ppermute | solution.py:605
  70.1 8.5 %collective-permute-start.9 = (bf16[136,1024]{1,0:T(8,128)(2,1)S(1)}, bf16[136,1024]{1,0:T(8,128)(2,1)S(1)}, u32[]{:S(2)}, u32[]{:S(2)}) collective-permute-start(bf16[136,1024]{1,0:T(8,128)(2,1)S(1)} %get-tuple-element.155), channel_id=1, source_target_pairs={{1,0},{2,1},{3,2},{5,4},{6,5},{7,6},{9,8},{10,9},{11,10},{13,12},{... | collective-permute-start | bytes 835592 | tf_op jit(solution)/shard_map/ppermute | solution.py:605
  81.4 2.0 %collective-permute-start.10 = (bf16[1024,256]{1,0:T(8,128)(2,1)S(1)}, bf16[1024,256]{1,0:T(8,128)(2,1)S(1)}, u32[]{:S(2)}, u32[]{:S(2)}) collective-permute-start(bf16[1024,256]{1,0:T(8,128)(2,1)S(1)} %get-tuple-element.159), channel_id=1, source_target_pairs={{0,4},{4,0},{8,12},{12,8},{16,20},{20,16},{24,28},{28,24},{32,36},... | collective-permute-start | bytes 1572872 | tf_op jit(solution)/shard_map/ppermute | solution.py:497
  82.6 2.2 %collective-permute-start.13 = (bf16[1152,256]{1,0:T(8,128)(2,1)S(1)}, bf16[1152,256]{1,0:T(8,128)(2,1)S(1)}, u32[]{:S(2)}, u32[]{:S(2)}) collective-permute-start(bf16[1152,256]{1,0:T(8,128)(2,1)S(1)} %get-tuple-element.164), channel_id=1, source_target_pairs={{0,4},{4,0},{8,12},{12,8},{16,20},{20,16},{24,28},{28,24},{32,36},... | collective-permute-start | bytes 1769480 | tf_op jit(solution)/shard_map/ppermute | solution.py:497
  83.5 8.4 %collective-permute-start.11 = (bf16[512,256]{1,0:T(8,128)(2,1)S(1)}, bf16[512,256]{1,0:T(8,128)(2,1)S(1)}, u32[]{:S(2)}, u32[]{:S(2)}) collective-permute-start(bf16[512,256]{1,0:T(8,128)(2,1)S(1)} %add_convert_fusion.1), channel_id=1, source_target_pairs={{0,64},{4,68},{8,72},{12,76},{16,80},{20,84},{24,88},{28,92},{32,9... | collective-permute-start | bytes 786440 | tf_op jit(solution)/shard_map/ppermute | solution.py:497
  84.9 10.9 %collective-permute-start.14 = (bf16[576,256]{1,0:T(8,128)(2,1)S(1)}, bf16[576,256]{1,0:T(8,128)(2,1)S(1)}, u32[]{:S(2)}, u32[]{:S(2)}) collective-permute-start(bf16[576,256]{1,0:T(8,128)(2,1)S(1)} %add_convert_fusion), channel_id=1, source_target_pairs={{0,192},{4,196},{8,200},{12,204},{16,208},{20,212},{24,216},{28,22... | collective-permute-start | bytes 884744 | tf_op jit(solution)/shard_map/ppermute | solution.py:497
  92.0 6.4 %collective-permute-start.12 = (bf16[256,256]{1,0:T(8,128)(2,1)S(1)}, bf16[256,256]{1,0:T(8,128)(2,1)S(1)}, u32[]{:S(2)}, u32[]{:S(2)}) collective-permute-start(bf16[256,256]{1,0:T(8,128)(2,1)S(1)} %add_convert_fusion.3), channel_id=1, source_target_pairs={{0,192},{4,196},{8,200},{12,204},{16,208},{20,212},{24,216},{28,22... | collective-permute-start | bytes 393224 | tf_op jit(solution)/shard_map/ppermute | solution.py:497
  95.9 5.2 %collective-permute-start.15 = (bf16[288,256]{1,0:T(8,128)(2,1)S(1)}, bf16[288,256]{1,0:T(8,128)(2,1)S(1)}, u32[]{:S(2)}, u32[]{:S(2)}) collective-permute-start(bf16[288,256]{1,0:T(8,128)(2,1)S(1)} %add_convert_fusion.2), channel_id=1, source_target_pairs={{0,64},{4,68},{8,72},{12,76},{16,80},{20,84},{24,88},{28,92},{32,9... | collective-permute-start | bytes 442376 | tf_op jit(solution)/shard_map/ppermute | solution.py:497
  101.3 5.1 %collective-permute-start.16 = (bf16[17,16,256]{2,1,0:T(8,128)(2,1)S(1)}, bf16[17,16,256]{2,1,0:T(8,128)(2,1)S(1)}, u32[]{:S(2)}, u32[]{:S(2)}) collective-permute-start(bf16[17,16,256]{2,1,0:T(8,128)(2,1)S(1)} %slice.146), channel_id=1, source_target_pairs={{0,8},{4,12},{8,0},{12,4},{16,24},{20,28},{24,16},{28,20},{32,40},... | collective-permute-start | bytes 417800 | tf_op jit(solution)/shard_map/ppermute | solution.py:497
  106.5 5.7 %collective-permute-start.17 = (bf16[17,8,256]{2,1,0:T(8,128)(2,1)S(1)}, bf16[17,8,256]{2,1,0:T(8,128)(2,1)S(1)}, u32[]{:S(2)}, u32[]{:S(2)}) collective-permute-start(bf16[17,8,256]{2,1,0:T(8,128)(2,1)S(1)} %slice.147), channel_id=1, source_target_pairs={{0,16},{4,20},{8,24},{12,28},{16,0},{20,4},{24,8},{28,12},{32,48},... | collective-permute-start | bytes 208904 | tf_op jit(solution)/shard_map/ppermute | solution.py:497
  112.2 6.1 %collective-permute-start.18 = (bf16[17,4,256]{2,1,0:T(4,128)(2,1)S(1)}, bf16[17,4,256]{2,1,0:T(4,128)(2,1)S(1)}, u32[]{:S(2)}, u32[]{:S(2)}) collective-permute-start(bf16[17,4,256]{2,1,0:T(4,128)(2,1)S(1)} %slice.148), channel_id=1, source_target_pairs={{0,48},{4,52},{8,56},{12,60},{16,32},{20,36},{24,40},{28,44},{32,1... | collective-permute-start | bytes 104456 | tf_op jit(solution)/shard_map/ppermute | solution.py:497

commit v7 on v6

--- a/solution.py
+++ b/solution.py
@@ -131,10 +131,12 @@
     hs[:, hgt + 1] = jnp.zeros((count, width + 2 * EDGE, inner_w), F32)
     hs[:, 1 : hgt + 1, EDGE : EDGE + width] = own_ref[these].astype(F32)
     xs[:, :, EDGE : EDGE + width] = x_ref[these].astype(F32)
-    for ref, at, keep in ((lo_ref, 0, ends[0]), (hi_ref, EDGE + width, ends[1])):
-        part = ref[these, :hgt]
-        xs[:, :, at : at + EDGE] = part.astype(F32)
-        hs[:, 1 : hgt + 1, at : at + EDGE] = hidden_one(part, wr_ref[...], inner_ref) * keep.astype(F32)
+    parts = jnp.concatenate([lo_ref[these, :hgt], hi_ref[these, :hgt]], axis=0)
+    outside = hidden_one(parts, wr_ref[...], inner_ref)
+    for n, (at, keep) in enumerate(((0, ends[0]), (EDGE + width, ends[1]))):
+        side = slice(n * count, (n + 1) * count)
+        xs[:, :, at : at + EDGE] = parts[side].astype(F32)
+        hs[:, 1 : hgt + 1, at : at + EDGE] = outside[side] * keep.astype(F32)
     pad_ref[into] = hs[...].astype(BF16)
     first = EDGE - RIM - 1
     for k in range(9):
@@ -223,7 +225,8 @@
     cols = gy_ref.shape[0] // hgt
     at = (wide - cols) // 2
     flat_s[: hgt * cols] = gy_ref[...].astype(F32)
-    wide_s[...] = jnp.zeros_like(wide_s)
+    wide_s[:, :8] = jnp.zeros((hgt, 8, ch), F32)
+    wide_s[:, wide - 8 :] = jnp.zeros((hgt, 8, ch), F32)
     for h in range(hgt):
         wide_s[h, at : at + cols] = flat_s[h * cols : (h + 1) * cols]
     gy = jnp.where(info[1] == 1, seed_ref[0].astype(F32), wide_s[...].reshape(pos, ch))

time: 119 us -> 120 us (level)
  no operation moved by 1% of the time
where the time goes in v7:
time: 120 us; the launch traced here: 119 us
  Pallas kernels  40.4 us (34%)
  waiting for transfers between devices  37.5 us (31%)
  starting transfers between devices  35 us (29%)
  local copies, waits for them, and re-layouts  3.47 us (3%)
  other arithmetic  1.55 us (1%)
    pallas_call x11, Pallas kernels, chain_step(): pl.pallas_call(functools.partial(chain_kernel, with_gi=with_gi), out_shap...  23.8 us
    ppermute x9, waiting for transfers between devices, swap(): return lax.ppermute(value.astype(BF16), 'tile', tile_pairs(partner))  22.7 us
    ppermute x8, starting transfers between devices, per_device(): arriving.append(lax.ppermute(saved[4], 'section', back_one))  17.6 us
    ppermute x8, waiting for transfers between devices, per_device(): arriving.append(lax.ppermute(saved[4], 'section', back_one))  14.4 us
    ppermute x9, starting transfers between devices, swap(): return lax.ppermute(value.astype(BF16), 'tile', tile_pairs(partner))  8.02 us
    ppermute x1, starting transfers between devices, neighbours(): high = lax.ppermute(first, 'tile', [(b, a) for a, b in pairs])  7.47 us
    pallas_call x3, Pallas kernels, weight_grads(): pl.pallas_call(functools.partial(weights_kernel, parts, rows, by_row, len...  5.05 us
    pallas_call x2, Pallas kernels, forward(): pl.pallas_call(functools.partial(forward_kernel, some, len(before)), out_...  4.68 us
  transfers between devices with their start and end apart: 19, of which 16 were waited for; matrix products, arithmetic and copies ran while one was open for 1% of the time, Pallas kernels for 25%

profile of v7, /device:TPU:22, one launch (start us, length us, event | category | flops | bytes accessed | tf_op | source)
XLA Modules:
  0.0 119.1 jit_solution(16821643729407783509)
XLA Ops:
  0.7 2.9 %edge_columns.1 = (bf16[4,6,8,1024]{3,2,1,0:T(8,128)(2,1)}, bf16[4,6,8,1024]{3,2,1,0:T(8,128)(2,1)}) custom-call(s32[4,4]{1,0:T(4,128)} %tissue.5, bf16[4,4,32,1024]{3,2,1,0:T(8,128)(2,1)} %bitcast.29, bf16[4,4,32,1024]{3,2,1,0:T(8,128)(2,1)} %og_ref.3), custom_call_target="tpu_custom_call" | custom-call | tf_op jit(solution)/shard_map/edge_columns/pallas_call | solution.py:69
  5.5 7.5 %collective-permute-start.1 = (bf16[4,6,8,1024]{3,2,1,0:T(8,128)(2,1)}, bf16[4,6,8,1024]{3,2,1,0:T(8,128)(2,1)S(1)}, u32[]{:S(2)}, u32[]{:S(2)}) collective-permute-start(bf16[4,6,8,1024]{3,2,1,0:T(8,128)(2,1)} %get-tuple-element.99), channel_id=1, source_target_pairs={{4,0},{8,4},{12,8},{16,12},{20,16},{24,20},{28,24},{32,28},{36,32}... | collective-permute-start | bytes 1179656 | tf_op jit(solution)/shard_map/ppermute | solution.py:561
  20.2 2.2 %chain_row.11 = (bf16[128,1024]{1,0:T(8,128)(2,1)S(1)}, bf16[128,256]{1,0:T(8,128)(2,1)S(1)}, bf16[128,256]{1,0:T(8,128)(2,1)S(1)}, bf16[128,1024]{1,0:T(8,128)(2,1)S(1)}, bf16[152,1024]{1,0:T(8,128)(2,1)S(1)}) custom-call(s32[2]{0:T(128)S(1)} %constant_dynamic-update-slice_fusion.info, bf16[136,1024]{1,0:T(8,128)(2,1)S(1)} %broadcast_in_dim.12.gy_ref, ...), custom_call_target="tpu_custom_call" | custom-call | flops 3600000000 | bytes 50000000 | tf_op jit(solution)/shard_map/chain_row/pallas_call | solution.py:273
  22.4 2.4 %collective-permute-start.2 = (bf16[152,1024]{1,0:T(8,128)(2,1)S(1)}, bf16[152,1024]{1,0:T(8,128)(2,1)S(1)}, u32[]{:S(2)}, u32[]{:S(2)}) collective-permute-start(bf16[152,1024]{1,0:T(8,128)(2,1)S(1)} %get-tuple-element.121), channel_id=1, source_target_pairs={{1,0},{2,1},{3,2},{5,4},{6,5},{7,6},{9,8},{10,9},{11,10},{13,12},{... | collective-permute-start | bytes 933896 | tf_op jit(solution)/shard_map/ppermute | solution.py:608
  24.8 3.0 %forward_rows.3 = (bf16[4,160,1024]{2,1,0:T(8,128)(2,1)S(1)}, bf16[4,160,256]{2,1,0:T(8,128)(2,1)S(1)}, bf16[4,160,256]{2,1,0:T(8,128)(2,1)S(1)}, bf16[4,6,48,25...) custom-call(s32[2]{0:T(128)S(1)} %add_convert_fusion.4.ends, s32[4,4]{1,0:T(4,128)S(1)} %copy-done.7, ...), custom_call_target="tpu_custom_call" | custom-call | flops 1800000000 | bytes 12000000 | tf_op jit(solution)/shard_map/forward_rows/pallas_call | solution.py:185
  27.8 2.2 %chain_row.12 = (bf16[128,1024]{1,0:T(8,128)(2,1)S(1)}, bf16[128,256]{1,0:T(8,128)(2,1)S(1)}, bf16[128,256]{1,0:T(8,128)(2,1)S(1)}, bf16[128,1024]{1,0:T(8,128)(2,1)S(1)}, bf16[152,1024]{1,0:T(8,128)(2,1)S(1)}) custom-call(s32[2]{0:T(128)S(1)} %get-tuple-element.183.info, bf16[136,1024]{1,0:T(8,128)(2,1)S(1)} %broadcast_in_dim.12.gy_ref, ...), custom_call_target="tpu_custom_call" | custom-call | flops 3600000000 | bytes 50000000 | tf_op jit(solution)/shard_map/chain_row/pallas_call | solution.py:273
  30.0 2.4 %collective-permute-start.3 = (bf16[152,1024]{1,0:T(8,128)(2,1)S(1)}, bf16[152,1024]{1,0:T(8,128)(2,1)S(1)}, u32[]{:S(2)}, u32[]{:S(2)}) collective-permute-start(bf16[152,1024]{1,0:T(8,128)(2,1)S(1)} %get-tuple-element.123), channel_id=1, source_target_pairs={{1,0},{2,1},{3,2},{5,4},{6,5},{7,6},{9,8},{10,9},{11,10},{13,12},{... | collective-permute-start | bytes 933896 | tf_op jit(solution)/shard_map/ppermute | solution.py:608
  33.5 2.2 %chain_row.13 = (bf16[128,1024]{1,0:T(8,128)(2,1)S(1)}, bf16[128,256]{1,0:T(8,128)(2,1)S(1)}, bf16[128,256]{1,0:T(8,128)(2,1)S(1)}, bf16[128,1024]{1,0:T(8,128)(2,1)S(1)}, bf16[152,1024]{1,0:T(8,128)(2,1)S(1)}) custom-call(s32[2]{0:T(128)S(1)} %pad_add_fusion.4.info, bf16[152,1024]{1,0:T(8,128)(2,1)S(1)} %collective-permute-done.2.gy_ref, ...), custom_call_target="tpu_custom_call" | custom-call | flops 3600000000 | bytes 50000000 | tf_op jit(solution)/shard_map/chain_row/pallas_call | solution.py:273
  37.6 2.7 %collective-permute-done.3.gy_ref = bf16[152,1024]{1,0:T(8,128)(2,1)S(1)} collective-permute-done((bf16[152,1024]{1,0:T(8,128)(2,1)S(1)}, bf16[152,1024]{1,0:T(8,128)(2,1)S(1)}, u32[]{:S(2)}, u32[]{:S(2)}) %collective-permute-start.3) | collective-permute-done | bytes 311328 | tf_op jit(solution)/shard_map/ppermute | solution.py:608
  40.3 2.2 %chain_row.14 = (bf16[128,1024]{1,0:T(8,128)(2,1)S(1)}, bf16[128,256]{1,0:T(8,128)(2,1)S(1)}, bf16[128,256]{1,0:T(8,128)(2,1)S(1)}, bf16[128,1024]{1,0:T(8,128)(2,1)S(1)}, bf16[152,1024]{1,0:T(8,128)(2,1)S(1)}) custom-call(s32[2]{0:T(128)S(1)} %pad_add_fusion.5.info, bf16[152,1024]{1,0:T(8,128)(2,1)S(1)} %collective-permute-done.3.gy_ref, ...), custom_call_target="tpu_custom_call" | custom-call | flops 3600000000 | bytes 50000000 | tf_op jit(solution)/shard_map/chain_row/pallas_call | solution.py:273
  42.4 2.5 %collective-permute-start.5 = (bf16[152,1024]{1,0:T(8,128)(2,1)S(1)}, bf16[152,1024]{1,0:T(8,128)(2,1)S(1)}, u32[]{:S(2)}, u32[]{:S(2)}) collective-permute-start(bf16[152,1024]{1,0:T(8,128)(2,1)S(1)} %get-tuple-element.127), channel_id=1, source_target_pairs={{1,0},{2,1},{3,2},{5,4},{6,5},{7,6},{9,8},{10,9},{11,10},{13,12},{... | collective-permute-start | bytes 933896 | tf_op jit(solution)/shard_map/ppermute | solution.py:608
  44.9 2.9 %collective-permute-done.4.gy_ref = bf16[152,1024]{1,0:T(8,128)(2,1)S(1)} collective-permute-done((bf16[152,1024]{1,0:T(8,128)(2,1)S(1)}, bf16[152,1024]{1,0:T(8,128)(2,1)S(1)}, u32[]{:S(2)}, u32[]{:S(2)}) %collective-permute-start.4) | collective-permute-done | bytes 311328 | tf_op jit(solution)/shard_map/ppermute | solution.py:608
  47.9 2.2 %chain_row.15 = (bf16[128,1024]{1,0:T(8,128)(2,1)S(1)}, bf16[128,256]{1,0:T(8,128)(2,1)S(1)}, bf16[128,256]{1,0:T(8,128)(2,1)S(1)}, bf16[128,1024]{1,0:T(8,128)(2,1)S(1)}, bf16[144,1024]{1,0:T(8,128)(2,1)S(1)}) custom-call(s32[2]{0:T(128)S(1)} %pad_add_fusion.6.info, bf16[152,1024]{1,0:T(8,128)(2,1)S(1)} %collective-permute-done.4.gy_ref, ...), custom_call_target="tpu_custom_call" | custom-call | flops 3600000000 | bytes 50000000 | tf_op jit(solution)/shard_map/chain_row/pallas_call | solution.py:273
  50.0 2.1 %collective-permute-start.6 = (bf16[144,1024]{1,0:T(8,128)(2,1)S(1)}, bf16[144,1024]{1,0:T(8,128)(2,1)S(1)}, u32[]{:S(2)}, u32[]{:S(2)}) collective-permute-start(bf16[144,1024]{1,0:T(8,128)(2,1)S(1)} %get-tuple-element.129), channel_id=1, source_target_pairs={{1,0},{2,1},{3,2},{5,4},{6,5},{7,6},{9,8},{10,9},{11,10},{13,12},{... | collective-permute-start | bytes 884744 | tf_op jit(solution)/shard_map/ppermute | solution.py:608
  52.1 2.2 %collective-permute-done.5.gy_ref = bf16[152,1024]{1,0:T(8,128)(2,1)S(1)} collective-permute-done((bf16[152,1024]{1,0:T(8,128)(2,1)S(1)}, bf16[152,1024]{1,0:T(8,128)(2,1)S(1)}, u32[]{:S(2)}, u32[]{:S(2)}) %collective-permute-start.5) | collective-permute-done | bytes 311328 | tf_op jit(solution)/shard_map/ppermute | solution.py:608
  54.4 2.2 %chain_row.16 = (bf16[128,1024]{1,0:T(8,128)(2,1)S(1)}, bf16[128,256]{1,0:T(8,128)(2,1)S(1)}, bf16[128,256]{1,0:T(8,128)(2,1)S(1)}, bf16[128,1024]{1,0:T(8,128)(2,1)S(1)}, bf16[144,1024]{1,0:T(8,128)(2,1)S(1)}) custom-call(s32[2]{0:T(128)S(1)} %pad_add_fusion.7.info, bf16[152,1024]{1,0:T(8,128)(2,1)S(1)} %collective-permute-done.5.gy_ref, ...), custom_call_target="tpu_custom_call" | custom-call | flops 3600000000 | bytes 50000000 | tf_op jit(solution)/shard_map/chain_row/pallas_call | solution.py:273
  60.4 2.2 %chain_row.17 = (bf16[128,1024]{1,0:T(8,128)(2,1)S(1)}, bf16[128,256]{1,0:T(8,128)(2,1)S(1)}, bf16[128,256]{1,0:T(8,128)(2,1)S(1)}, bf16[128,1024]{1,0:T(8,128)(2,1)S(1)}, bf16[136,1024]{1,0:T(8,128)(2,1)S(1)}) custom-call(s32[2]{0:T(128)S(1)} %pad_add_fusion.8.info, bf16[144,1024]{1,0:T(8,128)(2,1)S(1)} %collective-permute-done.6.gy_ref, ...), custom_call_target="tpu_custom_call" | custom-call | flops 3600000000 | bytes 50000000 | tf_op jit(solution)/shard_map/chain_row/pallas_call | solution.py:273
  62.6 2.5 %collective-permute-start.8 = (bf16[136,1024]{1,0:T(8,128)(2,1)S(1)}, bf16[136,1024]{1,0:T(8,128)(2,1)S(1)}, u32[]{:S(2)}, u32[]{:S(2)}) collective-permute-start(bf16[136,1024]{1,0:T(8,128)(2,1)S(1)} %get-tuple-element.133), channel_id=1, source_target_pairs={{1,0},{2,1},{3,2},{5,4},{6,5},{7,6},{9,8},{10,9},{11,10},{13,12},{... | collective-permute-start | bytes 835592 | tf_op jit(solution)/shard_map/ppermute | solution.py:608
  65.1 2.9 %collective-permute-done.7.gy_ref = bf16[144,1024]{1,0:T(8,128)(2,1)S(1)} collective-permute-done((bf16[144,1024]{1,0:T(8,128)(2,1)S(1)}, bf16[144,1024]{1,0:T(8,128)(2,1)S(1)}, u32[]{:S(2)}, u32[]{:S(2)}) %collective-permute-start.7) | collective-permute-done | bytes 294944 | tf_op jit(solution)/shard_map/ppermute | solution.py:608
  68.0 2.2 %chain_row.18 = (bf16[128,1024]{1,0:T(8,128)(2,1)S(1)}, bf16[128,256]{1,0:T(8,128)(2,1)S(1)}, bf16[128,256]{1,0:T(8,128)(2,1)S(1)}, bf16[128,1024]{1,0:T(8,128)(2,1)S(1)}, bf16[136,1024]{1,0:T(8,128)(2,1)S(1)}) custom-call(s32[2]{0:T(128)S(1)} %pad_add_fusion.9.info, bf16[144,1024]{1,0:T(8,128)(2,1)S(1)} %collective-permute-done.7.gy_ref, ...), custom_call_target="tpu_custom_call" | custom-call | flops 3600000000 | bytes 50000000 | tf_op jit(solution)/shard_map/chain_row/pallas_call | solution.py:273
  73.9 2.1 %chain_row.19 = (bf16[128,1024]{1,0:T(8,128)(2,1)S(1)}, bf16[128,256]{1,0:T(8,128)(2,1)S(1)}, bf16[128,256]{1,0:T(8,128)(2,1)S(1)}, bf16[128,1024]{1,0:T(8,128)(2,1)S(1)}) custom-call(s32[2]{0:T(128)S(1)} %pad_add_fusion.10.info, bf16[136,1024]{1,0:T(8,128)(2,1)S(1)} %collective-permute-done.8.gy_ref, bf16[4,160,1024]{2,1,0:T(8,128)(2,1)S(1)} %get-tuple-element.117.seed_ref, ...), custom_call_target="tpu_custom_call" | custom-call | flops 3600000000 | bytes 50000000 | tf_op jit(solution)/shard_map/chain_row/pallas_call | solution.py:273
  76.0 2.7 %weight_gradients_early.1 = (bf16[1024,256]{1,0:T(8,128)(2,1)S(1)}, bf16[1024,256]{1,0:T(8,128)(2,1)S(1)}, bf16[1152,256]{1,0:T(8,128)(2,1)S(1)}, bf16[1152,256]{1,0:T(8,128)(2,1)S(1)}) custom-call(s32[3]{0:T(128)S(1)} %pad_add_fusion.1.info, bf16[1024,512]{1,0:T(8,128)(2,1)S(1)} %get-tuple-element.113.refs_0_, ...), custom_call_target="tpu_custom_call" | custom-call | flops 900000000 | bytes 6000000 | tf_op jit(solution)/shard_map/weight_gradients_early/pallas_call | solution.py:435
  85.3 2.8 %chain_row.21 = (bf16[128,1024]{1,0:T(8,128)(2,1)}, bf16[128,256]{1,0:T(8,128)(2,1)}, bf16[128,256]{1,0:T(8,128)(2,1)}, bf16[128,1024]{1,0:T(8,128)(2,1)S(1)}) custom-call(s32[2]{0:T(128)S(1)} %pad_add_fusion.11.info, bf16[136,1024]{1,0:T(8,128)(2,1)S(1)} %collective-permute-done.9.gy_ref, bf16[4,160,1024]{2,1,0:T(8,128)(2,1)S(1)} %get-tuple-element.117.seed_ref, ...), custom_call_target="tpu_custom_call" | custom-call | flops 3600000000 | bytes 50000000 | tf_op jit(solution)/shard_map/chain_row/pallas_call | solution.py:273
  89.6 2.5 %collective-permute-done.11 = bf16[512,256]{1,0:T(8,128)(2,1)S(1)} collective-permute-done((bf16[512,256]{1,0:T(8,128)(2,1)S(1)}, bf16[512,256]{1,0:T(8,128)(2,1)S(1)}, u32[]{:S(2)}, u32[]{:S(2)}) %collective-permute-start.11) | collective-permute-done | bytes 262176 | tf_op jit(solution)/shard_map/ppermute | solution.py:500
  92.9 3.1 %collective-permute-done.14 = bf16[576,256]{1,0:T(8,128)(2,1)S(1)} collective-permute-done((bf16[576,256]{1,0:T(8,128)(2,1)S(1)}, bf16[576,256]{1,0:T(8,128)(2,1)S(1)}, u32[]{:S(2)}, u32[]{:S(2)}) %collective-permute-start.14) | collective-permute-done | bytes 294944 | tf_op jit(solution)/shard_map/ppermute | solution.py:500
  96.2 2.3 %collective-permute-done.12 = bf16[256,256]{1,0:T(8,128)(2,1)S(1)} collective-permute-done((bf16[256,256]{1,0:T(8,128)(2,1)S(1)}, bf16[256,256]{1,0:T(8,128)(2,1)S(1)}, u32[]{:S(2)}, u32[]{:S(2)}) %collective-permute-start.12) | collective-permute-done | bytes 131104 | tf_op jit(solution)/shard_map/ppermute | solution.py:500
  98.6 2.7 %collective-permute-done.15 = bf16[288,256]{1,0:T(8,128)(2,1)S(1)} collective-permute-done((bf16[288,256]{1,0:T(8,128)(2,1)S(1)}, bf16[288,256]{1,0:T(8,128)(2,1)S(1)}, u32[]{:S(2)}, u32[]{:S(2)}) %collective-permute-start.15) | collective-permute-done | bytes 147488 | tf_op jit(solution)/shard_map/ppermute | solution.py:500
  101.7 4.9 %collective-permute-done.16 = bf16[17,16,256]{2,1,0:T(8,128)(2,1)S(1)} collective-permute-done((bf16[17,16,256]{2,1,0:T(8,128)(2,1)S(1)}, bf16[17,16,256]{2,1,0:T(8,128)(2,1)S(1)}, u32[]{:S(2)}, u32[]{:S(2)}) %collective-permute-start.16) | collective-permute-done | bytes 139296 | tf_op jit(solution)/shard_map/ppermute | solution.py:500
  106.7 2.2 %collective-permute-start.17 = (bf16[17,8,256]{2,1,0:T(8,128)(2,1)S(1)}, bf16[17,8,256]{2,1,0:T(8,128)(2,1)S(1)}, u32[]{:S(2)}, u32[]{:S(2)}) collective-permute-start(bf16[17,8,256]{2,1,0:T(8,128)(2,1)S(1)} %slice.147), channel_id=1, source_target_pairs={{0,16},{4,20},{8,24},{12,28},{16,0},{20,4},{24,8},{28,12},{32,48},... | collective-permute-start | bytes 208904 | tf_op jit(solution)/shard_map/ppermute | solution.py:500
  108.9 3.4 %collective-permute-done.17 = bf16[17,8,256]{2,1,0:T(8,128)(2,1)S(1)} collective-permute-done((bf16[17,8,256]{2,1,0:T(8,128)(2,1)S(1)}, bf16[17,8,256]{2,1,0:T(8,128)(2,1)S(1)}, u32[]{:S(2)}, u32[]{:S(2)}) %collective-permute-start.17) | collective-permute-done | bytes 69664 | tf_op jit(solution)/shard_map/ppermute | solution.py:500
  112.3 3.5 %collective-permute-start.18 = (bf16[17,4,256]{2,1,0:T(4,128)(2,1)S(1)}, bf16[17,4,256]{2,1,0:T(4,128)(2,1)S(1)}, u32[]{:S(2)}, u32[]{:S(2)}) collective-permute-start(bf16[17,4,256]{2,1,0:T(4,128)(2,1)S(1)} %slice.148), channel_id=1, source_target_pairs={{0,48},{4,52},{8,56},{12,60},{16,32},{20,36},{24,40},{28,44},{32,1... | collective-permute-start | bytes 104456 | tf_op jit(solution)/shard_map/ppermute | solution.py:500
  115.8 2.6 %collective-permute-done.18.refs_0_ = bf16[17,4,256]{2,1,0:T(4,128)(2,1)S(1)} collective-permute-done((bf16[17,4,256]{2,1,0:T(4,128)(2,1)S(1)}, bf16[17,4,256]{2,1,0:T(4,128)(2,1)S(1)}, u32[]{:S(2)}, u32[]{:S(2)}) %collective-permute-start.18) | collective-permute-done | bytes 34848 | tf_op jit(solution)/shard_map/ppermute | solution.py:500
  (75 shorter events, 29.9 us)
Async XLA Ops:
  0.6 13.4 %copy-start = (bf16[4,4,32,1024]{3,2,1,0:T(8,128)(2,1)S(1)}, bf16[4,4,32,1024]{3,2,1,0:T(8,128)(2,1)}, u32[]{:S(2)}) copy-start(bf16[4,4,32,1024]{3,2,1,0:T(8,128)(2,1)} %og_ref.3) | copy-start | bytes 3145732
  0.6 13.4 %copy-start.1 = (bf16[1,4,4,32,1024]{4,3,2,1,0:T(8,128)(2,1)S(1)}, bf16[1,4,4,32,1024]{4,3,2,1,0:T(8,128)(2,1)}, u32[]{:S(2)}) copy-start(bf16[1,4,4,32,1024]{4,3,2,1,0:T(8,128)(2,1)} %param.11) | copy-start | bytes 3145732
  0.7 13.4 %copy-start.5 = (f32[1,4,256]{2,1,0:T(4,128)S(1)}, f32[1,4,256]{2,1,0:T(4,128)}, u32[]{:S(2)}) copy-start(f32[1,4,256]{2,1,0:T(4,128)} %param.17) | copy-start | bytes 12292
  3.5 14.7 %collective-permute-start = (bf16[4,6,8,1024]{3,2,1,0:T(8,128)(2,1)}, bf16[4,6,8,1024]{3,2,1,0:T(8,128)(2,1)S(1)}, u32[]{:S(2)}, u32[]{:S(2)}) collective-permute-start(bf16[4,6,8,1024]{3,2,1,0:T(8,128)(2,1)} %get-tuple-element.98), channel_id=1, source_target_pairs={{0,4},{4,8},{8,12},{12,16},{16,20},{20,24},{24,28},{28,32},{32,36}... | collective-permute-start | bytes 1179656 | tf_op jit(solution)/shard_map/ppermute | solution.py:560
  5.5 13.1 %collective-permute-start.1 = (bf16[4,6,8,1024]{3,2,1,0:T(8,128)(2,1)}, bf16[4,6,8,1024]{3,2,1,0:T(8,128)(2,1)S(1)}, u32[]{:S(2)}, u32[]{:S(2)}) collective-permute-start(bf16[4,6,8,1024]{3,2,1,0:T(8,128)(2,1)} %get-tuple-element.99), channel_id=1, source_target_pairs={{4,0},{8,4},{12,8},{16,12},{20,16},{24,20},{28,24},{32,28},{36,32}... | collective-permute-start | bytes 1179656 | tf_op jit(solution)/shard_map/ppermute | solution.py:561
  14.0 1.3 %copy-start.2 = (bf16[1,3,3,256,256]{4,3,2,1,0:T(8,128)(2,1)S(1)}, bf16[1,3,3,256,256]{4,3,2,1,0:T(8,128)(2,1)}, u32[]{:S(2)}) copy-start(bf16[1,3,3,256,256]{4,3,2,1,0:T(8,128)(2,1)} %param.15) | copy-start | bytes 3538948
  15.3 1.0 copy-start.3
  16.3 1.0 copy-start.4
  17.4 1.2 copy-start.6
  17.4 1.2 copy-start.7
  22.4 11.1 %collective-permute-start.2 = (bf16[152,1024]{1,0:T(8,128)(2,1)S(1)}, bf16[152,1024]{1,0:T(8,128)(2,1)S(1)}, u32[]{:S(2)}, u32[]{:S(2)}) collective-permute-start(bf16[152,1024]{1,0:T(8,128)(2,1)S(1)} %get-tuple-element.121), channel_id=1, source_target_pairs={{1,0},{2,1},{3,2},{5,4},{6,5},{7,6},{9,8},{10,9},{11,10},{13,12},{... | collective-permute-start | bytes 933896 | tf_op jit(solution)/shard_map/ppermute | solution.py:608
  30.0 10.3 %collective-permute-start.3 = (bf16[152,1024]{1,0:T(8,128)(2,1)S(1)}, bf16[152,1024]{1,0:T(8,128)(2,1)S(1)}, u32[]{:S(2)}, u32[]{:S(2)}) collective-permute-start(bf16[152,1024]{1,0:T(8,128)(2,1)S(1)} %get-tuple-element.123), channel_id=1, source_target_pairs={{1,0},{2,1},{3,2},{5,4},{6,5},{7,6},{9,8},{10,9},{11,10},{13,12},{... | collective-permute-start | bytes 933896 | tf_op jit(solution)/shard_map/ppermute | solution.py:608
  35.7 12.2 %collective-permute-start.4 = (bf16[152,1024]{1,0:T(8,128)(2,1)S(1)}, bf16[152,1024]{1,0:T(8,128)(2,1)S(1)}, u32[]{:S(2)}, u32[]{:S(2)}) collective-permute-start(bf16[152,1024]{1,0:T(8,128)(2,1)S(1)} %get-tuple-element.125), channel_id=1, source_target_pairs={{1,0},{2,1},{3,2},{5,4},{6,5},{7,6},{9,8},{10,9},{11,10},{13,12},{... | collective-permute-start | bytes 933896 | tf_op jit(solution)/shard_map/ppermute | solution.py:608
  42.4 12.0 %collective-permute-start.5 = (bf16[152,1024]{1,0:T(8,128)(2,1)S(1)}, bf16[152,1024]{1,0:T(8,128)(2,1)S(1)}, u32[]{:S(2)}, u32[]{:S(2)}) collective-permute-start(bf16[152,1024]{1,0:T(8,128)(2,1)S(1)} %get-tuple-element.127), channel_id=1, source_target_pairs={{1,0},{2,1},{3,2},{5,4},{6,5},{7,6},{9,8},{10,9},{11,10},{13,12},{... | collective-permute-start | bytes 933896 | tf_op jit(solution)/shard_map/ppermute | solution.py:608
  50.0 10.4 %collective-permute-start.6 = (bf16[144,1024]{1,0:T(8,128)(2,1)S(1)}, bf16[144,1024]{1,0:T(8,128)(2,1)S(1)}, u32[]{:S(2)}, u32[]{:S(2)}) collective-permute-start(bf16[144,1024]{1,0:T(8,128)(2,1)S(1)} %get-tuple-element.129), channel_id=1, source_target_pairs={{1,0},{2,1},{3,2},{5,4},{6,5},{7,6},{9,8},{10,9},{11,10},{13,12},{... | collective-permute-start | bytes 884744 | tf_op jit(solution)/shard_map/ppermute | solution.py:608
  56.5 11.5 %collective-permute-start.7 = (bf16[144,1024]{1,0:T(8,128)(2,1)S(1)}, bf16[144,1024]{1,0:T(8,128)(2,1)S(1)}, u32[]{:S(2)}, u32[]{:S(2)}) collective-permute-start(bf16[144,1024]{1,0:T(8,128)(2,1)S(1)} %get-tuple-element.131), channel_id=1, source_target_pairs={{1,0},{2,1},{3,2},{5,4},{6,5},{7,6},{9,8},{10,9},{11,10},{13,12},{... | collective-permute-start | bytes 884744 | tf_op jit(solution)/shard_map/ppermute | solution.py:608
  62.6 11.3 %collective-permute-start.8 = (bf16[136,1024]{1,0:T(8,128)(2,1)S(1)}, bf16[136,1024]{1,0:T(8,128)(2,1)S(1)}, u32[]{:S(2)}, u32[]{:S(2)}) collective-permute-start(bf16[136,1024]{1,0:T(8,128)(2,1)S(1)} %get-tuple-element.133), channel_id=1, source_target_pairs={{1,0},{2,1},{3,2},{5,4},{6,5},{7,6},{9,8},{10,9},{11,10},{13,12},{... | collective-permute-start | bytes 835592 | tf_op jit(solution)/shard_map/ppermute | solution.py:608
  70.2 8.5 %collective-permute-start.9 = (bf16[136,1024]{1,0:T(8,128)(2,1)S(1)}, bf16[136,1024]{1,0:T(8,128)(2,1)S(1)}, u32[]{:S(2)}, u32[]{:S(2)}) collective-permute-start(bf16[136,1024]{1,0:T(8,128)(2,1)S(1)} %get-tuple-element.155), channel_id=1, source_target_pairs={{1,0},{2,1},{3,2},{5,4},{6,5},{7,6},{9,8},{10,9},{11,10},{13,12},{... | collective-permute-start | bytes 835592 | tf_op jit(solution)/shard_map/ppermute | solution.py:608
  81.6 2.0 %collective-permute-start.10 = (bf16[1024,256]{1,0:T(8,128)(2,1)S(1)}, bf16[1024,256]{1,0:T(8,128)(2,1)S(1)}, u32[]{:S(2)}, u32[]{:S(2)}) collective-permute-start(bf16[1024,256]{1,0:T(8,128)(2,1)S(1)} %get-tuple-element.159), channel_id=1, source_target_pairs={{0,4},{4,0},{8,12},{12,8},{16,20},{20,16},{24,28},{28,24},{32,36},... | collective-permute-start | bytes 1572872 | tf_op jit(solution)/shard_map/ppermute | solution.py:500
  82.8 2.2 %collective-permute-start.13 = (bf16[1152,256]{1,0:T(8,128)(2,1)S(1)}, bf16[1152,256]{1,0:T(8,128)(2,1)S(1)}, u32[]{:S(2)}, u32[]{:S(2)}) collective-permute-start(bf16[1152,256]{1,0:T(8,128)(2,1)S(1)} %get-tuple-element.164), channel_id=1, source_target_pairs={{0,4},{4,0},{8,12},{12,8},{16,20},{20,16},{24,28},{28,24},{32,36},... | collective-permute-start | bytes 1769480 | tf_op jit(solution)/shard_map/ppermute | solution.py:500
  83.6 8.4 %collective-permute-start.11 = (bf16[512,256]{1,0:T(8,128)(2,1)S(1)}, bf16[512,256]{1,0:T(8,128)(2,1)S(1)}, u32[]{:S(2)}, u32[]{:S(2)}) collective-permute-start(bf16[512,256]{1,0:T(8,128)(2,1)S(1)} %add_convert_fusion.1), channel_id=1, source_target_pairs={{0,64},{4,68},{8,72},{12,76},{16,80},{20,84},{24,88},{28,92},{32,9... | collective-permute-start | bytes 786440 | tf_op jit(solution)/shard_map/ppermute | solution.py:500
  85.1 10.9 %collective-permute-start.14 = (bf16[576,256]{1,0:T(8,128)(2,1)S(1)}, bf16[576,256]{1,0:T(8,128)(2,1)S(1)}, u32[]{:S(2)}, u32[]{:S(2)}) collective-permute-start(bf16[576,256]{1,0:T(8,128)(2,1)S(1)} %add_convert_fusion), channel_id=1, source_target_pairs={{0,192},{4,196},{8,200},{12,204},{16,208},{20,212},{24,216},{28,22... | collective-permute-start | bytes 884744 | tf_op jit(solution)/shard_map/ppermute | solution.py:500
  92.1 6.4 %collective-permute-start.12 = (bf16[256,256]{1,0:T(8,128)(2,1)S(1)}, bf16[256,256]{1,0:T(8,128)(2,1)S(1)}, u32[]{:S(2)}, u32[]{:S(2)}) collective-permute-start(bf16[256,256]{1,0:T(8,128)(2,1)S(1)} %add_convert_fusion.3), channel_id=1, source_target_pairs={{0,192},{4,196},{8,200},{12,204},{16,208},{20,212},{24,216},{28,22... | collective-permute-start | bytes 393224 | tf_op jit(solution)/shard_map/ppermute | solution.py:500
  96.1 5.2 %collective-permute-start.15 = (bf16[288,256]{1,0:T(8,128)(2,1)S(1)}, bf16[288,256]{1,0:T(8,128)(2,1)S(1)}, u32[]{:S(2)}, u32[]{:S(2)}) collective-permute-start(bf16[288,256]{1,0:T(8,128)(2,1)S(1)} %add_convert_fusion.2), channel_id=1, source_target_pairs={{0,64},{4,68},{8,72},{12,76},{16,80},{20,84},{24,88},{28,92},{32,9... | collective-permute-start | bytes 442376 | tf_op jit(solution)/shard_map/ppermute | solution.py:500
  101.5 5.1 %collective-permute-start.16 = (bf16[17,16,256]{2,1,0:T(8,128)(2,1)S(1)}, bf16[17,16,256]{2,1,0:T(8,128)(2,1)S(1)}, u32[]{:S(2)}, u32[]{:S(2)}) collective-permute-start(bf16[17,16,256]{2,1,0:T(8,128)(2,1)S(1)} %slice.146), channel_id=1, source_target_pairs={{0,8},{4,12},{8,0},{12,4},{16,24},{20,28},{24,16},{28,20},{32,40},... | collective-permute-start | bytes 417800 | tf_op jit(solution)/shard_map/ppermute | solution.py:500
  106.7 5.6 %collective-permute-start.17 = (bf16[17,8,256]{2,1,0:T(8,128)(2,1)S(1)}, bf16[17,8,256]{2,1,0:T(8,128)(2,1)S(1)}, u32[]{:S(2)}, u32[]{:S(2)}) collective-permute-start(bf16[17,8,256]{2,1,0:T(8,128)(2,1)S(1)} %slice.147), channel_id=1, source_target_pairs={{0,16},{4,20},{8,24},{12,28},{16,0},{20,4},{24,8},{28,12},{32,48},... | collective-permute-start | bytes 208904 | tf_op jit(solution)/shard_map/ppermute | solution.py:500
  112.3 6.1 %collective-permute-start.18 = (bf16[17,4,256]{2,1,0:T(4,128)(2,1)S(1)}, bf16[17,4,256]{2,1,0:T(4,128)(2,1)S(1)}, u32[]{:S(2)}, u32[]{:S(2)}) collective-permute-start(bf16[17,4,256]{2,1,0:T(4,128)(2,1)S(1)} %slice.148), channel_id=1, source_target_pairs={{0,48},{4,52},{8,56},{12,60},{16,32},{20,36},{24,40},{28,44},{32,1... | collective-permute-start | bytes 104456 | tf_op jit(solution)/shard_map/ppermute | solution.py:500
